TPU v7x, 256 devices: a whole 4x4x8 slice. The times are simulated.
256 devices in a mesh: depth: 256 (over y, z, x, core).
Axes of the slice: x: 4, y: 4, z: 8, core: 2. Of those that a mesh axis runs over, the one named last changes fastest.
Arguments:
- state_guess: float32 [256, 128, 512], P('depth'), may hold values from -6 to 6
- adjoint_guess: float32 [256, 128, 512], P('depth'), may hold values from -6 to 6
- w_in: bfloat16 [512, 512, 2048], P('depth'), may hold values from -0.25 to 0.25
- w_out: bfloat16 [512, 2048, 512], P('depth'), may hold values from -0.03125 to 0.03125
- norm_gain: float32 [512, 512], P('depth'), may hold values from 0.5 to 1.5
- decay: float32 [512, 512], P('depth'), may hold values from 0.5 to 1
Outputs:
- forward_states: float32 [512, 128, 512], P('depth')
- adjoint_states: float32 [512, 128, 512], P('depth')
All inputs are finite; a program needn't handle non-finite values.
Results may differ from a plain program's by a relative error of at most 0.009.
Values sent between devices are 32-bit elements; how exact they have to be, the bound alone decides.
A program may use at most 192 MiB of HBM per device.

v0:
```python
import jax
import jax.numpy as jnp
from jax import lax
from jax.sharding import PartitionSpec as P


def shifted(block, axis, distance):
    devices = range(lax.axis_size(axis))
    route = [(i - distance, i) for i in devices if i - distance in devices]
    return lax.ppermute(block, axis, route)


def doubling_scan(factor, offset, axis, reverse):
    size, position = (lax.axis_size(axis), lax.axis_index(axis))
    rows = offset.shape[0]
    packed = jnp.concatenate([offset, factor[None, :]], axis=0)
    distance = 1
    while distance < size:
        step = -distance if reverse else distance
        came = shifted(packed, axis, step)
        reached = position + distance < size if reverse else position >= distance
        scale = packed[rows:]
        joined = jnp.concatenate(
            [packed[:rows] + scale * came[:rows], scale * came[rows:]], axis=0
        )
        packed = jnp.where(reached, joined, packed)
        distance *= 2
    return packed[:rows]


def prepare_block(state, w_first, gain_row):
    inverse = lax.rsqrt(jnp.mean(state * state, axis=-1, keepdims=True) + 1e-05)
    normed = (state * inverse * gain_row).astype(jnp.bfloat16)
    preact = jnp.dot(normed, w_first, preferred_element_type=jnp.float32)
    return (inverse, preact)


def finish_block(state, preact, w_second, decay_row):
    hidden = jax.nn.silu(preact).astype(jnp.bfloat16)
    return decay_row * state + jnp.dot(hidden, w_second, preferred_element_type=jnp.float32)


def backward_block(state, inverse, preact, upstream, w_first, w_second, gain_row, decay_row):
    grad_hidden = lax.dot_general(
        upstream.astype(jnp.bfloat16),
        w_second,
        (((1,), (1,)), ((), ())),
        preferred_element_type=jnp.float32,
    )
    sigma = jax.nn.sigmoid(preact)
    grad_pre = (grad_hidden * sigma * (1.0 + preact * (1.0 - sigma))).astype(jnp.bfloat16)
    grad_norm = lax.dot_general(
        grad_pre, w_first, (((1,), (1,)), ((), ())), preferred_element_type=jnp.float32
    )
    scaled = grad_norm * gain_row
    inner = jnp.mean(scaled * state, axis=-1, keepdims=True)
    return decay_row * upstream + inverse * scaled - state * inverse**3 * inner


def relax_forward(start, w_in, w_out, norm_gain, decay, want_end):
    state = start
    count = w_in.shape[0]
    states_list, inverse_list, preact_list = ([], [], [])
    for block in range(count):
        states_list.append(state)
        inverse, preact = prepare_block(state, w_in[block], norm_gain[block])
        inverse_list.append(inverse)
        preact_list.append(preact)
        if want_end or block + 1 < count:
            state = finish_block(state, preact, w_out[block], decay[block])
    return (state, states_list, inverse_list, preact_list)


def relax_backward(start, states, inverses, preacts, w_in, w_out, norm_gain, decay):
    adjoint = start
    count = w_in.shape[0]
    collected = [None] * count
    for block in reversed(range(count)):
        adjoint = backward_block(
            states[block],
            inverses[block],
            preacts[block],
            adjoint,
            w_in[block],
            w_out[block],
            norm_gain[block],
            decay[block],
        )
        collected[block] = adjoint
    return (adjoint, collected)


def compose(earlier, later):
    return (later[0] * earlier[0], later[0] * earlier[1] + later[1])


def shards(state_guess, adjoint_guess, w_in, w_out, norm_gain, decay):
    position = lax.axis_index("depth")
    devices = lax.axis_size("depth")
    factor = jnp.prod(decay, axis=0)
    at_first = position == 0
    at_last = position == devices - 1
    factor_before = shifted(factor, "depth", 1)
    factor_after = shifted(factor, "depth", -1)
    guess_state = state_guess[0]
    end_state, _, _, _ = relax_forward(guess_state, w_in, w_out, norm_gain, decay, True)
    end_before = shifted(end_state, "depth", 1)
    resid = jnp.where(at_first, jnp.zeros_like(guess_state), end_before - guess_state)
    correction = doubling_scan(factor_before, resid, "depth", False)
    start = guess_state + correction
    _, states, inverses, preacts = relax_forward(start, w_in, w_out, norm_gain, decay, False)
    guess_adjoint = adjoint_guess[0]
    first_adjoint, _ = relax_backward(
        guess_adjoint, states, inverses, preacts, w_in, w_out, norm_gain, decay
    )
    first_after = shifted(first_adjoint, "depth", -1)
    rho = jnp.where(at_last, jnp.zeros_like(guess_adjoint), first_after - guess_adjoint)
    eps = doubling_scan(factor_after, rho, "depth", True)
    head = guess_adjoint + eps
    _, lambdas = relax_backward(head, states, inverses, preacts, w_in, w_out, norm_gain, decay)
    return (jnp.stack(states), jnp.stack(lambdas))


def solution(mesh):
    placed = (
        P("depth", None, None),
        P("depth", None, None),
        P("depth", None, None),
        P("depth", None, None),
        P("depth", None),
        P("depth", None),
    )
    return jax.shard_map(
        shards,
        mesh=mesh,
        in_specs=placed,
        out_specs=(P("depth", None, None), P("depth", None, None)),
        check_vma=False,
    )
```

profile of v0, /device:TPU:1, one launch (start us, length us, event | category | flops | bytes accessed | tf_op | source)
XLA Modules:
  0.0 258.5 jit_solution(3919632354560151582)
XLA Ops:
  9.5 4.5 %collective-permute-start = (f32[128,512]{1,0:T(8,128)S(1)}, f32[128,512]{1,0:T(8,128)S(1)}, u32[]{:S(2)}, u32[]{:S(2)}) collective-permute-start(f32[128,512]{1,0:T(8,128)S(1)} %fusion.67), channel_id=1, source_target_pairs={{0,1},{1,2},{2,3},{3,4},{4,5},{5,6},{6,7},{7,8},{8,9},{9,10},{10,1... | collective-permute-start | bytes 786440 | tf_op jit(solution)/shard_map/ppermute | solution.py:10
  17.4 4.4 %collective-permute-start.2 = (f32[129,512]{1,0:T(8,128)S(1)}, f32[129,512]{1,0:T(8,128)S(1)}, u32[]{:S(2)}, u32[]{:S(2)}) collective-permute-start(f32[129,512]{1,0:T(8,128)S(1)} %pad_maximum_fusion.2), channel_id=1, source_target_pairs={{0,1},{1,2},{2,3},{3,4},{4,5},{5,6},{6,7},{7,8},{8,9},{9,10},{10,1... | collective-permute-start | bytes 792584 | tf_op jit(solution)/shard_map/ppermute | solution.py:10
  28.5 4.5 %collective-permute-done.3 = f32[129,512]{1,0:T(8,128)S(1)} collective-permute-done((f32[129,512]{1,0:T(8,128)S(1)}, f32[129,512]{1,0:T(8,128)S(1)}, u32[]{:S(2)}, u32[]{:S(2)}) %collective-permute-start.3) | collective-permute-done | bytes 264224 | tf_op jit(solution)/shard_map/ppermute | solution.py:10
  33.1 8.1 %collective-permute-start.4 = (f32[129,512]{1,0:T(8,128)S(1)}, f32[129,512]{1,0:T(8,128)S(1)}, u32[]{:S(2)}, u32[]{:S(2)}) collective-permute-start(f32[129,512]{1,0:T(8,128)S(1)} %maximum_select_fusion.1), channel_id=1, source_target_pairs={{0,4},{1,5},{2,6},{3,7},{4,8},{5,9},{6,10},{7,11},{8,12},{9,13},{1... | collective-permute-start | bytes 792584 | tf_op jit(solution)/shard_map/ppermute | solution.py:10
  41.3 6.1 %collective-permute-done.4 = f32[129,512]{1,0:T(8,128)S(1)} collective-permute-done((f32[129,512]{1,0:T(8,128)S(1)}, f32[129,512]{1,0:T(8,128)S(1)}, u32[]{:S(2)}, u32[]{:S(2)}) %collective-permute-start.4) | collective-permute-done | bytes 264224 | tf_op jit(solution)/shard_map/ppermute | solution.py:10
  52.7 5.2 %collective-permute-start.6 = (f32[129,512]{1,0:T(8,128)S(1)}, f32[129,512]{1,0:T(8,128)S(1)}, u32[]{:S(2)}, u32[]{:S(2)}) collective-permute-start(f32[129,512]{1,0:T(8,128)S(1)} %maximum_select_fusion.3), channel_id=1, source_target_pairs={{0,16},{1,17},{2,18},{3,19},{4,20},{5,21},{6,22},{7,23},{8,24},{9,... | collective-permute-start | bytes 792584 | tf_op jit(solution)/shard_map/ppermute | solution.py:10
  57.9 5.2 %collective-permute-done.6 = f32[129,512]{1,0:T(8,128)S(1)} collective-permute-done((f32[129,512]{1,0:T(8,128)S(1)}, f32[129,512]{1,0:T(8,128)S(1)}, u32[]{:S(2)}, u32[]{:S(2)}) %collective-permute-start.6) | collective-permute-done | bytes 264224 | tf_op jit(solution)/shard_map/ppermute | solution.py:10
  63.2 14.6 %collective-permute-start.7 = (f32[129,512]{1,0:T(8,128)S(1)}, f32[129,512]{1,0:T(8,128)S(1)}, u32[]{:S(2)}, u32[]{:S(2)}) collective-permute-start(f32[129,512]{1,0:T(8,128)S(1)} %maximum_select_fusion.4), channel_id=1, source_target_pairs={{0,32},{1,33},{2,34},{3,35},{4,36},{5,37},{6,38},{7,39},{8,40},{9,... | collective-permute-start | bytes 792584 | tf_op jit(solution)/shard_map/ppermute | solution.py:10
  81.4 13.9 %collective-permute-start.8 = (f32[129,512]{1,0:T(8,128)S(1)}, f32[129,512]{1,0:T(8,128)S(1)}, u32[]{:S(2)}, u32[]{:S(2)}) collective-permute-start(f32[129,512]{1,0:T(8,128)S(1)} %maximum_select_fusion.5), channel_id=1, source_target_pairs={{0,64},{1,65},{2,66},{3,67},{4,68},{5,69},{6,70},{7,71},{8,72},{9,... | collective-permute-start | bytes 792584 | tf_op jit(solution)/shard_map/ppermute | solution.py:10
  95.3 3.8 %collective-permute-done.8 = f32[129,512]{1,0:T(8,128)S(1)} collective-permute-done((f32[129,512]{1,0:T(8,128)S(1)}, f32[129,512]{1,0:T(8,128)S(1)}, u32[]{:S(2)}, u32[]{:S(2)}) %collective-permute-start.8) | collective-permute-done | bytes 264224 | tf_op jit(solution)/shard_map/ppermute | solution.py:10
  99.3 4.8 %collective-permute-start.9 = (f32[129,512]{1,0:T(8,128)S(1)}, f32[129,512]{1,0:T(8,128)S(1)}, u32[]{:S(2)}, u32[]{:S(2)}) collective-permute-start(f32[129,512]{1,0:T(8,128)S(1)} %maximum_select_fusion.6), channel_id=1, source_target_pairs={{0,128},{1,129},{2,130},{3,131},{4,132},{5,133},{6,134},{7,135},{8... | collective-permute-start | bytes 792584 | tf_op jit(solution)/shard_map/ppermute | solution.py:10
  112.6 3.9 %multiply_reduce_fusion.3 = (f32[128]{0:T(128)S(1)}, f32[128,512]{1,0:T(8,128)S(1)}) fusion(f32[128,512]{1,0:T(8,128)S(1)} %get-tuple-element.43, f32[512]{0:T(512)S(1)} %bitcast.167, bf16[2,512,2048]{2,1,0:T(8,128)(2,1)} %param.8, bf16[2,2048,512]{2,1,0:T(8,128)(2,1)} %param.9, f32[128,2048]{1,0:T(8,128)S(1)} %fusion.16, f32[1,128,512]{2,1,0:T(8,128)S(1)} %copy-done.2), kind=kOutput, calls=%fused_computation.146 | convolution fusion | flops 539492224 | bytes 6031872 | tf_op jit(solution)/shard_map/dot_general | solution.py:52
  116.6 4.5 %multiply_reduce_fusion.2 = (f32[128]{0:T(128)S(1)}, f32[128,512]{1,0:T(8,128)}) fusion(f32[128,512]{1,0:T(8,128)S(1)} %get-tuple-element.3, f32[512]{0:T(512)S(1)} %bitcast.163, bf16[2,512,2048]{2,1,0:T(8,128)(2,1)} %param.8, bf16[2,2048,512]{2,1,0:T(8,128)(2,1)} %param.9, f32[128,2048]{1,0:T(8,128)S(1)} %fusion.30, f32[128,512]{1,0:T(8,128)S(1)} %fusion.114), kind=kOutput, calls=%fused_computation.145 | convolution fusion | flops 539492224 | bytes 6031872 | tf_op jit(solution)/shard_map/dot_general | solution.py:52
  122.2 23.8 %collective-permute-start.10 = (f32[128,512]{1,0:T(8,128)S(1)}, f32[128,512]{1,0:T(8,128)S(1)}, u32[]{:S(2)}, u32[]{:S(2)}) collective-permute-start(f32[128,512]{1,0:T(8,128)S(1)} %multiply_subtract_fusion.1), channel_id=1, source_target_pairs={{1,0},{2,1},{3,2},{4,3},{5,4},{6,5},{7,6},{8,7},{9,8},{10,9},{11,1... | collective-permute-start | bytes 786440 | tf_op jit(solution)/shard_map/ppermute | solution.py:10
  152.9 6.0 %collective-permute-done.12 = f32[129,512]{1,0:T(8,128)} collective-permute-done((f32[129,512]{1,0:T(8,128)S(1)}, f32[129,512]{1,0:T(8,128)}, u32[]{:S(2)}, u32[]{:S(2)}) %collective-permute-start.12) | collective-permute-done | bytes 264224 | tf_op jit(solution)/shard_map/ppermute | solution.py:10
  162.0 7.5 %collective-permute-done.13 = f32[129,512]{1,0:T(8,128)S(1)} collective-permute-done((f32[129,512]{1,0:T(8,128)S(1)}, f32[129,512]{1,0:T(8,128)S(1)}, u32[]{:S(2)}, u32[]{:S(2)}) %collective-permute-start.13) | collective-permute-done | bytes 264224 | tf_op jit(solution)/shard_map/ppermute | solution.py:10
  171.0 10.1 %collective-permute-done.14 = f32[129,512]{1,0:T(8,128)S(1)} collective-permute-done((f32[129,512]{1,0:T(8,128)S(1)}, f32[129,512]{1,0:T(8,128)S(1)}, u32[]{:S(2)}, u32[]{:S(2)}) %collective-permute-start.14) | collective-permute-done | bytes 264224 | tf_op jit(solution)/shard_map/ppermute | solution.py:10
  182.5 8.5 %collective-permute-done.15 = f32[129,512]{1,0:T(8,128)S(1)} collective-permute-done((f32[129,512]{1,0:T(8,128)S(1)}, f32[129,512]{1,0:T(8,128)S(1)}, u32[]{:S(2)}, u32[]{:S(2)}) %collective-permute-start.15) | collective-permute-done | bytes 264224 | tf_op jit(solution)/shard_map/ppermute | solution.py:10
  192.4 15.6 %collective-permute-done.16 = f32[129,512]{1,0:T(8,128)S(1)} collective-permute-done((f32[129,512]{1,0:T(8,128)S(1)}, f32[129,512]{1,0:T(8,128)S(1)}, u32[]{:S(2)}, u32[]{:S(2)}) %collective-permute-start.16) | collective-permute-done | bytes 264224 | tf_op jit(solution)/shard_map/ppermute | solution.py:10
  209.5 11.8 %collective-permute-done.17 = f32[129,512]{1,0:T(8,128)S(1)} collective-permute-done((f32[129,512]{1,0:T(8,128)S(1)}, f32[129,512]{1,0:T(8,128)S(1)}, u32[]{:S(2)}, u32[]{:S(2)}) %collective-permute-start.17) | collective-permute-done | bytes 264224 | tf_op jit(solution)/shard_map/ppermute | solution.py:10
  222.7 16.2 %collective-permute-done.18 = f32[129,512]{1,0:T(8,128)S(1)} collective-permute-done((f32[129,512]{1,0:T(8,128)S(1)}, f32[129,512]{1,0:T(8,128)S(1)}, u32[]{:S(2)}, u32[]{:S(2)}) %collective-permute-start.18) | collective-permute-done | bytes 264224 | tf_op jit(solution)/shard_map/ppermute | solution.py:10
  241.1 8.4 %collective-permute-done.19 = f32[129,512]{1,0:T(8,128)S(1)} collective-permute-done((f32[129,512]{1,0:T(8,128)S(1)}, f32[129,512]{1,0:T(8,128)S(1)}, u32[]{:S(2)}, u32[]{:S(2)}) %collective-permute-start.19) | collective-permute-done | bytes 264224 | tf_op jit(solution)/shard_map/ppermute | solution.py:10
  249.6 3.9 %multiply_reduce_fusion.1 = (f32[128]{0:T(128)S(1)}, f32[128,512]{1,0:T(8,128)S(1)}) fusion(f32[128,512]{1,0:T(8,128)S(1)} %get-tuple-element.43, f32[512]{0:T(512)S(1)} %bitcast.168, bf16[2,512,2048]{2,1,0:T(8,128)(2,1)} %param.8, bf16[2,2048,512]{2,1,0:T(8,128)(2,1)} %param.9, f32[128,2048]{1,0:T(8,128)S(1)} %fusion.16, f32[128,512]{1,0:T(8,128)S(1)} %fusion.94), kind=kOutput, calls=%fused_computation.143 | convolution fusion | flops 539492224 | bytes 6031872 | tf_op jit(solution)/shard_map/dot_general | solution.py:52
  253.7 3.9 %multiply_reduce_fusion = (f32[128]{0:T(128)S(1)}, f32[128,512]{1,0:T(8,128)S(1)}) fusion(f32[128,512]{1,0:T(8,128)S(1)} %get-tuple-element.3, f32[512]{0:T(512)S(1)} %bitcast.164, bf16[2,512,2048]{2,1,0:T(8,128)(2,1)} %param.8, bf16[2,2048,512]{2,1,0:T(8,128)(2,1)} %param.9, f32[128,2048]{1,0:T(8,128)S(1)} %fusion.30, ...), kind=kOutput, calls=%fused_computation.141 | convolution fusion | flops 539492224 | bytes 6031872 | tf_op jit(solution)/shard_map/dot_general | solution.py:52
  (105 shorter events, 57.9 us)
Async XLA Ops:
  6.4 7.6 %copy-start.3 = (f32[2,512]{1,0:T(2,128)S(1)}, f32[2,512]{1,0:T(2,128)}, u32[]{:S(2)}) copy-start(f32[2,512]{1,0:T(2,128)} %param.11) | copy-start | bytes 12292
  6.4 10.9 %copy-start.1 = (f32[1,128,512]{2,1,0:T(8,128)S(1)}, f32[1,128,512]{2,1,0:T(8,128)}, u32[]{:S(2)}) copy-start(f32[1,128,512]{2,1,0:T(8,128)} %param.6) | copy-start | bytes 786436
  9.5 7.8 %collective-permute-start = (f32[128,512]{1,0:T(8,128)S(1)}, f32[128,512]{1,0:T(8,128)S(1)}, u32[]{:S(2)}, u32[]{:S(2)}) collective-permute-start(f32[128,512]{1,0:T(8,128)S(1)} %fusion.67), channel_id=1, source_target_pairs={{0,1},{1,2},{2,3},{3,4},{4,5},{5,6},{6,7},{7,8},{8,9},{9,10},{10,1... | collective-permute-start | bytes 786440 | tf_op jit(solution)/shard_map/ppermute | solution.py:10
  14.0 3.3 %collective-permute-start.1 = (f32[512]{0:T(512)S(1)}, f32[512]{0:T(512)S(1)}, u32[]{:S(2)}, u32[]{:S(2)}) collective-permute-start(f32[512]{0:T(512)S(1)} %reduce_prod.9), channel_id=1, source_target_pairs={{0,1},{1,2},{2,3},{3,4},{4,5},{5,6},{6,7},{7,8},{8,9},{9,10},{10,1... | collective-permute-start | bytes 6152 | tf_op jit(solution)/shard_map/ppermute | solution.py:10
  17.4 7.9 %collective-permute-start.2 = (f32[129,512]{1,0:T(8,128)S(1)}, f32[129,512]{1,0:T(8,128)S(1)}, u32[]{:S(2)}, u32[]{:S(2)}) collective-permute-start(f32[129,512]{1,0:T(8,128)S(1)} %pad_maximum_fusion.2), channel_id=1, source_target_pairs={{0,1},{1,2},{2,3},{3,4},{4,5},{5,6},{6,7},{7,8},{8,9},{9,10},{10,1... | collective-permute-start | bytes 792584 | tf_op jit(solution)/shard_map/ppermute | solution.py:10
  25.4 7.7 %collective-permute-start.3 = (f32[129,512]{1,0:T(8,128)S(1)}, f32[129,512]{1,0:T(8,128)S(1)}, u32[]{:S(2)}, u32[]{:S(2)}) collective-permute-start(f32[129,512]{1,0:T(8,128)S(1)} %maximum_select_fusion), channel_id=1, source_target_pairs={{0,2},{1,3},{2,4},{3,5},{4,6},{5,7},{6,8},{7,9},{8,10},{9,11},{10,... | collective-permute-start | bytes 792584 | tf_op jit(solution)/shard_map/ppermute | solution.py:10
  33.1 14.3 %collective-permute-start.4 = (f32[129,512]{1,0:T(8,128)S(1)}, f32[129,512]{1,0:T(8,128)S(1)}, u32[]{:S(2)}, u32[]{:S(2)}) collective-permute-start(f32[129,512]{1,0:T(8,128)S(1)} %maximum_select_fusion.1), channel_id=1, source_target_pairs={{0,4},{1,5},{2,6},{3,7},{4,8},{5,9},{6,10},{7,11},{8,12},{9,13},{1... | collective-permute-start | bytes 792584 | tf_op jit(solution)/shard_map/ppermute | solution.py:10
  47.5 5.1 %collective-permute-start.5 = (f32[129,512]{1,0:T(8,128)S(1)}, f32[129,512]{1,0:T(8,128)S(1)}, u32[]{:S(2)}, u32[]{:S(2)}) collective-permute-start(f32[129,512]{1,0:T(8,128)S(1)} %maximum_select_fusion.2), channel_id=1, source_target_pairs={{0,8},{1,9},{2,10},{3,11},{4,12},{5,13},{6,14},{7,15},{8,16},{9,17... | collective-permute-start | bytes 792584 | tf_op jit(solution)/shard_map/ppermute | solution.py:10
  52.7 10.4 %collective-permute-start.6 = (f32[129,512]{1,0:T(8,128)S(1)}, f32[129,512]{1,0:T(8,128)S(1)}, u32[]{:S(2)}, u32[]{:S(2)}) collective-permute-start(f32[129,512]{1,0:T(8,128)S(1)} %maximum_select_fusion.3), channel_id=1, source_target_pairs={{0,16},{1,17},{2,18},{3,19},{4,20},{5,21},{6,22},{7,23},{8,24},{9,... | collective-permute-start | bytes 792584 | tf_op jit(solution)/shard_map/ppermute | solution.py:10
  63.2 18.1 %collective-permute-start.7 = (f32[129,512]{1,0:T(8,128)S(1)}, f32[129,512]{1,0:T(8,128)S(1)}, u32[]{:S(2)}, u32[]{:S(2)}) collective-permute-start(f32[129,512]{1,0:T(8,128)S(1)} %maximum_select_fusion.4), channel_id=1, source_target_pairs={{0,32},{1,33},{2,34},{3,35},{4,36},{5,37},{6,38},{7,39},{8,40},{9,... | collective-permute-start | bytes 792584 | tf_op jit(solution)/shard_map/ppermute | solution.py:10
  81.4 17.8 %collective-permute-start.8 = (f32[129,512]{1,0:T(8,128)S(1)}, f32[129,512]{1,0:T(8,128)S(1)}, u32[]{:S(2)}, u32[]{:S(2)}) collective-permute-start(f32[129,512]{1,0:T(8,128)S(1)} %maximum_select_fusion.5), channel_id=1, source_target_pairs={{0,64},{1,65},{2,66},{3,67},{4,68},{5,69},{6,70},{7,71},{8,72},{9,... | collective-permute-start | bytes 792584 | tf_op jit(solution)/shard_map/ppermute | solution.py:10
  99.3 8.4 %collective-permute-start.9 = (f32[129,512]{1,0:T(8,128)S(1)}, f32[129,512]{1,0:T(8,128)S(1)}, u32[]{:S(2)}, u32[]{:S(2)}) collective-permute-start(f32[129,512]{1,0:T(8,128)S(1)} %maximum_select_fusion.6), channel_id=1, source_target_pairs={{0,128},{1,129},{2,130},{3,131},{4,132},{5,133},{6,134},{7,135},{8... | collective-permute-start | bytes 792584 | tf_op jit(solution)/shard_map/ppermute | solution.py:10
  104.1 5.8 %copy-start.4 = (bf16[2,2048,512]{2,1,0:T(8,128)(2,1)S(1)}, bf16[2,2048,512]{2,1,0:T(8,128)(2,1)}, u32[]{:S(2)}) copy-start(bf16[2,2048,512]{2,1,0:T(8,128)(2,1)} %param.9) | copy-start | bytes 12582916
  109.9 2.7 %copy-start.2 = (f32[1,128,512]{2,1,0:T(8,128)S(1)}, f32[1,128,512]{2,1,0:T(8,128)}, u32[]{:S(2)}) copy-start(f32[1,128,512]{2,1,0:T(8,128)} %param.7) | copy-start | bytes 786436
  122.2 25.8 %collective-permute-start.10 = (f32[128,512]{1,0:T(8,128)S(1)}, f32[128,512]{1,0:T(8,128)S(1)}, u32[]{:S(2)}, u32[]{:S(2)}) collective-permute-start(f32[128,512]{1,0:T(8,128)S(1)} %multiply_subtract_fusion.1), channel_id=1, source_target_pairs={{1,0},{2,1},{3,2},{4,3},{5,4},{6,5},{7,6},{8,7},{9,8},{10,9},{11,1... | collective-permute-start | bytes 786440 | tf_op jit(solution)/shard_map/ppermute | solution.py:10
  146.0 4.9 %collective-permute-start.11 = (f32[512]{0:T(512)S(1)}, f32[512]{0:T(512)S(1)}, u32[]{:S(2)}, u32[]{:S(2)}) collective-permute-start(f32[512]{0:T(512)S(1)} %reduce_prod.9), channel_id=1, source_target_pairs={{1,0},{2,1},{3,2},{4,3},{5,4},{6,5},{7,6},{8,7},{9,8},{10,9},{11,1... | collective-permute-start | bytes 6152 | tf_op jit(solution)/shard_map/ppermute | solution.py:10
  151.0 8.0 %collective-permute-start.12 = (f32[129,512]{1,0:T(8,128)S(1)}, f32[129,512]{1,0:T(8,128)}, u32[]{:S(2)}, u32[]{:S(2)}) collective-permute-start(f32[129,512]{1,0:T(8,128)S(1)} %pad_maximum_fusion.3), channel_id=1, source_target_pairs={{1,0},{2,1},{3,2},{4,3},{5,4},{6,5},{7,6},{8,7},{9,8},{10,9},{11,1... | collective-permute-start | bytes 792584 | tf_op jit(solution)/shard_map/ppermute | solution.py:10
  160.7 8.9 %collective-permute-start.13 = (f32[129,512]{1,0:T(8,128)S(1)}, f32[129,512]{1,0:T(8,128)S(1)}, u32[]{:S(2)}, u32[]{:S(2)}) collective-permute-start(f32[129,512]{1,0:T(8,128)S(1)} %maximum_select_fusion.7), channel_id=1, source_target_pairs={{2,0},{3,1},{4,2},{5,3},{6,4},{7,5},{8,6},{9,7},{10,8},{11,9},{12,... | collective-permute-start | bytes 792584 | tf_op jit(solution)/shard_map/ppermute | solution.py:10
  169.7 11.4 %collective-permute-start.14 = (f32[129,512]{1,0:T(8,128)S(1)}, f32[129,512]{1,0:T(8,128)S(1)}, u32[]{:S(2)}, u32[]{:S(2)}) collective-permute-start(f32[129,512]{1,0:T(8,128)S(1)} %maximum_select_fusion.8), channel_id=1, source_target_pairs={{4,0},{5,1},{6,2},{7,3},{8,4},{9,5},{10,6},{11,7},{12,8},{13,9},{1... | collective-permute-start | bytes 792584 | tf_op jit(solution)/shard_map/ppermute | solution.py:10
  181.2 9.8 %collective-permute-start.15 = (f32[129,512]{1,0:T(8,128)S(1)}, f32[129,512]{1,0:T(8,128)S(1)}, u32[]{:S(2)}, u32[]{:S(2)}) collective-permute-start(f32[129,512]{1,0:T(8,128)S(1)} %maximum_select_fusion.9), channel_id=1, source_target_pairs={{8,0},{9,1},{10,2},{11,3},{12,4},{13,5},{14,6},{15,7},{16,8},{17,9... | collective-permute-start | bytes 792584 | tf_op jit(solution)/shard_map/ppermute | solution.py:10
  191.1 16.9 %collective-permute-start.16 = (f32[129,512]{1,0:T(8,128)S(1)}, f32[129,512]{1,0:T(8,128)S(1)}, u32[]{:S(2)}, u32[]{:S(2)}) collective-permute-start(f32[129,512]{1,0:T(8,128)S(1)} %maximum_select_fusion.10), channel_id=1, source_target_pairs={{16,0},{17,1},{18,2},{19,3},{20,4},{21,5},{22,6},{23,7},{24,8},{25... | collective-permute-start | bytes 792584 | tf_op jit(solution)/shard_map/ppermute | solution.py:10
  208.2 13.1 %collective-permute-start.17 = (f32[129,512]{1,0:T(8,128)S(1)}, f32[129,512]{1,0:T(8,128)S(1)}, u32[]{:S(2)}, u32[]{:S(2)}) collective-permute-start(f32[129,512]{1,0:T(8,128)S(1)} %maximum_select_fusion.11), channel_id=1, source_target_pairs={{32,0},{33,1},{34,2},{35,3},{36,4},{37,5},{38,6},{39,7},{40,8},{41... | collective-permute-start | bytes 792584 | tf_op jit(solution)/shard_map/ppermute | solution.py:10
  221.3 17.5 %collective-permute-start.18 = (f32[129,512]{1,0:T(8,128)S(1)}, f32[129,512]{1,0:T(8,128)S(1)}, u32[]{:S(2)}, u32[]{:S(2)}) collective-permute-start(f32[129,512]{1,0:T(8,128)S(1)} %maximum_select_fusion.12), channel_id=1, source_target_pairs={{64,0},{65,1},{66,2},{67,3},{68,4},{69,5},{70,6},{71,7},{72,8},{73... | collective-permute-start | bytes 792584 | tf_op jit(solution)/shard_map/ppermute | solution.py:10
  239.0 10.5 %collective-permute-start.19 = (f32[129,512]{1,0:T(8,128)S(1)}, f32[129,512]{1,0:T(8,128)S(1)}, u32[]{:S(2)}, u32[]{:S(2)}) collective-permute-start(f32[129,512]{1,0:T(8,128)S(1)} %maximum_select_fusion.13), channel_id=1, source_target_pairs={{128,0},{129,1},{130,2},{131,3},{132,4},{133,5},{134,6},{135,7},{1... | collective-permute-start | bytes 792584 | tf_op jit(solution)/shard_map/ppermute | solution.py:10
  (1 other events, 2.2 us)
where the time goes:
time: 262 us; the launch traced here: 258 us
  waiting for transfers between devices  122 us (47%)
  starting transfers between devices  99 us (38%)
  matrix products  25.5 us (10%)
  other arithmetic  7.69 us (3%)
  local copies, waits for them, and re-layouts  3.08 us (1%)
    ppermute x20, waiting for transfers between devices, shifted(): return lax.ppermute(block, axis, route)  122 us
    ppermute x20, starting transfers between devices, shifted(): return lax.ppermute(block, axis, route)  99 us
    dot_general x4, matrix products, backward_block(): lax.dot_general(grad_pre, w_first, (((1,), (1,)), ((), ())), preferred_el...  16.1 us
    dot_general x3, matrix products, finish_block(): jnp.dot(hidden, w_second, preferred_element_type=jnp.float32)  6.85 us
  transfers between devices with their start and end apart: 20, of which 18 were waited for; matrix products, arithmetic and copies ran while one was open for 0% of the time, Pallas kernels for 0%

commit v1 on v0

--- a/solution.py
+++ b/solution.py
@@ -10,22 +10,43 @@
     return lax.ppermute(block, axis, route)
 
 
-def doubling_scan(factor, offset, axis, reverse):
+def later_of(later, earlier, rows):
+    scale = later[rows:]
+    return jnp.concatenate([later[:rows] + scale * earlier[:rows], scale * earlier[rows:]], axis=0)
+
+
+def chip_scan(factor, offset, axis, reverse):
     size, position = (lax.axis_size(axis), lax.axis_index(axis))
-    rows = offset.shape[0]
+    rows, width = offset.shape
+    half = width // 2
+    order = size - 1 - position if reverse else position
+    core, chip = (order % 2, order // 2)
+
+    def placed(q):
+        return size - 1 - q if reverse else q
+
+    def move(block, pairs):
+        return lax.ppermute(block, axis, [(placed(a), placed(b)) for a, b in pairs])
+
     packed = jnp.concatenate([offset, factor[None, :]], axis=0)
+    mine = lax.dynamic_slice_in_dim(packed, core * half, half, axis=1)
+    other = lax.dynamic_slice_in_dim(packed, (1 - core) * half, half, axis=1)
+    swap = [(q, q + 1) for q in range(0, size, 2)] + [(q + 1, q) for q in range(0, size, 2)]
+    got = move(other, swap)
+    first = core == 0
+    total = later_of(jnp.where(first, got, mine), jnp.where(first, mine, got), rows)
+    chips = size // 2
     distance = 1
-    while distance < size:
-        step = -distance if reverse else distance
-        came = shifted(packed, axis, step)
-        reached = position + distance < size if reverse else position >= distance
-        scale = packed[rows:]
-        joined = jnp.concatenate(
-            [packed[:rows] + scale * came[:rows], scale * came[rows:]], axis=0
-        )
-        packed = jnp.where(reached, joined, packed)
+    while distance < chips:
+        came = move(total, [(q, q + 2 * distance) for q in range(size - 2 * distance)])
+        total = jnp.where(chip >= distance, later_of(total, came, rows), total)
         distance *= 2
-    return packed[:rows]
+    near = move(total, [(q, q + 1) for q in range(size - 1)])
+    far = move(total, [(q, q + 2) for q in range(0, size - 2, 2)])
+    second_full = jnp.concatenate([near[:rows], total[:rows]], axis=1)
+    before = jnp.concatenate([far[:rows], near[:rows]], axis=1)
+    first_full = jnp.where(chip >= 1, offset + factor[None, :] * before, offset)
+    return jnp.where(first, first_full, second_full)
 
 
 def prepare_block(state, w_first, gain_row):
@@ -106,7 +127,7 @@
     end_state, _, _, _ = relax_forward(guess_state, w_in, w_out, norm_gain, decay, True)
     end_before = shifted(end_state, "depth", 1)
     resid = jnp.where(at_first, jnp.zeros_like(guess_state), end_before - guess_state)
-    correction = doubling_scan(factor_before, resid, "depth", False)
+    correction = chip_scan(factor_before, resid, "depth", False)
     start = guess_state + correction
     _, states, inverses, preacts = relax_forward(start, w_in, w_out, norm_gain, decay, False)
     guess_adjoint = adjoint_guess[0]
@@ -115,7 +136,7 @@
     )
     first_after = shifted(first_adjoint, "depth", -1)
     rho = jnp.where(at_last, jnp.zeros_like(guess_adjoint), first_after - guess_adjoint)
-    eps = doubling_scan(factor_after, rho, "depth", True)
+    eps = chip_scan(factor_after, rho, "depth", True)
     head = guess_adjoint + eps
     _, lambdas = relax_backward(head, states, inverses, preacts, w_in, w_out, norm_gain, decay)
     return (jnp.stack(states), jnp.stack(lambdas))

time: 262 us -> 220 us (0.84)
  the two profiles are of different devices: /device:TPU:1 before, /device:TPU:17 now
where the time goes in v1:
time: 220 us; the launch traced here: 219 us
  waiting for transfers between devices  92.7 us (42%)
  starting transfers between devices  91.6 us (42%)
  matrix products  25.6 us (12%)
  other arithmetic  4.51 us (2%)
  local copies, waits for them, and re-layouts  3.15 us (1%)
    ppermute x20, waiting for transfers between devices, move(): return lax.ppermute(block, axis, [(placed(a), placed(b)) for a, b in pairs])  88.5 us
    ppermute x20, starting transfers between devices, move(): return lax.ppermute(block, axis, [(placed(a), placed(b)) for a, b in pairs])  74.5 us
    ppermute x4, starting transfers between devices, shifted(): return lax.ppermute(block, axis, route)  17 us
    dot_general x4, matrix products, backward_block(): lax.dot_general(grad_pre, w_first, (((1,), (1,)), ((), ())), preferred_el...  16.2 us
    dot_general x3, matrix products, finish_block(): jnp.dot(hidden, w_second, preferred_element_type=jnp.float32)  6.85 us
  transfers between devices with their start and end apart: 24, of which 20 were waited for; matrix products, arithmetic and copies ran while one was open for 0% of the time, Pallas kernels for 0%

profile of v1, /device:TPU:17, one launch (start us, length us, event | category | flops | bytes accessed | tf_op | source)
XLA Modules:
  0.0 219.0 jit_solution(8206496954584182729)
XLA Ops:
  9.5 3.7 %collective-permute-start = (f32[128,512]{1,0:T(8,128)S(1)}, f32[128,512]{1,0:T(8,128)S(1)}, u32[]{:S(2)}, u32[]{:S(2)}) collective-permute-start(f32[128,512]{1,0:T(8,128)S(1)} %fusion.67), channel_id=1, source_target_pairs={{0,1},{1,2},{2,3},{3,4},{4,5},{5,6},{6,7},{7,8},{8,9},{9,10},{10,1... | collective-permute-start | bytes 786440 | tf_op jit(solution)/shard_map/ppermute | solution.py:10
  16.5 7.1 %collective-permute-start.2 = (f32[129,256]{1,0:T(8,128)S(1)}, f32[129,256]{1,0:T(8,128)S(1)}, u32[]{:S(2)}, u32[]{:S(2)}) collective-permute-start(f32[129,256]{1,0:T(8,128)S(1)} %fusion.105), channel_id=1, source_target_pairs={{0,1},{2,3},{4,5},{6,7},{8,9},{10,11},{12,13},{14,15},{16,17},{18,... | collective-permute-start | bytes 396296 | tf_op jit(solution)/shard_map/ppermute | solution.py:29
  26.7 9.1 %collective-permute-done.3 = f32[129,256]{1,0:T(8,128)S(1)} collective-permute-done((f32[129,256]{1,0:T(8,128)S(1)}, f32[129,256]{1,0:T(8,128)S(1)}, u32[]{:S(2)}, u32[]{:S(2)}) %collective-permute-start.3) | collective-permute-done | bytes 132128 | tf_op jit(solution)/shard_map/ppermute | solution.py:29
  37.7 8.4 %collective-permute-done.4 = f32[129,256]{1,0:T(8,128)S(1)} collective-permute-done((f32[129,256]{1,0:T(8,128)S(1)}, f32[129,256]{1,0:T(8,128)S(1)}, u32[]{:S(2)}, u32[]{:S(2)}) %collective-permute-start.4) | collective-permute-done | bytes 132128 | tf_op jit(solution)/shard_map/ppermute | solution.py:29
  48.1 6.0 %collective-permute-done.5 = f32[129,256]{1,0:T(8,128)S(1)} collective-permute-done((f32[129,256]{1,0:T(8,128)S(1)}, f32[129,256]{1,0:T(8,128)S(1)}, u32[]{:S(2)}, u32[]{:S(2)}) %collective-permute-start.5) | collective-permute-done | bytes 132128 | tf_op jit(solution)/shard_map/ppermute | solution.py:29
  56.1 7.1 %collective-permute-done.6 = f32[129,256]{1,0:T(8,128)S(1)} collective-permute-done((f32[129,256]{1,0:T(8,128)S(1)}, f32[129,256]{1,0:T(8,128)S(1)}, u32[]{:S(2)}, u32[]{:S(2)}) %collective-permute-start.6) | collective-permute-done | bytes 132128 | tf_op jit(solution)/shard_map/ppermute | solution.py:29
  65.9 8.2 %collective-permute-done.7 = f32[129,256]{1,0:T(8,128)S(1)} collective-permute-done((f32[129,256]{1,0:T(8,128)S(1)}, f32[129,256]{1,0:T(8,128)S(1)}, u32[]{:S(2)}, u32[]{:S(2)}) %collective-permute-start.7) | collective-permute-done | bytes 132128 | tf_op jit(solution)/shard_map/ppermute | solution.py:29
  74.2 3.2 %collective-permute-start.8 = (f32[129,256]{1,0:T(8,128)S(1)}, f32[129,256]{1,0:T(8,128)S(1)}, u32[]{:S(2)}, u32[]{:S(2)}) collective-permute-start(f32[129,256]{1,0:T(8,128)S(1)} %maximum_select_fusion.4), channel_id=1, source_target_pairs={{0,64},{1,65},{2,66},{3,67},{4,68},{5,69},{6,70},{7,71},{8,72},{9,... | collective-permute-start | bytes 396296 | tf_op jit(solution)/shard_map/ppermute | solution.py:29
  81.6 6.0 %collective-permute-done.9 = f32[129,256]{1,0:T(8,128)S(1)} collective-permute-done((f32[129,256]{1,0:T(8,128)S(1)}, f32[129,256]{1,0:T(8,128)S(1)}, u32[]{:S(2)}, u32[]{:S(2)}) %collective-permute-start.9) | collective-permute-done | bytes 132128 | tf_op jit(solution)/shard_map/ppermute | solution.py:29
  88.3 8.5 %collective-permute-start.11 = (f32[129,256]{1,0:T(8,128)S(1)}, f32[129,256]{1,0:T(8,128)S(1)}, u32[]{:S(2)}, u32[]{:S(2)}) collective-permute-start(f32[129,256]{1,0:T(8,128)S(1)} %maximum_select_fusion.6), channel_id=1, source_target_pairs={{0,1},{1,2},{2,3},{3,4},{4,5},{5,6},{6,7},{7,8},{8,9},{9,10},{10,1... | collective-permute-start | bytes 396296 | tf_op jit(solution)/shard_map/ppermute | solution.py:29
  105.0 4.3 %multiply_reduce_fusion.3 = (f32[128]{0:T(128)S(1)}, f32[128,512]{1,0:T(8,128)S(1)}) fusion(f32[128,512]{1,0:T(8,128)S(1)} %get-tuple-element.47, f32[512]{0:T(512)S(1)} %bitcast.169, bf16[2,512,2048]{2,1,0:T(8,128)(2,1)} %param.8, bf16[2,2048,512]{2,1,0:T(8,128)(2,1)} %param.9, f32[128,2048]{1,0:T(8,128)S(1)} %fusion.16, f32[1,128,512]{2,1,0:T(8,128)S(1)} %copy-done.2), kind=kOutput, calls=%fused_computation.108 | convolution fusion | flops 539492224 | bytes 6031872 | tf_op jit(solution)/shard_map/dot_general | solution.py:73
  109.4 3.9 %multiply_reduce_fusion.2 = (f32[128]{0:T(128)S(1)}, f32[128,512]{1,0:T(8,128)S(1)}) fusion(f32[128,512]{1,0:T(8,128)S(1)} %get-tuple-element.3, f32[512]{0:T(512)S(1)} %bitcast.165, bf16[2,512,2048]{2,1,0:T(8,128)(2,1)} %param.8, bf16[2,2048,512]{2,1,0:T(8,128)(2,1)} %param.9, f32[128,2048]{1,0:T(8,128)S(1)} %fusion.30, f32[128,512]{1,0:T(8,128)S(1)} %fusion.98), kind=kOutput, calls=%fused_computation.107 | convolution fusion | flops 539492224 | bytes 6031872 | tf_op jit(solution)/shard_map/dot_general | solution.py:73
  113.5 9.5 %collective-permute-start.12 = (f32[128,512]{1,0:T(8,128)S(1)}, f32[128,512]{1,0:T(8,128)S(1)}, u32[]{:S(2)}, u32[]{:S(2)}) collective-permute-start(f32[128,512]{1,0:T(8,128)S(1)} %multiply_subtract_fusion.1), channel_id=1, source_target_pairs={{1,0},{2,1},{3,2},{4,3},{5,4},{6,5},{7,6},{8,7},{9,8},{10,9},{11,1... | collective-permute-start | bytes 786440 | tf_op jit(solution)/shard_map/ppermute | solution.py:10
  129.5 7.7 %collective-permute-start.15 = (f32[129,256]{1,0:T(8,128)S(1)}, f32[129,256]{1,0:T(8,128)S(1)}, u32[]{:S(2)}, u32[]{:S(2)}) collective-permute-start(f32[129,256]{1,0:T(8,128)S(1)} %pad_maximum_fusion.3), channel_id=1, source_target_pairs={{255,253},{254,252},{253,251},{252,250},{251,249},{250,248},{249,2... | collective-permute-start | bytes 396296 | tf_op jit(solution)/shard_map/ppermute | solution.py:29
  140.2 4.1 %collective-permute-start.16 = (f32[129,256]{1,0:T(8,128)S(1)}, f32[129,256]{1,0:T(8,128)S(1)}, u32[]{:S(2)}, u32[]{:S(2)}) collective-permute-start(f32[129,256]{1,0:T(8,128)S(1)} %maximum_select_fusion.7), channel_id=1, source_target_pairs={{255,251},{254,250},{253,249},{252,248},{251,247},{250,246},{249,2... | collective-permute-start | bytes 396296 | tf_op jit(solution)/shard_map/ppermute | solution.py:29
  144.3 3.5 %collective-permute-done.16 = f32[129,256]{1,0:T(8,128)S(1)} collective-permute-done((f32[129,256]{1,0:T(8,128)S(1)}, f32[129,256]{1,0:T(8,128)S(1)}, u32[]{:S(2)}, u32[]{:S(2)}) %collective-permute-start.16) | collective-permute-done | bytes 132128 | tf_op jit(solution)/shard_map/ppermute | solution.py:29
  149.9 3.8 %collective-permute-done.17 = f32[129,256]{1,0:T(8,128)S(1)} collective-permute-done((f32[129,256]{1,0:T(8,128)S(1)}, f32[129,256]{1,0:T(8,128)S(1)}, u32[]{:S(2)}, u32[]{:S(2)}) %collective-permute-start.17) | collective-permute-done | bytes 132128 | tf_op jit(solution)/shard_map/ppermute | solution.py:29
  155.6 7.9 %collective-permute-done.18 = f32[129,256]{1,0:T(8,128)S(1)} collective-permute-done((f32[129,256]{1,0:T(8,128)S(1)}, f32[129,256]{1,0:T(8,128)S(1)}, u32[]{:S(2)}, u32[]{:S(2)}) %collective-permute-start.18) | collective-permute-done | bytes 132128 | tf_op jit(solution)/shard_map/ppermute | solution.py:29
  165.6 8.3 %collective-permute-done.19 = f32[129,256]{1,0:T(8,128)S(1)} collective-permute-done((f32[129,256]{1,0:T(8,128)S(1)}, f32[129,256]{1,0:T(8,128)S(1)}, u32[]{:S(2)}, u32[]{:S(2)}) %collective-permute-start.19) | collective-permute-done | bytes 132128 | tf_op jit(solution)/shard_map/ppermute | solution.py:29
  175.8 3.9 %collective-permute-done.20 = f32[129,256]{1,0:T(8,128)S(1)} collective-permute-done((f32[129,256]{1,0:T(8,128)S(1)}, f32[129,256]{1,0:T(8,128)S(1)}, u32[]{:S(2)}, u32[]{:S(2)}) %collective-permute-start.20) | collective-permute-done | bytes 132128 | tf_op jit(solution)/shard_map/ppermute | solution.py:29
  183.1 20.2 %collective-permute-start.22 = (f32[129,256]{1,0:T(8,128)S(1)}, f32[129,256]{1,0:T(8,128)S(1)}, u32[]{:S(2)}, u32[]{:S(2)}) collective-permute-start(f32[129,256]{1,0:T(8,128)S(1)} %maximum_select_fusion.13), channel_id=1, source_target_pairs={{255,253},{253,251},{251,249},{249,247},{247,245},{245,243},{243,2... | collective-permute-start | bytes 396296 | tf_op jit(solution)/shard_map/ppermute | solution.py:29
  206.1 3.6 %collective-permute-done.23 = f32[129,256]{1,0:T(8,128)S(1)} collective-permute-done((f32[129,256]{1,0:T(8,128)S(1)}, f32[129,256]{1,0:T(8,128)S(1)}, u32[]{:S(2)}, u32[]{:S(2)}) %collective-permute-start.23) | collective-permute-done | bytes 132128 | tf_op jit(solution)/shard_map/ppermute | solution.py:29
  209.8 4.2 %multiply_reduce_fusion.1 = (f32[128]{0:T(128)S(1)}, f32[128,512]{1,0:T(8,128)S(1)}) fusion(f32[128,512]{1,0:T(8,128)S(1)} %get-tuple-element.47, f32[512]{0:T(512)S(1)} %bitcast.170, bf16[2,512,2048]{2,1,0:T(8,128)(2,1)} %param.8, bf16[2,2048,512]{2,1,0:T(8,128)(2,1)} %param.9, f32[128,2048]{1,0:T(8,128)} %copy-done.3, f32[128,512]{1,0:T(8,128)S(1)} %fusion.96), kind=kOutput, calls=%fused_computation.105 | convolution fusion | flops 539492224 | bytes 6031872 | tf_op jit(solution)/shard_map/dot_general | solution.py:73
  214.1 3.9 %multiply_reduce_fusion = (f32[128]{0:T(128)S(1)}, f32[128,512]{1,0:T(8,128)S(1)}) fusion(f32[128,512]{1,0:T(8,128)S(1)} %get-tuple-element.3, f32[512]{0:T(512)S(1)} %bitcast.166, bf16[2,512,2048]{2,1,0:T(8,128)(2,1)} %param.8, bf16[2,2048,512]{2,1,0:T(8,128)(2,1)} %param.9, f32[128,2048]{1,0:T(8,128)S(1)} %fusion.30, ...), kind=kOutput, calls=%fused_computation.103 | convolution fusion | flops 539492224 | bytes 6031872 | tf_op jit(solution)/shard_map/dot_general | solution.py:73
  (125 shorter events, 61.7 us)
Async XLA Ops:
  9.5 7.0 %collective-permute-start = (f32[128,512]{1,0:T(8,128)S(1)}, f32[128,512]{1,0:T(8,128)S(1)}, u32[]{:S(2)}, u32[]{:S(2)}) collective-permute-start(f32[128,512]{1,0:T(8,128)S(1)} %fusion.67), channel_id=1, source_target_pairs={{0,1},{1,2},{2,3},{3,4},{4,5},{5,6},{6,7},{7,8},{8,9},{9,10},{10,1... | collective-permute-start | bytes 786440 | tf_op jit(solution)/shard_map/ppermute | solution.py:10
  13.2 3.3 %collective-permute-start.1 = (f32[512]{0:T(512)S(1)}, f32[512]{0:T(512)S(1)}, u32[]{:S(2)}, u32[]{:S(2)}) collective-permute-start(f32[512]{0:T(512)S(1)} %reduce_prod.9), channel_id=1, source_target_pairs={{0,1},{1,2},{2,3},{3,4},{4,5},{5,6},{6,7},{7,8},{8,9},{9,10},{10,1... | collective-permute-start | bytes 6152 | tf_op jit(solution)/shard_map/ppermute | solution.py:10
  16.5 8.1 %collective-permute-start.2 = (f32[129,256]{1,0:T(8,128)S(1)}, f32[129,256]{1,0:T(8,128)S(1)}, u32[]{:S(2)}, u32[]{:S(2)}) collective-permute-start(f32[129,256]{1,0:T(8,128)S(1)} %fusion.105), channel_id=1, source_target_pairs={{0,1},{2,3},{4,5},{6,7},{8,9},{10,11},{12,13},{14,15},{16,17},{18,... | collective-permute-start | bytes 396296 | tf_op jit(solution)/shard_map/ppermute | solution.py:29
  24.7 11.0 %collective-permute-start.3 = (f32[129,256]{1,0:T(8,128)S(1)}, f32[129,256]{1,0:T(8,128)S(1)}, u32[]{:S(2)}, u32[]{:S(2)}) collective-permute-start(f32[129,256]{1,0:T(8,128)S(1)} %pad_maximum_fusion.2), channel_id=1, source_target_pairs={{0,2},{1,3},{2,4},{3,5},{4,6},{5,7},{6,8},{7,9},{8,10},{9,11},{10,... | collective-permute-start | bytes 396296 | tf_op jit(solution)/shard_map/ppermute | solution.py:29
  35.8 10.3 %collective-permute-start.4 = (f32[129,256]{1,0:T(8,128)S(1)}, f32[129,256]{1,0:T(8,128)S(1)}, u32[]{:S(2)}, u32[]{:S(2)}) collective-permute-start(f32[129,256]{1,0:T(8,128)S(1)} %maximum_select_fusion), channel_id=1, source_target_pairs={{0,4},{1,5},{2,6},{3,7},{4,8},{5,9},{6,10},{7,11},{8,12},{9,13},{1... | collective-permute-start | bytes 396296 | tf_op jit(solution)/shard_map/ppermute | solution.py:29
  46.2 7.9 %collective-permute-start.5 = (f32[129,256]{1,0:T(8,128)S(1)}, f32[129,256]{1,0:T(8,128)S(1)}, u32[]{:S(2)}, u32[]{:S(2)}) collective-permute-start(f32[129,256]{1,0:T(8,128)S(1)} %maximum_select_fusion.1), channel_id=1, source_target_pairs={{0,8},{1,9},{2,10},{3,11},{4,12},{5,13},{6,14},{7,15},{8,16},{9,17... | collective-permute-start | bytes 396296 | tf_op jit(solution)/shard_map/ppermute | solution.py:29
  54.1 9.1 %collective-permute-start.6 = (f32[129,256]{1,0:T(8,128)S(1)}, f32[129,256]{1,0:T(8,128)S(1)}, u32[]{:S(2)}, u32[]{:S(2)}) collective-permute-start(f32[129,256]{1,0:T(8,128)S(1)} %maximum_select_fusion.2), channel_id=1, source_target_pairs={{0,16},{1,17},{2,18},{3,19},{4,20},{5,21},{6,22},{7,23},{8,24},{9,... | collective-permute-start | bytes 396296 | tf_op jit(solution)/shard_map/ppermute | solution.py:29
  63.3 10.9 %collective-permute-start.7 = (f32[129,256]{1,0:T(8,128)S(1)}, f32[129,256]{1,0:T(8,128)S(1)}, u32[]{:S(2)}, u32[]{:S(2)}) collective-permute-start(f32[129,256]{1,0:T(8,128)S(1)} %maximum_select_fusion.3), channel_id=1, source_target_pairs={{0,32},{1,33},{2,34},{3,35},{4,36},{5,37},{6,38},{7,39},{8,40},{9,... | collective-permute-start | bytes 396296 | tf_op jit(solution)/shard_map/ppermute | solution.py:29
  74.2 6.0 %collective-permute-start.8 = (f32[129,256]{1,0:T(8,128)S(1)}, f32[129,256]{1,0:T(8,128)S(1)}, u32[]{:S(2)}, u32[]{:S(2)}) collective-permute-start(f32[129,256]{1,0:T(8,128)S(1)} %maximum_select_fusion.4), channel_id=1, source_target_pairs={{0,64},{1,65},{2,66},{3,67},{4,68},{5,69},{6,70},{7,71},{8,72},{9,... | collective-permute-start | bytes 396296 | tf_op jit(solution)/shard_map/ppermute | solution.py:29
  80.3 7.3 %collective-permute-start.9 = (f32[129,256]{1,0:T(8,128)S(1)}, f32[129,256]{1,0:T(8,128)S(1)}, u32[]{:S(2)}, u32[]{:S(2)}) collective-permute-start(f32[129,256]{1,0:T(8,128)S(1)} %maximum_select_fusion.5), channel_id=1, source_target_pairs={{0,128},{1,129},{2,130},{3,131},{4,132},{5,133},{6,134},{7,135},{8... | collective-permute-start | bytes 396296 | tf_op jit(solution)/shard_map/ppermute | solution.py:29
  87.6 9.2 %collective-permute-start.10 = (f32[129,256]{1,0:T(8,128)S(1)}, f32[129,256]{1,0:T(8,128)S(1)}, u32[]{:S(2)}, u32[]{:S(2)}) collective-permute-start(f32[129,256]{1,0:T(8,128)S(1)} %maximum_select_fusion.6), channel_id=1, source_target_pairs={{0,2},{2,4},{4,6},{6,8},{8,10},{10,12},{12,14},{14,16},{16,18},{18... | collective-permute-start | bytes 396296 | tf_op jit(solution)/shard_map/ppermute | solution.py:29
  88.3 11.7 %collective-permute-start.11 = (f32[129,256]{1,0:T(8,128)S(1)}, f32[129,256]{1,0:T(8,128)S(1)}, u32[]{:S(2)}, u32[]{:S(2)}) collective-permute-start(f32[129,256]{1,0:T(8,128)S(1)} %maximum_select_fusion.6), channel_id=1, source_target_pairs={{0,1},{1,2},{2,3},{3,4},{4,5},{5,6},{6,7},{7,8},{8,9},{9,10},{10,1... | collective-permute-start | bytes 396296 | tf_op jit(solution)/shard_map/ppermute | solution.py:29
  113.5 11.5 %collective-permute-start.12 = (f32[128,512]{1,0:T(8,128)S(1)}, f32[128,512]{1,0:T(8,128)S(1)}, u32[]{:S(2)}, u32[]{:S(2)}) collective-permute-start(f32[128,512]{1,0:T(8,128)S(1)} %multiply_subtract_fusion.1), channel_id=1, source_target_pairs={{1,0},{2,1},{3,2},{4,3},{5,4},{6,5},{7,6},{8,7},{9,8},{10,9},{11,1... | collective-permute-start | bytes 786440 | tf_op jit(solution)/shard_map/ppermute | solution.py:10
  123.0 4.9 %collective-permute-start.13 = (f32[512]{0:T(512)S(1)}, f32[512]{0:T(512)S(1)}, u32[]{:S(2)}, u32[]{:S(2)}) collective-permute-start(f32[512]{0:T(512)S(1)} %reduce_prod.9), channel_id=1, source_target_pairs={{1,0},{2,1},{3,2},{4,3},{5,4},{6,5},{7,6},{8,7},{9,8},{10,9},{11,1... | collective-permute-start | bytes 6152 | tf_op jit(solution)/shard_map/ppermute | solution.py:10
  128.0 1.4 collective-permute-start.14
  129.5 10.6 %collective-permute-start.15 = (f32[129,256]{1,0:T(8,128)S(1)}, f32[129,256]{1,0:T(8,128)S(1)}, u32[]{:S(2)}, u32[]{:S(2)}) collective-permute-start(f32[129,256]{1,0:T(8,128)S(1)} %pad_maximum_fusion.3), channel_id=1, source_target_pairs={{255,253},{254,252},{253,251},{252,250},{251,249},{250,248},{249,2... | collective-permute-start | bytes 396296 | tf_op jit(solution)/shard_map/ppermute | solution.py:29
  140.2 7.6 %collective-permute-start.16 = (f32[129,256]{1,0:T(8,128)S(1)}, f32[129,256]{1,0:T(8,128)S(1)}, u32[]{:S(2)}, u32[]{:S(2)}) collective-permute-start(f32[129,256]{1,0:T(8,128)S(1)} %maximum_select_fusion.7), channel_id=1, source_target_pairs={{255,251},{254,250},{253,249},{252,248},{251,247},{250,246},{249,2... | collective-permute-start | bytes 396296 | tf_op jit(solution)/shard_map/ppermute | solution.py:29
  147.9 5.8 %collective-permute-start.17 = (f32[129,256]{1,0:T(8,128)S(1)}, f32[129,256]{1,0:T(8,128)S(1)}, u32[]{:S(2)}, u32[]{:S(2)}) collective-permute-start(f32[129,256]{1,0:T(8,128)S(1)} %maximum_select_fusion.8), channel_id=1, source_target_pairs={{255,247},{254,246},{253,245},{252,244},{251,243},{250,242},{249,2... | collective-permute-start | bytes 396296 | tf_op jit(solution)/shard_map/ppermute | solution.py:29
  153.7 9.8 %collective-permute-start.18 = (f32[129,256]{1,0:T(8,128)S(1)}, f32[129,256]{1,0:T(8,128)S(1)}, u32[]{:S(2)}, u32[]{:S(2)}) collective-permute-start(f32[129,256]{1,0:T(8,128)S(1)} %maximum_select_fusion.9), channel_id=1, source_target_pairs={{255,239},{254,238},{253,237},{252,236},{251,235},{250,234},{249,2... | collective-permute-start | bytes 396296 | tf_op jit(solution)/shard_map/ppermute | solution.py:29
  163.6 10.2 %collective-permute-start.19 = (f32[129,256]{1,0:T(8,128)S(1)}, f32[129,256]{1,0:T(8,128)S(1)}, u32[]{:S(2)}, u32[]{:S(2)}) collective-permute-start(f32[129,256]{1,0:T(8,128)S(1)} %maximum_select_fusion.10), channel_id=1, source_target_pairs={{255,223},{254,222},{253,221},{252,220},{251,219},{250,218},{249,2... | collective-permute-start | bytes 396296 | tf_op jit(solution)/shard_map/ppermute | solution.py:29
  173.9 5.8 %collective-permute-start.20 = (f32[129,256]{1,0:T(8,128)S(1)}, f32[129,256]{1,0:T(8,128)S(1)}, u32[]{:S(2)}, u32[]{:S(2)}) collective-permute-start(f32[129,256]{1,0:T(8,128)S(1)} %maximum_select_fusion.11), channel_id=1, source_target_pairs={{255,191},{254,190},{253,189},{252,188},{251,187},{250,186},{249,1... | collective-permute-start | bytes 396296 | tf_op jit(solution)/shard_map/ppermute | solution.py:29
  179.7 3.3 %collective-permute-start.21 = (f32[129,256]{1,0:T(8,128)S(1)}, f32[129,256]{1,0:T(8,128)S(1)}, u32[]{:S(2)}, u32[]{:S(2)}) collective-permute-start(f32[129,256]{1,0:T(8,128)S(1)} %maximum_select_fusion.12), channel_id=1, source_target_pairs={{255,127},{254,126},{253,125},{252,124},{251,123},{250,122},{249,1... | collective-permute-start | bytes 396296 | tf_op jit(solution)/shard_map/ppermute | solution.py:29
  183.1 23.0 %collective-permute-start.22 = (f32[129,256]{1,0:T(8,128)S(1)}, f32[129,256]{1,0:T(8,128)S(1)}, u32[]{:S(2)}, u32[]{:S(2)}) collective-permute-start(f32[129,256]{1,0:T(8,128)S(1)} %maximum_select_fusion.13), channel_id=1, source_target_pairs={{255,253},{253,251},{251,249},{249,247},{247,245},{245,243},{243,2... | collective-permute-start | bytes 396296 | tf_op jit(solution)/shard_map/ppermute | solution.py:29
  203.3 6.4 %collective-permute-start.23 = (f32[129,256]{1,0:T(8,128)S(1)}, f32[129,256]{1,0:T(8,128)S(1)}, u32[]{:S(2)}, u32[]{:S(2)}) collective-permute-start(f32[129,256]{1,0:T(8,128)S(1)} %maximum_select_fusion.13), channel_id=1, source_target_pairs={{255,254},{254,253},{253,252},{252,251},{251,250},{250,249},{249,2... | collective-permute-start | bytes 396296 | tf_op jit(solution)/shard_map/ppermute | solution.py:29
  (6 other events, 46.7 us)

commit v2 on v0

--- a/solution.py
+++ b/solution.py
@@ -1,6 +1,10 @@
+import functools
+
 import jax
 import jax.numpy as jnp
 from jax import lax
+from jax.experimental import pallas as pl
+from jax.experimental.pallas import tpu as pltpu
 from jax.sharding import PartitionSpec as P
 
 
@@ -10,22 +14,106 @@
     return lax.ppermute(block, axis, route)
 
 
-def doubling_scan(factor, offset, axis, reverse):
-    size, position = (lax.axis_size(axis), lax.axis_index(axis))
-    rows = offset.shape[0]
-    packed = jnp.concatenate([offset, factor[None, :]], axis=0)
+MESH = pl.DeviceIdType.MESH
+
+
+def joined(later, earlier, rows):
+    scale = later[rows : rows + 1, :]
+    top = later[:rows, :] + scale * earlier[:rows, :]
+    return jnp.concatenate([top, later[rows:, :] * earlier[rows:, :]], axis=0)
+
+
+def scan_kernel(size, reverse, mine_ref, other_ref, offset_ref, factor_ref, out_ref, got, total, sends, recvs):
+    position = lax.axis_index("depth")
+    order = size - 1 - position if reverse else position
+    core, chip = (order % 2, order // 2)
+    rows = offset_ref.shape[0]
+    half = mine_ref.shape[1]
+    chips = size // 2
+    hops = []
     distance = 1
-    while distance < size:
-        step = -distance if reverse else distance
-        came = shifted(packed, axis, step)
-        reached = position + distance < size if reverse else position >= distance
-        scale = packed[rows:]
-        joined = jnp.concatenate(
-            [packed[:rows] + scale * came[:rows], scale * came[rows:]], axis=0
+    while distance < chips:
+        hops.append(2 * distance)
+        distance *= 2
+
+    def device(q):
+        q = lax.rem(q + 2 * size, size)
+        return (size - 1 - q if reverse else q,)
+
+    partner = order + 1 - 2 * core
+    barrier = pltpu.get_barrier_semaphore()
+    targets = [partner] + [order + h for h in hops] + [order - h for h in hops]
+    targets += [order + 1, order - 1, order + 2, order - 2]
+    for target in targets:
+        pl.semaphore_signal(barrier, inc=1, device_id=device(target), device_id_type=MESH)
+    pl.semaphore_wait(barrier, len(targets))
+
+    def send(src, slot, target):
+        copy = pltpu.make_async_remote_copy(
+            src_ref=src,
+            dst_ref=got.at[slot],
+            send_sem=sends.at[slot],
+            recv_sem=recvs.at[slot],
+            device_id=device(target),
+            device_id_type=MESH,
         )
-        packed = jnp.where(reached, joined, packed)
-        distance *= 2
-    return packed[:rows]
+        copy.start()
+        return copy
+
+    send(other_ref, 0, partner).wait()
+    first = core == 0
+    mine = mine_ref[...]
+    came = got[0]
+    total[0] = joined(jnp.where(first, came, mine), jnp.where(first, mine, came), rows)
+    for step, hop in enumerate(hops):
+        send(total.at[step], step + 1, order + hop).wait()
+        held = total[step]
+        total[step + 1] = jnp.where(chip >= hop // 2, joined(held, got[step + 1], rows), held)
+    last = len(hops)
+    near = send(total.at[last], last + 1, order + 1)
+    far = send(total.at[last], last + 2, order + 2)
+    near.wait()
+    far.wait()
+    close = got[last + 1, :rows, :]
+    own = total[last, :rows, :]
+    before_left = got[last + 2, :rows, :]
+    offset_left = offset_ref[:, :half]
+    offset_right = offset_ref[:, half:]
+    factor_left = factor_ref[0:1, :half]
+    factor_right = factor_ref[0:1, half:]
+    early = chip >= 1
+    out_ref[:, :half] = jnp.where(
+        first, jnp.where(early, offset_left + factor_left * before_left, offset_left), close
+    )
+    out_ref[:, half:] = jnp.where(
+        first, jnp.where(early, offset_right + factor_right * close, offset_right), own
+    )
+
+
+def kernel_scan(factor, offset, reverse, ident):
+    size, position = (lax.axis_size("depth"), lax.axis_index("depth"))
+    rows, width = offset.shape
+    half = width // 2
+    order = size - 1 - position if reverse else position
+    core = order % 2
+    spread = jnp.broadcast_to(factor[None, :], (8, width))
+    packed = jnp.concatenate([offset, spread], axis=0)
+    mine = lax.dynamic_slice_in_dim(packed, core * half, half, axis=1)
+    other = lax.dynamic_slice_in_dim(packed, (1 - core) * half, half, axis=1)
+    stages = 3 + (size // 2).bit_length() - 1
+    return pl.pallas_call(
+        functools.partial(scan_kernel, size, reverse),
+        out_shape=jax.ShapeDtypeStruct((rows, width), jnp.float32),
+        in_specs=[pl.BlockSpec(memory_space=pltpu.VMEM)] * 4,
+        out_specs=pl.BlockSpec(memory_space=pltpu.VMEM),
+        scratch_shapes=[
+            pltpu.VMEM((stages, rows + 8, half), jnp.float32),
+            pltpu.VMEM((stages - 2, rows + 8, half), jnp.float32),
+            pltpu.SemaphoreType.DMA((stages,)),
+            pltpu.SemaphoreType.DMA((stages,)),
+        ],
+        compiler_params=pltpu.CompilerParams(collective_id=ident, has_side_effects=True),
+    )(mine, other, offset, spread)
 
 
 def prepare_block(state, w_first, gain_row):
@@ -106,7 +194,7 @@
     end_state, _, _, _ = relax_forward(guess_state, w_in, w_out, norm_gain, decay, True)
     end_before = shifted(end_state, "depth", 1)
     resid = jnp.where(at_first, jnp.zeros_like(guess_state), end_before - guess_state)
-    correction = doubling_scan(factor_before, resid, "depth", False)
+    correction = kernel_scan(factor_before, resid, False, 0)
     start = guess_state + correction
     _, states, inverses, preacts = relax_forward(start, w_in, w_out, norm_gain, decay, False)
     guess_adjoint = adjoint_guess[0]
@@ -115,7 +203,7 @@
     )
     first_after = shifted(first_adjoint, "depth", -1)
     rho = jnp.where(at_last, jnp.zeros_like(guess_adjoint), first_after - guess_adjoint)
-    eps = doubling_scan(factor_after, rho, "depth", True)
+    eps = kernel_scan(factor_after, rho, True, 1)
     head = guess_adjoint + eps
     _, lambdas = relax_backward(head, states, inverses, preacts, w_in, w_out, norm_gain, decay)
     return (jnp.stack(states), jnp.stack(lambdas))

time: 262 us -> 177 us (0.68)
  waiting for transfers between devices: 122 us -> 3.39 us
  Pallas kernels: 0 us -> 112 us
  starting transfers between devices: 99 us -> 22.7 us
    ppermute x20 -> x4, waiting for transfers between devices: 122 us -> 3.39 us  [shifted(): return lax.ppermute(block, axis, route)]
    pallas_call x0 -> x2, Pallas kernels: none -> 112 us  [kernel_scan(): pl.pallas_call(functools.partial(scan_kernel, size, reverse), out_shape=j...]
    ppermute x20 -> x4, starting transfers between devices: 99 us -> 22.7 us  [shifted(): return lax.ppermute(block, axis, route)]
  transfers between devices with their start and end apart: 20 -> 4, of which waited for: 18 -> 2; matrix products, arithmetic and copies ran while one was open for 0% -> 1% of each run, Pallas kernels for 0% -> 0%
where the time goes in v2:
time: 177 us; the launch traced here: 175 us
  Pallas kernels  112 us (63%)
  matrix products  25.7 us (15%)
  starting transfers between devices  22.7 us (13%)
  other arithmetic  7.01 us (4%)
  waiting for transfers between devices  3.39 us (2%)
  local copies, waits for them, and re-layouts  3.11 us (2%)
    pallas_call x2, Pallas kernels, kernel_scan(): pl.pallas_call(functools.partial(scan_kernel, size, reverse), out_shape=j...  112 us
    ppermute x4, starting transfers between devices, shifted(): return lax.ppermute(block, axis, route)  22.7 us
    dot_general x4, matrix products, backward_block(): lax.dot_general(grad_pre, w_first, (((1,), (1,)), ((), ())), preferred_el...  16.2 us
    dot_general x3, matrix products, finish_block(): jnp.dot(hidden, w_second, preferred_element_type=jnp.float32)  6.86 us
  transfers between devices with their start and end apart: 4, of which 2 were waited for; matrix products, arithmetic and copies ran while one was open for 1% of the time, Pallas kernels for 0%

profile of v2, /device:TPU:1, one launch (start us, length us, event | category | flops | bytes accessed | tf_op | source)
XLA Modules:
  0.0 174.9 jit_solution(6295840981519396415)
XLA Ops:
  0.6 0.8 fusion.133
  1.4 0.8 fusion.134
  2.2 1.1 fusion.93
  3.2 3.2 %multiply_reduce_fusion.6 = (f32[128]{0:T(128)S(1)}, f32[128,512]{1,0:T(8,128)S(1)}) fusion(bf16[2,2048,512]{2,1,0:T(8,128)(2,1)} %param.9, bf16[2,512,2048]{2,1,0:T(8,128)(2,1)} %param.8, f32[1,128,512]{2,1,0:T(8,128)} %param.6, f32[512]{0:T(512)S(1)} %bitcast.147, f32[128]{0:T(128)S(1)} %add_rsqrt_fusion.3, f32[512]{0:T(512)S(1)} %bitcast.140), kind=kOutput, calls=%fused_computation.108 | convolution fusion | flops 538640256 | bytes 4985856 | tf_op jit(solution)/shard_map/dot_general | solution.py:128
  6.4 3.0 %fusion.64 = f32[128,512]{1,0:T(8,128)S(1)} fusion(bf16[2,2048,512]{2,1,0:T(8,128)(2,1)} %param.9, bf16[2,512,2048]{2,1,0:T(8,128)(2,1)} %param.8, f32[128,512]{1,0:T(8,128)S(1)} %get-tuple-element.17, f32[512]{0:T(512)S(1)} %bitcast.151, f32[128]{0:T(128)S(1)} %add_rsqrt_fusion.2, f32[512]{0:T(512)S(1)} %bitcast.144), kind=kOutput, calls=%fused_computation.58 | convolution fusion | flops 538509312 | bytes 4985344 | tf_op jit(solution)/shard_map/dot_general | solution.py:128
  9.5 4.5 %collective-permute-start = (f32[128,512]{1,0:T(8,128)S(1)}, f32[128,512]{1,0:T(8,128)S(1)}, u32[]{:S(2)}, u32[]{:S(2)}) collective-permute-start(f32[128,512]{1,0:T(8,128)S(1)} %fusion.64), channel_id=1, source_target_pairs={{0,1},{1,2},{2,3},{3,4},{4,5},{5,6},{6,7},{7,8},{8,9},{9,10},{10,1... | collective-permute-start | bytes 786440 | tf_op jit(solution)/shard_map/ppermute | solution.py:14
  14.0 1.9 %collective-permute-start.1 = (f32[512]{0:T(512)S(1)}, f32[512]{0:T(512)S(1)}, u32[]{:S(2)}, u32[]{:S(2)}) collective-permute-start(f32[512]{0:T(512)S(1)} %reduce_prod.9), channel_id=1, source_target_pairs={{0,1},{1,2},{2,3},{3,4},{4,5},{5,6},{6,7},{7,8},{8,9},{9,10},{10,1... | collective-permute-start | bytes 6152 | tf_op jit(solution)/shard_map/ppermute | solution.py:14
  16.0 1.3 collective-permute-done
  17.4 0.8 fusion.97
  18.2 56.2 %shard_map.77 = f32[128,512]{1,0:T(8,128)} custom-call(f32[136,256]{1,0:T(8,128)} %get-tuple-element.7.mine_ref, f32[136,256]{1,0:T(8,128)} %get-tuple-element.6.other_ref, f32[128,512]{1,0:T(8,128)} %copy-done.2, f32[8,512]{1,0:T(8,128)} %copy-done.6), custom_call_target="tpu_custom_call" | custom-call | tf_op jit(solution)/shard_map/pallas_call | solution.py:104
  74.4 1.2 multiply_reduce_fusion.5
  75.6 2.2 %fusion.30 = f32[128,2048]{1,0:T(8,128)S(1)} fusion(bf16[2,512,2048]{2,1,0:T(8,128)(2,1)} %param.8, f32[128,512]{1,0:T(8,128)S(1)} %get-tuple-element.3, f32[512]{0:T(512)S(1)} %bitcast.148, f32[128]{0:T(128)S(1)} %get-tuple-element.13), kind=kOutput, calls=%fused_computation.34 | convolution fusion | flops 268632064 | bytes 3410432 | tf_op jit(solution)/shard_map/dot_general | solution.py:122
  78.5 1.5 copy-done
  80.5 3.9 %multiply_reduce_fusion.3 = (f32[128]{0:T(128)S(1)}, f32[128,512]{1,0:T(8,128)S(1)}) fusion(f32[128,512]{1,0:T(8,128)S(1)} %get-tuple-element.19, f32[512]{0:T(512)S(1)} %bitcast.153, bf16[2,512,2048]{2,1,0:T(8,128)(2,1)} %param.8, bf16[2,2048,512]{2,1,0:T(8,128)(2,1)} %param.9, f32[128,2048]{1,0:T(8,128)S(1)} %fusion.16, f32[1,128,512]{2,1,0:T(8,128)S(1)} %copy-done.3), kind=kOutput, calls=%fused_computation.101 | convolution fusion | flops 539492224 | bytes 6031872 | tf_op jit(solution)/shard_map/dot_general | solution.py:140
  84.5 4.5 %multiply_reduce_fusion.2 = (f32[128]{0:T(128)S(1)}, f32[128,512]{1,0:T(8,128)}) fusion(f32[128,512]{1,0:T(8,128)S(1)} %get-tuple-element.3, f32[512]{0:T(512)S(1)} %bitcast.149, bf16[2,512,2048]{2,1,0:T(8,128)(2,1)} %param.8, bf16[2,2048,512]{2,1,0:T(8,128)(2,1)} %param.9, f32[128,2048]{1,0:T(8,128)S(1)} %fusion.30, f32[128,512]{1,0:T(8,128)S(1)} %fusion.91), kind=kOutput, calls=%fused_computation.100 | convolution fusion | flops 539492224 | bytes 6031872 | tf_op jit(solution)/shard_map/dot_general | solution.py:140
  89.0 1.1 multiply_subtract_fusion.1
  90.1 14.4 %collective-permute-start.2 = (f32[128,512]{1,0:T(8,128)S(1)}, f32[128,512]{1,0:T(8,128)S(1)}, u32[]{:S(2)}, u32[]{:S(2)}) collective-permute-start(f32[128,512]{1,0:T(8,128)S(1)} %multiply_subtract_fusion.1), channel_id=1, source_target_pairs={{1,0},{2,1},{3,2},{4,3},{5,4},{6,5},{7,6},{8,7},{9,8},{10,9},{11,1... | collective-permute-start | bytes 786440 | tf_op jit(solution)/shard_map/ppermute | solution.py:14
  104.5 1.9 %collective-permute-start.3 = (f32[512]{0:T(512)S(1)}, f32[512]{0:T(512)S(1)}, u32[]{:S(2)}, u32[]{:S(2)}) collective-permute-start(f32[512]{0:T(512)S(1)} %reduce_prod.9), channel_id=1, source_target_pairs={{1,0},{2,1},{3,2},{4,3},{5,4},{6,5},{7,6},{8,7},{9,8},{10,9},{11,1... | collective-permute-start | bytes 6152 | tf_op jit(solution)/shard_map/ppermute | solution.py:14
  106.4 0.8 pad_maximum_fusion
  107.3 2.1 %collective-permute-done.3 = f32[512]{0:T(512)S(1)} collective-permute-done((f32[512]{0:T(512)S(1)}, f32[512]{0:T(512)S(1)}, u32[]{:S(2)}, u32[]{:S(2)}) %collective-permute-start.3) | collective-permute-done | bytes 2080 | tf_op jit(solution)/shard_map/ppermute | solution.py:14
  110.1 55.8 %shard_map.78 = f32[128,512]{1,0:T(8,128)} custom-call(f32[136,256]{1,0:T(8,128)} %get-tuple-element.5.mine_ref, f32[136,256]{1,0:T(8,128)} %get-tuple-element.4.other_ref, f32[128,512]{1,0:T(8,128)} %copy-done.1, f32[8,512]{1,0:T(8,128)} %copy-done.7), custom_call_target="tpu_custom_call" | custom-call | tf_op jit(solution)/shard_map/pallas_call | solution.py:104
  165.9 4.0 %multiply_reduce_fusion.1 = (f32[128]{0:T(128)S(1)}, f32[128,512]{1,0:T(8,128)S(1)}) fusion(f32[128,512]{1,0:T(8,128)S(1)} %get-tuple-element.19, f32[512]{0:T(512)S(1)} %bitcast.154, bf16[2,512,2048]{2,1,0:T(8,128)(2,1)} %param.8, bf16[2,2048,512]{2,1,0:T(8,128)(2,1)} %param.9, f32[128,2048]{1,0:T(8,128)S(1)} %fusion.16, f32[128,512]{1,0:T(8,128)} %shard_map.78, ...), kind=kOutput, calls=%fused_computation.98 | convolution fusion | flops 539557760 | bytes 6294016 | tf_op jit(solution)/shard_map/dot_general | solution.py:140
  170.1 3.9 %multiply_reduce_fusion = (f32[128]{0:T(128)S(1)}, f32[128,512]{1,0:T(8,128)S(1)}) fusion(f32[128,512]{1,0:T(8,128)S(1)} %get-tuple-element.3, f32[512]{0:T(512)S(1)} %bitcast.150, bf16[2,512,2048]{2,1,0:T(8,128)(2,1)} %param.8, bf16[2,2048,512]{2,1,0:T(8,128)(2,1)} %param.9, f32[128,2048]{1,0:T(8,128)S(1)} %fusion.30, f32[128,512]{1,0:T(8,128)S(1)} %multiply_subtract_fusion), kind=kOutput, calls=%fused_computation.96 | convolution fusion | flops 539492224 | bytes 6031872 | tf_op jit(solution)/shard_map/dot_general | solution.py:140
  174.1 0.8 pad_maximum_fusion.1
  (40 shorter events, 2.4 us)
Async XLA Ops:
  6.4 7.6 %copy-start.8 = (f32[2,512]{1,0:T(2,128)S(1)}, f32[2,512]{1,0:T(2,128)}, u32[]{:S(2)}) copy-start(f32[2,512]{1,0:T(2,128)} %param.11) | copy-start | bytes 12292
  6.4 10.9 %copy-start.4 = (f32[1,128,512]{2,1,0:T(8,128)S(1)}, f32[1,128,512]{2,1,0:T(8,128)}, u32[]{:S(2)}) copy-start(f32[1,128,512]{2,1,0:T(8,128)} %param.6) | copy-start | bytes 786436
  9.5 7.8 %collective-permute-start = (f32[128,512]{1,0:T(8,128)S(1)}, f32[128,512]{1,0:T(8,128)S(1)}, u32[]{:S(2)}, u32[]{:S(2)}) collective-permute-start(f32[128,512]{1,0:T(8,128)S(1)} %fusion.64), channel_id=1, source_target_pairs={{0,1},{1,2},{2,3},{3,4},{4,5},{5,6},{6,7},{7,8},{8,9},{9,10},{10,1... | collective-permute-start | bytes 786440 | tf_op jit(solution)/shard_map/ppermute | solution.py:14
  14.0 3.3 %collective-permute-start.1 = (f32[512]{0:T(512)S(1)}, f32[512]{0:T(512)S(1)}, u32[]{:S(2)}, u32[]{:S(2)}) collective-permute-start(f32[512]{0:T(512)S(1)} %reduce_prod.9), channel_id=1, source_target_pairs={{0,1},{1,2},{2,3},{3,4},{4,5},{5,6},{6,7},{7,8},{8,9},{9,10},{10,1... | collective-permute-start | bytes 6152 | tf_op jit(solution)/shard_map/ppermute | solution.py:14
  17.4 0.8 copy-start.2
  17.4 0.8 copy-start.6
  74.4 3.4 %copy-start.9 = (bf16[2,2048,512]{2,1,0:T(8,128)(2,1)S(1)}, bf16[2,2048,512]{2,1,0:T(8,128)(2,1)}, u32[]{:S(2)}) copy-start(bf16[2,2048,512]{2,1,0:T(8,128)(2,1)} %param.9) | copy-start | bytes 12582916
  77.8 2.2 %copy-start = (bf16[2,512,2048]{2,1,0:T(8,128)(2,1)S(1)}, bf16[2,512,2048]{2,1,0:T(8,128)(2,1)}, u32[]{:S(2)}) copy-start(bf16[2,512,2048]{2,1,0:T(8,128)(2,1)} %param.8) | copy-start | bytes 12582916
  77.8 2.7 %copy-start.3 = (f32[1,128,512]{2,1,0:T(8,128)S(1)}, f32[1,128,512]{2,1,0:T(8,128)}, u32[]{:S(2)}) copy-start(f32[1,128,512]{2,1,0:T(8,128)} %param.7) | copy-start | bytes 786436
  90.1 17.2 %collective-permute-start.2 = (f32[128,512]{1,0:T(8,128)S(1)}, f32[128,512]{1,0:T(8,128)S(1)}, u32[]{:S(2)}, u32[]{:S(2)}) collective-permute-start(f32[128,512]{1,0:T(8,128)S(1)} %multiply_subtract_fusion.1), channel_id=1, source_target_pairs={{1,0},{2,1},{3,2},{4,3},{5,4},{6,5},{7,6},{8,7},{9,8},{10,9},{11,1... | collective-permute-start | bytes 786440 | tf_op jit(solution)/shard_map/ppermute | solution.py:14
  104.5 4.9 %collective-permute-start.3 = (f32[512]{0:T(512)S(1)}, f32[512]{0:T(512)S(1)}, u32[]{:S(2)}, u32[]{:S(2)}) collective-permute-start(f32[512]{0:T(512)S(1)} %reduce_prod.9), channel_id=1, source_target_pairs={{1,0},{2,1},{3,2},{4,3},{5,4},{6,5},{7,6},{8,7},{9,8},{10,9},{11,1... | collective-permute-start | bytes 6152 | tf_op jit(solution)/shard_map/ppermute | solution.py:14
  107.3 2.8 %copy-start.1 = (f32[128,512]{1,0:T(8,128)}, f32[128,512]{1,0:T(8,128)S(1)}, u32[]{:S(2)}) copy-start(f32[128,512]{1,0:T(8,128)S(1)} %fusion.92.offset_ref) | copy-start | bytes 786436
  109.4 0.7 copy-start.7
  165.9 4.0 %copy-start.5 = (f32[128,512]{1,0:T(8,128)S(1)}, f32[128,512]{1,0:T(8,128)}, u32[]{:S(2)}) copy-start(f32[128,512]{1,0:T(8,128)} %shard_map.78) | copy-start | bytes 786436

commit v3 on v2

--- a/solution.py
+++ b/solution.py
@@ -17,19 +17,15 @@
 MESH = pl.DeviceIdType.MESH
 
 
-def joined(later, earlier, rows):
-    scale = later[rows : rows + 1, :]
-    top = later[:rows, :] + scale * earlier[:rows, :]
-    return jnp.concatenate([top, later[rows:, :] * earlier[rows:, :]], axis=0)
-
-
-def scan_kernel(size, reverse, mine_ref, other_ref, offset_ref, factor_ref, out_ref, got, total, sends, recvs):
+def scan_kernel(size, reverse, pieces, mine_ref, other_ref, offset_ref, factor_ref, out_ref, got, total, sends, recvs):
     position = lax.axis_index("depth")
     order = size - 1 - position if reverse else position
     core, chip = (order % 2, order // 2)
     rows = offset_ref.shape[0]
     half = mine_ref.shape[1]
     chips = size // 2
+    step_rows = rows // pieces
+    spans = [(rows, 8)] + [(k * step_rows, step_rows) for k in range(pieces)]
     hops = []
     distance = 1
     while distance < chips:
@@ -48,46 +44,79 @@
         pl.semaphore_signal(barrier, inc=1, device_id=device(target), device_id_type=MESH)
     pl.semaphore_wait(barrier, len(targets))
 
-    def send(src, slot, target):
+    started = []
+
+    def send(src, slot, piece, target):
+        first_row, count = spans[piece]
         copy = pltpu.make_async_remote_copy(
-            src_ref=src,
-            dst_ref=got.at[slot],
-            send_sem=sends.at[slot],
-            recv_sem=recvs.at[slot],
+            src_ref=src.at[pl.ds(first_row, count), :],
+            dst_ref=got.at[slot].at[pl.ds(first_row, count), :],
+            send_sem=sends.at[slot, piece],
+            recv_sem=recvs.at[slot, piece],
             device_id=device(target),
             device_id_type=MESH,
         )
         copy.start()
+        started.append(copy)
         return copy
 
-    send(other_ref, 0, partner).wait()
     first = core == 0
-    mine = mine_ref[...]
-    came = got[0]
-    total[0] = joined(jnp.where(first, came, mine), jnp.where(first, mine, came), rows)
-    for step, hop in enumerate(hops):
-        send(total.at[step], step + 1, order + hop).wait()
-        held = total[step]
-        total[step + 1] = jnp.where(chip >= hop // 2, joined(held, got[step + 1], rows), held)
+    pending = [send(other_ref, 0, piece, partner) for piece in range(pieces + 1)]
+    factor_row = slice(rows, rows + 1)
+    for stage in range(len(hops) + 1):
+        following = []
+        for piece in range(pieces + 1):
+            first_row, count = spans[piece]
+            part = slice(first_row, first_row + count)
+            pending[piece].wait_recv()
+            came = got[stage, part, :]
+            if stage == 0:
+                mine = mine_ref[part, :]
+                later = jnp.where(first, came, mine)
+                earlier = jnp.where(first, mine, came)
+                scale = jnp.where(first, got[0, factor_row, :], mine_ref[factor_row, :])
+                if piece == 0:
+                    value = later * earlier
+                else:
+                    value = later + scale * earlier
+            else:
+                held = total[stage - 1, part, :]
+                scale = total[stage - 1, factor_row, :]
+                if piece == 0:
+                    combined = held * came
+                else:
+                    combined = held + scale * came
+                value = jnp.where(chip >= hops[stage - 1] // 2, combined, held)
+            total[stage, part, :] = value
+            if stage < len(hops):
+                following.append(send(total.at[stage], stage + 1, piece, order + hops[stage]))
+        pending = following
     last = len(hops)
-    near = send(total.at[last], last + 1, order + 1)
-    far = send(total.at[last], last + 2, order + 2)
-    near.wait()
-    far.wait()
-    close = got[last + 1, :rows, :]
-    own = total[last, :rows, :]
-    before_left = got[last + 2, :rows, :]
-    offset_left = offset_ref[:, :half]
-    offset_right = offset_ref[:, half:]
-    factor_left = factor_ref[0:1, :half]
-    factor_right = factor_ref[0:1, half:]
+    near = [None] + [send(total.at[last], last + 1, piece, order + 1) for piece in range(1, pieces + 1)]
+    far = [None] + [send(total.at[last], last + 2, piece, order + 2) for piece in range(1, pieces + 1)]
     early = chip >= 1
-    out_ref[:, :half] = jnp.where(
-        first, jnp.where(early, offset_left + factor_left * before_left, offset_left), close
-    )
-    out_ref[:, half:] = jnp.where(
-        first, jnp.where(early, offset_right + factor_right * close, offset_right), own
-    )
+    for piece in range(1, pieces + 1):
+        first_row, count = spans[piece]
+        part = slice(first_row, first_row + count)
+        near[piece].wait_recv()
+        far[piece].wait_recv()
+        close = got[last + 1, part, :]
+        own = total[last, part, :]
+        before_left = got[last + 2, part, :]
+        offset_left = offset_ref[part, :half]
+        offset_right = offset_ref[part, half:]
+        out_ref[part, :half] = jnp.where(
+            first,
+            jnp.where(early, offset_left + factor_ref[0:1, :half] * before_left, offset_left),
+            close,
+        )
+        out_ref[part, half:] = jnp.where(
+            first,
+            jnp.where(early, offset_right + factor_ref[0:1, half:] * close, offset_right),
+            own,
+        )
+    for copy in started:
+        copy.wait_send()
 
 
 def kernel_scan(factor, offset, reverse, ident):
@@ -102,15 +131,15 @@
     other = lax.dynamic_slice_in_dim(packed, (1 - core) * half, half, axis=1)
     stages = 3 + (size // 2).bit_length() - 1
     return pl.pallas_call(
-        functools.partial(scan_kernel, size, reverse),
+        functools.partial(scan_kernel, size, reverse, 4),
         out_shape=jax.ShapeDtypeStruct((rows, width), jnp.float32),
         in_specs=[pl.BlockSpec(memory_space=pltpu.VMEM)] * 4,
         out_specs=pl.BlockSpec(memory_space=pltpu.VMEM),
         scratch_shapes=[
             pltpu.VMEM((stages, rows + 8, half), jnp.float32),
             pltpu.VMEM((stages - 2, rows + 8, half), jnp.float32),
-            pltpu.SemaphoreType.DMA((stages,)),
-            pltpu.SemaphoreType.DMA((stages,)),
+            pltpu.SemaphoreType.DMA((stages, 5)),
+            pltpu.SemaphoreType.DMA((stages, 5)),
         ],
         compiler_params=pltpu.CompilerParams(collective_id=ident, has_side_effects=True),
     )(mine, other, offset, spread)

time: 177 us -> 162 us (0.915)
  the two profiles are of different devices: /device:TPU:1 before, /device:TPU:4 now
where the time goes in v3:
time: 162 us; the launch traced here: 161 us
  Pallas kernels  112 us (69%)
  matrix products  25.7 us (16%)
  starting transfers between devices  9.55 us (6%)
  other arithmetic  7.05 us (4%)
  local copies, waits for them, and re-layouts  3.12 us (2%)
  waiting for transfers between devices  3 us (2%)
    pallas_call x2, Pallas kernels, kernel_scan(): pl.pallas_call(functools.partial(scan_kernel, size, reverse, 4), out_shap...  112 us
    dot_general x4, matrix products, backward_block(): lax.dot_general(grad_pre, w_first, (((1,), (1,)), ((), ())), preferred_el...  16.2 us
    ppermute x4, starting transfers between devices, shifted(): return lax.ppermute(block, axis, route)  9.55 us
    dot_general x3, matrix products, finish_block(): jnp.dot(hidden, w_second, preferred_element_type=jnp.float32)  6.85 us
  transfers between devices with their start and end apart: 4, of which 2 were waited for; matrix products, arithmetic and copies ran while one was open for 1% of the time, Pallas kernels for 0%

profile of v3, /device:TPU:4, one launch (start us, length us, event | category | flops | bytes accessed | tf_op | source)
XLA Modules:
  0.0 161.5 jit_solution(11599004840000650381)
XLA Ops:
  0.6 0.8 fusion.133
  1.4 0.8 fusion.134
  2.2 1.1 fusion.93
  3.2 3.2 %multiply_reduce_fusion.6 = (f32[128]{0:T(128)S(1)}, f32[128,512]{1,0:T(8,128)S(1)}) fusion(bf16[2,2048,512]{2,1,0:T(8,128)(2,1)} %param.9, bf16[2,512,2048]{2,1,0:T(8,128)(2,1)} %param.8, f32[1,128,512]{2,1,0:T(8,128)} %param.6, f32[512]{0:T(512)S(1)} %bitcast.147, f32[128]{0:T(128)S(1)} %add_rsqrt_fusion.3, f32[512]{0:T(512)S(1)} %bitcast.140), kind=kOutput, calls=%fused_computation.108 | convolution fusion | flops 538640256 | bytes 4985856 | tf_op jit(solution)/shard_map/dot_general | solution.py:157
  6.4 3.0 %fusion.64 = f32[128,512]{1,0:T(8,128)S(1)} fusion(bf16[2,2048,512]{2,1,0:T(8,128)(2,1)} %param.9, bf16[2,512,2048]{2,1,0:T(8,128)(2,1)} %param.8, f32[128,512]{1,0:T(8,128)S(1)} %get-tuple-element.17, f32[512]{0:T(512)S(1)} %bitcast.151, f32[128]{0:T(128)S(1)} %add_rsqrt_fusion.2, f32[512]{0:T(512)S(1)} %bitcast.144), kind=kOutput, calls=%fused_computation.58 | convolution fusion | flops 538509312 | bytes 4985344 | tf_op jit(solution)/shard_map/dot_general | solution.py:157
  9.5 1.9 %collective-permute-start = (f32[128,512]{1,0:T(8,128)S(1)}, f32[128,512]{1,0:T(8,128)S(1)}, u32[]{:S(2)}, u32[]{:S(2)}) collective-permute-start(f32[128,512]{1,0:T(8,128)S(1)} %fusion.64), channel_id=1, source_target_pairs={{0,1},{1,2},{2,3},{3,4},{4,5},{5,6},{6,7},{7,8},{8,9},{9,10},{10,1... | collective-permute-start | bytes 786440 | tf_op jit(solution)/shard_map/ppermute | solution.py:14
  11.5 3.2 %collective-permute-start.1 = (f32[512]{0:T(512)S(1)}, f32[512]{0:T(512)S(1)}, u32[]{:S(2)}, u32[]{:S(2)}) collective-permute-start(f32[512]{0:T(512)S(1)} %reduce_prod.9), channel_id=1, source_target_pairs={{0,1},{1,2},{2,3},{3,4},{4,5},{5,6},{6,7},{7,8},{8,9},{9,10},{10,1... | collective-permute-start | bytes 6152 | tf_op jit(solution)/shard_map/ppermute | solution.py:14
  14.7 2.5 %collective-permute-done = f32[128,512]{1,0:T(8,128)S(1)} collective-permute-done((f32[128,512]{1,0:T(8,128)S(1)}, f32[128,512]{1,0:T(8,128)S(1)}, u32[]{:S(2)}, u32[]{:S(2)}) %collective-permute-start) | collective-permute-done | bytes 262176 | tf_op jit(solution)/shard_map/ppermute | solution.py:14
  17.3 0.8 fusion.97
  18.0 53.5 %shard_map.77 = f32[128,512]{1,0:T(8,128)} custom-call(f32[136,256]{1,0:T(8,128)} %get-tuple-element.7.mine_ref, f32[136,256]{1,0:T(8,128)} %get-tuple-element.6.other_ref, f32[128,512]{1,0:T(8,128)} %copy-done.2, f32[8,512]{1,0:T(8,128)} %copy-done.6), custom_call_target="tpu_custom_call" | custom-call | tf_op jit(solution)/shard_map/pallas_call | solution.py:133
  71.6 1.2 multiply_reduce_fusion.5
  72.8 2.2 %fusion.30 = f32[128,2048]{1,0:T(8,128)S(1)} fusion(bf16[2,512,2048]{2,1,0:T(8,128)(2,1)} %param.8, f32[128,512]{1,0:T(8,128)S(1)} %get-tuple-element.3, f32[512]{0:T(512)S(1)} %bitcast.148, f32[128]{0:T(128)S(1)} %get-tuple-element.13), kind=kOutput, calls=%fused_computation.34 | convolution fusion | flops 268632064 | bytes 3410432 | tf_op jit(solution)/shard_map/dot_general | solution.py:151
  75.7 1.5 copy-done
  77.7 3.9 %multiply_reduce_fusion.3 = (f32[128]{0:T(128)S(1)}, f32[128,512]{1,0:T(8,128)S(1)}) fusion(f32[128,512]{1,0:T(8,128)S(1)} %get-tuple-element.19, f32[512]{0:T(512)S(1)} %bitcast.153, bf16[2,512,2048]{2,1,0:T(8,128)(2,1)} %param.8, bf16[2,2048,512]{2,1,0:T(8,128)(2,1)} %param.9, f32[128,2048]{1,0:T(8,128)S(1)} %fusion.16, f32[1,128,512]{2,1,0:T(8,128)S(1)} %copy-done.3), kind=kOutput, calls=%fused_computation.101 | convolution fusion | flops 539492224 | bytes 6031872 | tf_op jit(solution)/shard_map/dot_general | solution.py:169
  81.7 4.5 %multiply_reduce_fusion.2 = (f32[128]{0:T(128)S(1)}, f32[128,512]{1,0:T(8,128)}) fusion(f32[128,512]{1,0:T(8,128)S(1)} %get-tuple-element.3, f32[512]{0:T(512)S(1)} %bitcast.149, bf16[2,512,2048]{2,1,0:T(8,128)(2,1)} %param.8, bf16[2,2048,512]{2,1,0:T(8,128)(2,1)} %param.9, f32[128,2048]{1,0:T(8,128)S(1)} %fusion.30, f32[128,512]{1,0:T(8,128)S(1)} %fusion.91), kind=kOutput, calls=%fused_computation.100 | convolution fusion | flops 539492224 | bytes 6031872 | tf_op jit(solution)/shard_map/dot_general | solution.py:169
  86.2 1.1 multiply_subtract_fusion.1
  87.3 1.9 %collective-permute-start.2 = (f32[128,512]{1,0:T(8,128)S(1)}, f32[128,512]{1,0:T(8,128)S(1)}, u32[]{:S(2)}, u32[]{:S(2)}) collective-permute-start(f32[128,512]{1,0:T(8,128)S(1)} %multiply_subtract_fusion.1), channel_id=1, source_target_pairs={{1,0},{2,1},{3,2},{4,3},{5,4},{6,5},{7,6},{8,7},{9,8},{10,9},{11,1... | collective-permute-start | bytes 786440 | tf_op jit(solution)/shard_map/ppermute | solution.py:14
  89.2 2.5 %collective-permute-start.3 = (f32[512]{0:T(512)S(1)}, f32[512]{0:T(512)S(1)}, u32[]{:S(2)}, u32[]{:S(2)}) collective-permute-start(f32[512]{0:T(512)S(1)} %reduce_prod.9), channel_id=1, source_target_pairs={{1,0},{2,1},{3,2},{4,3},{5,4},{6,5},{7,6},{8,7},{9,8},{10,9},{11,1... | collective-permute-start | bytes 6152 | tf_op jit(solution)/shard_map/ppermute | solution.py:14
  91.8 0.8 pad_maximum_fusion
  93.2 0.8 fusion.95
  93.9 58.5 %shard_map.78 = f32[128,512]{1,0:T(8,128)} custom-call(f32[136,256]{1,0:T(8,128)} %get-tuple-element.5.mine_ref, f32[136,256]{1,0:T(8,128)} %get-tuple-element.4.other_ref, f32[128,512]{1,0:T(8,128)} %copy-done.1, f32[8,512]{1,0:T(8,128)} %copy-done.7), custom_call_target="tpu_custom_call" | custom-call | tf_op jit(solution)/shard_map/pallas_call | solution.py:133
  152.5 4.0 %multiply_reduce_fusion.1 = (f32[128]{0:T(128)S(1)}, f32[128,512]{1,0:T(8,128)S(1)}) fusion(f32[128,512]{1,0:T(8,128)S(1)} %get-tuple-element.19, f32[512]{0:T(512)S(1)} %bitcast.154, bf16[2,512,2048]{2,1,0:T(8,128)(2,1)} %param.8, bf16[2,2048,512]{2,1,0:T(8,128)(2,1)} %param.9, f32[128,2048]{1,0:T(8,128)S(1)} %fusion.16, f32[128,512]{1,0:T(8,128)} %shard_map.78, ...), kind=kOutput, calls=%fused_computation.98 | convolution fusion | flops 539557760 | bytes 6294016 | tf_op jit(solution)/shard_map/dot_general | solution.py:169
  156.6 3.9 %multiply_reduce_fusion = (f32[128]{0:T(128)S(1)}, f32[128,512]{1,0:T(8,128)S(1)}) fusion(f32[128,512]{1,0:T(8,128)S(1)} %get-tuple-element.3, f32[512]{0:T(512)S(1)} %bitcast.150, bf16[2,512,2048]{2,1,0:T(8,128)(2,1)} %param.8, bf16[2,2048,512]{2,1,0:T(8,128)(2,1)} %param.9, f32[128,2048]{1,0:T(8,128)S(1)} %fusion.30, f32[128,512]{1,0:T(8,128)S(1)} %multiply_subtract_fusion), kind=kOutput, calls=%fused_computation.96 | convolution fusion | flops 539492224 | bytes 6031872 | tf_op jit(solution)/shard_map/dot_general | solution.py:169
  160.6 0.8 pad_maximum_fusion.1
  (40 shorter events, 2.2 us)
Async XLA Ops:
  6.4 5.0 %copy-start.8 = (f32[2,512]{1,0:T(2,128)S(1)}, f32[2,512]{1,0:T(2,128)}, u32[]{:S(2)}) copy-start(f32[2,512]{1,0:T(2,128)} %param.11) | copy-start | bytes 12292
  6.4 10.8 %copy-start.4 = (f32[1,128,512]{2,1,0:T(8,128)S(1)}, f32[1,128,512]{2,1,0:T(8,128)}, u32[]{:S(2)}) copy-start(f32[1,128,512]{2,1,0:T(8,128)} %param.6) | copy-start | bytes 786436
  9.5 7.7 %collective-permute-start = (f32[128,512]{1,0:T(8,128)S(1)}, f32[128,512]{1,0:T(8,128)S(1)}, u32[]{:S(2)}, u32[]{:S(2)}) collective-permute-start(f32[128,512]{1,0:T(8,128)S(1)} %fusion.64), channel_id=1, source_target_pairs={{0,1},{1,2},{2,3},{3,4},{4,5},{5,6},{6,7},{7,8},{8,9},{9,10},{10,1... | collective-permute-start | bytes 786440 | tf_op jit(solution)/shard_map/ppermute | solution.py:14
  11.5 5.8 %collective-permute-start.1 = (f32[512]{0:T(512)S(1)}, f32[512]{0:T(512)S(1)}, u32[]{:S(2)}, u32[]{:S(2)}) collective-permute-start(f32[512]{0:T(512)S(1)} %reduce_prod.9), channel_id=1, source_target_pairs={{0,1},{1,2},{2,3},{3,4},{4,5},{5,6},{6,7},{7,8},{8,9},{9,10},{10,1... | collective-permute-start | bytes 6152 | tf_op jit(solution)/shard_map/ppermute | solution.py:14
  17.2 0.8 copy-start.2
  17.3 0.8 copy-start.6
  71.6 3.4 %copy-start.9 = (bf16[2,2048,512]{2,1,0:T(8,128)(2,1)S(1)}, bf16[2,2048,512]{2,1,0:T(8,128)(2,1)}, u32[]{:S(2)}) copy-start(bf16[2,2048,512]{2,1,0:T(8,128)(2,1)} %param.9) | copy-start | bytes 12582916
  75.0 2.2 %copy-start = (bf16[2,512,2048]{2,1,0:T(8,128)(2,1)S(1)}, bf16[2,512,2048]{2,1,0:T(8,128)(2,1)}, u32[]{:S(2)}) copy-start(bf16[2,512,2048]{2,1,0:T(8,128)(2,1)} %param.8) | copy-start | bytes 12582916
  75.0 2.7 %copy-start.3 = (f32[1,128,512]{2,1,0:T(8,128)S(1)}, f32[1,128,512]{2,1,0:T(8,128)}, u32[]{:S(2)}) copy-start(f32[1,128,512]{2,1,0:T(8,128)} %param.7) | copy-start | bytes 786436
  87.3 5.8 %collective-permute-start.2 = (f32[128,512]{1,0:T(8,128)S(1)}, f32[128,512]{1,0:T(8,128)S(1)}, u32[]{:S(2)}, u32[]{:S(2)}) collective-permute-start(f32[128,512]{1,0:T(8,128)S(1)} %multiply_subtract_fusion.1), channel_id=1, source_target_pairs={{1,0},{2,1},{3,2},{4,3},{5,4},{6,5},{7,6},{8,7},{9,8},{10,9},{11,1... | collective-permute-start | bytes 786440 | tf_op jit(solution)/shard_map/ppermute | solution.py:14
  89.2 3.9 %collective-permute-start.3 = (f32[512]{0:T(512)S(1)}, f32[512]{0:T(512)S(1)}, u32[]{:S(2)}, u32[]{:S(2)}) collective-permute-start(f32[512]{0:T(512)S(1)} %reduce_prod.9), channel_id=1, source_target_pairs={{1,0},{2,1},{3,2},{4,3},{5,4},{6,5},{7,6},{8,7},{9,8},{10,9},{11,1... | collective-permute-start | bytes 6152 | tf_op jit(solution)/shard_map/ppermute | solution.py:14
  93.1 0.8 copy-start.1
  93.2 0.8 copy-start.7
  152.5 4.0 %copy-start.5 = (f32[128,512]{1,0:T(8,128)S(1)}, f32[128,512]{1,0:T(8,128)}, u32[]{:S(2)}) copy-start(f32[128,512]{1,0:T(8,128)} %shard_map.78) | copy-start | bytes 786436

commit v4 on v3

--- a/solution.py
+++ b/solution.py
@@ -131,15 +131,15 @@
     other = lax.dynamic_slice_in_dim(packed, (1 - core) * half, half, axis=1)
     stages = 3 + (size // 2).bit_length() - 1
     return pl.pallas_call(
-        functools.partial(scan_kernel, size, reverse, 4),
+        functools.partial(scan_kernel, size, reverse, 8),
         out_shape=jax.ShapeDtypeStruct((rows, width), jnp.float32),
         in_specs=[pl.BlockSpec(memory_space=pltpu.VMEM)] * 4,
         out_specs=pl.BlockSpec(memory_space=pltpu.VMEM),
         scratch_shapes=[
             pltpu.VMEM((stages, rows + 8, half), jnp.float32),
             pltpu.VMEM((stages - 2, rows + 8, half), jnp.float32),
-            pltpu.SemaphoreType.DMA((stages, 5)),
-            pltpu.SemaphoreType.DMA((stages, 5)),
+            pltpu.SemaphoreType.DMA((stages, 9)),
+            pltpu.SemaphoreType.DMA((stages, 9)),
         ],
         compiler_params=pltpu.CompilerParams(collective_id=ident, has_side_effects=True),
     )(mine, other, offset, spread)

time: 162 us -> 162 us (level)
  no operation moved by 1% of the time
where the time goes in v4:
time: 162 us
  Pallas kernels  112 us (69%)
  matrix products  25.7 us (16%)
  starting transfers between devices  9.58 us (6%)
  other arithmetic  7.05 us (4%)
  local copies, waits for them, and re-layouts  3.11 us (2%)
  waiting for transfers between devices  2.97 us (2%)
    pallas_call x2, Pallas kernels, kernel_scan(): pl.pallas_call(functools.partial(scan_kernel, size, reverse, 8), out_shap...  112 us
    dot_general x4, matrix products, backward_block(): lax.dot_general(grad_pre, w_first, (((1,), (1,)), ((), ())), preferred_el...  16.2 us
    ppermute x4, starting transfers between devices, shifted(): return lax.ppermute(block, axis, route)  9.58 us
    dot_general x3, matrix products, finish_block(): jnp.dot(hidden, w_second, preferred_element_type=jnp.float32)  6.85 us
  transfers between devices with their start and end apart: 4, of which 2 were waited for; matrix products, arithmetic and copies ran while one was open for 1% of the time, Pallas kernels for 0%

profile of v4, /device:TPU:4, one launch (start us, length us, event | category | flops | bytes accessed | tf_op | source)
XLA Modules:
  0.0 161.6 jit_solution(4621495766546246653)
XLA Ops:
  0.6 0.8 fusion.133
  1.4 0.8 fusion.134
  2.2 1.1 fusion.93
  3.2 3.2 %multiply_reduce_fusion.6 = (f32[128]{0:T(128)S(1)}, f32[128,512]{1,0:T(8,128)S(1)}) fusion(bf16[2,2048,512]{2,1,0:T(8,128)(2,1)} %param.9, bf16[2,512,2048]{2,1,0:T(8,128)(2,1)} %param.8, f32[1,128,512]{2,1,0:T(8,128)} %param.6, f32[512]{0:T(512)S(1)} %bitcast.147, f32[128]{0:T(128)S(1)} %add_rsqrt_fusion.3, f32[512]{0:T(512)S(1)} %bitcast.140), kind=kOutput, calls=%fused_computation.108 | convolution fusion | flops 538640256 | bytes 4985856 | tf_op jit(solution)/shard_map/dot_general | solution.py:157
  6.4 3.0 %fusion.64 = f32[128,512]{1,0:T(8,128)S(1)} fusion(bf16[2,2048,512]{2,1,0:T(8,128)(2,1)} %param.9, bf16[2,512,2048]{2,1,0:T(8,128)(2,1)} %param.8, f32[128,512]{1,0:T(8,128)S(1)} %get-tuple-element.17, f32[512]{0:T(512)S(1)} %bitcast.151, f32[128]{0:T(128)S(1)} %add_rsqrt_fusion.2, f32[512]{0:T(512)S(1)} %bitcast.144), kind=kOutput, calls=%fused_computation.58 | convolution fusion | flops 538509312 | bytes 4985344 | tf_op jit(solution)/shard_map/dot_general | solution.py:157
  9.5 1.9 %collective-permute-start = (f32[128,512]{1,0:T(8,128)S(1)}, f32[128,512]{1,0:T(8,128)S(1)}, u32[]{:S(2)}, u32[]{:S(2)}) collective-permute-start(f32[128,512]{1,0:T(8,128)S(1)} %fusion.64), channel_id=1, source_target_pairs={{0,1},{1,2},{2,3},{3,4},{4,5},{5,6},{6,7},{7,8},{8,9},{9,10},{10,1... | collective-permute-start | bytes 786440 | tf_op jit(solution)/shard_map/ppermute | solution.py:14
  11.5 3.2 %collective-permute-start.1 = (f32[512]{0:T(512)S(1)}, f32[512]{0:T(512)S(1)}, u32[]{:S(2)}, u32[]{:S(2)}) collective-permute-start(f32[512]{0:T(512)S(1)} %reduce_prod.9), channel_id=1, source_target_pairs={{0,1},{1,2},{2,3},{3,4},{4,5},{5,6},{6,7},{7,8},{8,9},{9,10},{10,1... | collective-permute-start | bytes 6152 | tf_op jit(solution)/shard_map/ppermute | solution.py:14
  14.7 2.5 %collective-permute-done = f32[128,512]{1,0:T(8,128)S(1)} collective-permute-done((f32[128,512]{1,0:T(8,128)S(1)}, f32[128,512]{1,0:T(8,128)S(1)}, u32[]{:S(2)}, u32[]{:S(2)}) %collective-permute-start) | collective-permute-done | bytes 262176 | tf_op jit(solution)/shard_map/ppermute | solution.py:14
  17.3 0.8 fusion.97
  18.0 53.8 %shard_map.77 = f32[128,512]{1,0:T(8,128)} custom-call(f32[136,256]{1,0:T(8,128)} %get-tuple-element.7.mine_ref, f32[136,256]{1,0:T(8,128)} %get-tuple-element.6.other_ref, f32[128,512]{1,0:T(8,128)} %copy-done.2, f32[8,512]{1,0:T(8,128)} %copy-done.6), custom_call_target="tpu_custom_call" | custom-call | tf_op jit(solution)/shard_map/pallas_call | solution.py:133
  71.8 1.2 multiply_reduce_fusion.5
  73.1 2.2 %fusion.30 = f32[128,2048]{1,0:T(8,128)S(1)} fusion(bf16[2,512,2048]{2,1,0:T(8,128)(2,1)} %param.8, f32[128,512]{1,0:T(8,128)S(1)} %get-tuple-element.3, f32[512]{0:T(512)S(1)} %bitcast.148, f32[128]{0:T(128)S(1)} %get-tuple-element.13), kind=kOutput, calls=%fused_computation.34 | convolution fusion | flops 268632064 | bytes 3410432 | tf_op jit(solution)/shard_map/dot_general | solution.py:151
  75.9 1.5 copy-done
  78.0 3.9 %multiply_reduce_fusion.3 = (f32[128]{0:T(128)S(1)}, f32[128,512]{1,0:T(8,128)S(1)}) fusion(f32[128,512]{1,0:T(8,128)S(1)} %get-tuple-element.19, f32[512]{0:T(512)S(1)} %bitcast.153, bf16[2,512,2048]{2,1,0:T(8,128)(2,1)} %param.8, bf16[2,2048,512]{2,1,0:T(8,128)(2,1)} %param.9, f32[128,2048]{1,0:T(8,128)S(1)} %fusion.16, f32[1,128,512]{2,1,0:T(8,128)S(1)} %copy-done.3), kind=kOutput, calls=%fused_computation.101 | convolution fusion | flops 539492224 | bytes 6031872 | tf_op jit(solution)/shard_map/dot_general | solution.py:169
  82.0 4.5 %multiply_reduce_fusion.2 = (f32[128]{0:T(128)S(1)}, f32[128,512]{1,0:T(8,128)}) fusion(f32[128,512]{1,0:T(8,128)S(1)} %get-tuple-element.3, f32[512]{0:T(512)S(1)} %bitcast.149, bf16[2,512,2048]{2,1,0:T(8,128)(2,1)} %param.8, bf16[2,2048,512]{2,1,0:T(8,128)(2,1)} %param.9, f32[128,2048]{1,0:T(8,128)S(1)} %fusion.30, f32[128,512]{1,0:T(8,128)S(1)} %fusion.91), kind=kOutput, calls=%fused_computation.100 | convolution fusion | flops 539492224 | bytes 6031872 | tf_op jit(solution)/shard_map/dot_general | solution.py:169
  86.5 1.1 multiply_subtract_fusion.1
  87.5 1.9 %collective-permute-start.2 = (f32[128,512]{1,0:T(8,128)S(1)}, f32[128,512]{1,0:T(8,128)S(1)}, u32[]{:S(2)}, u32[]{:S(2)}) collective-permute-start(f32[128,512]{1,0:T(8,128)S(1)} %multiply_subtract_fusion.1), channel_id=1, source_target_pairs={{1,0},{2,1},{3,2},{4,3},{5,4},{6,5},{7,6},{8,7},{9,8},{10,9},{11,1... | collective-permute-start | bytes 786440 | tf_op jit(solution)/shard_map/ppermute | solution.py:14
  89.5 2.5 %collective-permute-start.3 = (f32[512]{0:T(512)S(1)}, f32[512]{0:T(512)S(1)}, u32[]{:S(2)}, u32[]{:S(2)}) collective-permute-start(f32[512]{0:T(512)S(1)} %reduce_prod.9), channel_id=1, source_target_pairs={{1,0},{2,1},{3,2},{4,3},{5,4},{6,5},{7,6},{8,7},{9,8},{10,9},{11,1... | collective-permute-start | bytes 6152 | tf_op jit(solution)/shard_map/ppermute | solution.py:14
  92.0 0.8 pad_maximum_fusion
  93.4 0.8 fusion.95
  94.2 58.4 %shard_map.78 = f32[128,512]{1,0:T(8,128)} custom-call(f32[136,256]{1,0:T(8,128)} %get-tuple-element.5.mine_ref, f32[136,256]{1,0:T(8,128)} %get-tuple-element.4.other_ref, f32[128,512]{1,0:T(8,128)} %copy-done.1, f32[8,512]{1,0:T(8,128)} %copy-done.7), custom_call_target="tpu_custom_call" | custom-call | tf_op jit(solution)/shard_map/pallas_call | solution.py:133
  152.6 4.0 %multiply_reduce_fusion.1 = (f32[128]{0:T(128)S(1)}, f32[128,512]{1,0:T(8,128)S(1)}) fusion(f32[128,512]{1,0:T(8,128)S(1)} %get-tuple-element.19, f32[512]{0:T(512)S(1)} %bitcast.154, bf16[2,512,2048]{2,1,0:T(8,128)(2,1)} %param.8, bf16[2,2048,512]{2,1,0:T(8,128)(2,1)} %param.9, f32[128,2048]{1,0:T(8,128)S(1)} %fusion.16, f32[128,512]{1,0:T(8,128)} %shard_map.78, ...), kind=kOutput, calls=%fused_computation.98 | convolution fusion | flops 539557760 | bytes 6294016 | tf_op jit(solution)/shard_map/dot_general | solution.py:169
  156.8 3.9 %multiply_reduce_fusion = (f32[128]{0:T(128)S(1)}, f32[128,512]{1,0:T(8,128)S(1)}) fusion(f32[128,512]{1,0:T(8,128)S(1)} %get-tuple-element.3, f32[512]{0:T(512)S(1)} %bitcast.150, bf16[2,512,2048]{2,1,0:T(8,128)(2,1)} %param.8, bf16[2,2048,512]{2,1,0:T(8,128)(2,1)} %param.9, f32[128,2048]{1,0:T(8,128)S(1)} %fusion.30, f32[128,512]{1,0:T(8,128)S(1)} %multiply_subtract_fusion), kind=kOutput, calls=%fused_computation.96 | convolution fusion | flops 539492224 | bytes 6031872 | tf_op jit(solution)/shard_map/dot_general | solution.py:169
  160.8 0.8 pad_maximum_fusion.1
  (40 shorter events, 2.2 us)
Async XLA Ops:
  6.4 5.0 %copy-start.8 = (f32[2,512]{1,0:T(2,128)S(1)}, f32[2,512]{1,0:T(2,128)}, u32[]{:S(2)}) copy-start(f32[2,512]{1,0:T(2,128)} %param.11) | copy-start | bytes 12292
  6.4 10.8 %copy-start.4 = (f32[1,128,512]{2,1,0:T(8,128)S(1)}, f32[1,128,512]{2,1,0:T(8,128)}, u32[]{:S(2)}) copy-start(f32[1,128,512]{2,1,0:T(8,128)} %param.6) | copy-start | bytes 786436
  9.5 7.7 %collective-permute-start = (f32[128,512]{1,0:T(8,128)S(1)}, f32[128,512]{1,0:T(8,128)S(1)}, u32[]{:S(2)}, u32[]{:S(2)}) collective-permute-start(f32[128,512]{1,0:T(8,128)S(1)} %fusion.64), channel_id=1, source_target_pairs={{0,1},{1,2},{2,3},{3,4},{4,5},{5,6},{6,7},{7,8},{8,9},{9,10},{10,1... | collective-permute-start | bytes 786440 | tf_op jit(solution)/shard_map/ppermute | solution.py:14
  11.5 5.8 %collective-permute-start.1 = (f32[512]{0:T(512)S(1)}, f32[512]{0:T(512)S(1)}, u32[]{:S(2)}, u32[]{:S(2)}) collective-permute-start(f32[512]{0:T(512)S(1)} %reduce_prod.9), channel_id=1, source_target_pairs={{0,1},{1,2},{2,3},{3,4},{4,5},{5,6},{6,7},{7,8},{8,9},{9,10},{10,1... | collective-permute-start | bytes 6152 | tf_op jit(solution)/shard_map/ppermute | solution.py:14
  17.2 0.8 copy-start.2
  17.3 0.8 copy-start.6
  71.8 3.4 %copy-start.9 = (bf16[2,2048,512]{2,1,0:T(8,128)(2,1)S(1)}, bf16[2,2048,512]{2,1,0:T(8,128)(2,1)}, u32[]{:S(2)}) copy-start(bf16[2,2048,512]{2,1,0:T(8,128)(2,1)} %param.9) | copy-start | bytes 12582916
  75.3 2.2 %copy-start = (bf16[2,512,2048]{2,1,0:T(8,128)(2,1)S(1)}, bf16[2,512,2048]{2,1,0:T(8,128)(2,1)}, u32[]{:S(2)}) copy-start(bf16[2,512,2048]{2,1,0:T(8,128)(2,1)} %param.8) | copy-start | bytes 12582916
  75.3 2.7 %copy-start.3 = (f32[1,128,512]{2,1,0:T(8,128)S(1)}, f32[1,128,512]{2,1,0:T(8,128)}, u32[]{:S(2)}) copy-start(f32[1,128,512]{2,1,0:T(8,128)} %param.7) | copy-start | bytes 786436
  87.5 5.8 %collective-permute-start.2 = (f32[128,512]{1,0:T(8,128)S(1)}, f32[128,512]{1,0:T(8,128)S(1)}, u32[]{:S(2)}, u32[]{:S(2)}) collective-permute-start(f32[128,512]{1,0:T(8,128)S(1)} %multiply_subtract_fusion.1), channel_id=1, source_target_pairs={{1,0},{2,1},{3,2},{4,3},{5,4},{6,5},{7,6},{8,7},{9,8},{10,9},{11,1... | collective-permute-start | bytes 786440 | tf_op jit(solution)/shard_map/ppermute | solution.py:14
  89.5 3.9 %collective-permute-start.3 = (f32[512]{0:T(512)S(1)}, f32[512]{0:T(512)S(1)}, u32[]{:S(2)}, u32[]{:S(2)}) collective-permute-start(f32[512]{0:T(512)S(1)} %reduce_prod.9), channel_id=1, source_target_pairs={{1,0},{2,1},{3,2},{4,3},{5,4},{6,5},{7,6},{8,7},{9,8},{10,9},{11,1... | collective-permute-start | bytes 6152 | tf_op jit(solution)/shard_map/ppermute | solution.py:14
  93.4 0.8 copy-start.1
  93.4 0.8 copy-start.7
  152.6 4.0 %copy-start.5 = (f32[128,512]{1,0:T(8,128)S(1)}, f32[128,512]{1,0:T(8,128)}, u32[]{:S(2)}) copy-start(f32[128,512]{1,0:T(8,128)} %shard_map.78) | copy-start | bytes 786436

commit v5 on v2

--- a/solution.py
+++ b/solution.py
@@ -17,77 +17,175 @@
 MESH = pl.DeviceIdType.MESH
 
 
-def joined(later, earlier, rows):
-    scale = later[rows : rows + 1, :]
-    top = later[:rows, :] + scale * earlier[:rows, :]
-    return jnp.concatenate([top, later[rows:, :] * earlier[rows:, :]], axis=0)
-
-
-def scan_kernel(size, reverse, mine_ref, other_ref, offset_ref, factor_ref, out_ref, got, total, sends, recvs):
+def group_kernel(size, reverse, pieces, mine_ref, other_ref, offset_ref, factor_ref, out_ref, got, state, q_got, q_state, gathered, full, final, sends, recvs):
     position = lax.axis_index("depth")
     order = size - 1 - position if reverse else position
     core, chip = (order % 2, order // 2)
+    ring, group = (chip % 4, chip // 4)
     rows = offset_ref.shape[0]
     half = mine_ref.shape[1]
-    chips = size // 2
-    hops = []
+    groups = size // 8
+    quarter = rows // 4
+    step_rows = rows // pieces
+    spans = [(rows, 8)] + [(k * step_rows, step_rows) for k in range(pieces)]
+    spreads = []
     distance = 1
-    while distance < chips:
-        hops.append(2 * distance)
+    while distance < groups:
+        spreads.append(distance)
         distance *= 2
+    depth = len(spreads)
+    slot_c, slot_e, slot_f = (3, 4 + depth, 5 + depth)
 
     def device(q):
         q = lax.rem(q + 2 * size, size)
         return (size - 1 - q if reverse else q,)
 
+    def in_ring(step):
+        return order + 2 * ((ring + step + 4) % 4 - ring)
+
     partner = order + 1 - 2 * core
+    source = order - 8 + 2 * (3 - ring)
+    sinks = [order + 8 + 2 * (k - 3) for k in range(4)]
+    targets = [partner, in_ring(1), in_ring(-1), in_ring(2), in_ring(-2)]
+    targets += [order + 8 + 2 * (k - ring) for k in range(4)]
+    targets += [order - 8 + 2 * (k - ring) for k in range(4)]
+    targets += [order + 8 * s for s in spreads] + [order - 8 * s for s in spreads]
+    targets += [in_ring(t) for t in (1, 2, 3)] + [in_ring(-t) for t in (1, 2, 3)]
+    targets += [order + 1, order - 1, order + 2, order - 2]
     barrier = pltpu.get_barrier_semaphore()
-    targets = [partner] + [order + h for h in hops] + [order - h for h in hops]
-    targets += [order + 1, order - 1, order + 2, order - 2]
     for target in targets:
         pl.semaphore_signal(barrier, inc=1, device_id=device(target), device_id_type=MESH)
+    last_of_ring = ring == 3
     pl.semaphore_wait(barrier, len(targets))
 
-    def send(src, slot, target):
-        copy = pltpu.make_async_remote_copy(
+    started = []
+
+    def copy(src, dst, slot, piece, target, start=True, keep=True, landing=None):
+        handle = pltpu.make_async_remote_copy(
             src_ref=src,
-            dst_ref=got.at[slot],
-            send_sem=sends.at[slot],
-            recv_sem=recvs.at[slot],
+            dst_ref=dst,
+            send_sem=sends.at[slot, piece],
+            recv_sem=recvs.at[slot, piece if landing is None else landing],
             device_id=device(target),
             device_id_type=MESH,
         )
-        copy.start()
-        return copy
-
-    send(other_ref, 0, partner).wait()
+        if start:
+            handle.start()
+        if start and keep:
+            started.append(handle)
+        return handle
+
+    def block(ref, piece):
+        first_row, count = spans[piece]
+        return ref.at[pl.ds(first_row, count), :]
+
     first = core == 0
-    mine = mine_ref[...]
-    came = got[0]
-    total[0] = joined(jnp.where(first, came, mine), jnp.where(first, mine, came), rows)
-    for step, hop in enumerate(hops):
-        send(total.at[step], step + 1, order + hop).wait()
-        held = total[step]
-        total[step + 1] = jnp.where(chip >= hop // 2, joined(held, got[step + 1], rows), held)
-    last = len(hops)
-    near = send(total.at[last], last + 1, order + 1)
-    far = send(total.at[last], last + 2, order + 2)
-    near.wait()
-    far.wait()
-    close = got[last + 1, :rows, :]
-    own = total[last, :rows, :]
-    before_left = got[last + 2, :rows, :]
+    factor_row = slice(rows, rows + 1)
+    pending = [copy(block(other_ref, k), block(got.at[0], k), 0, k, partner) for k in range(pieces + 1)]
+    for stage in range(3):
+        following = []
+        for piece in range(pieces + 1):
+            first_row, count = spans[piece]
+            part = slice(first_row, first_row + count)
+            pending[piece].wait_recv()
+            came = got[stage, part, :]
+            if stage == 0:
+                mine = mine_ref[part, :]
+                later = jnp.where(first, came, mine)
+                earlier = jnp.where(first, mine, came)
+                scale = jnp.where(first, got[0, factor_row, :], mine_ref[factor_row, :])
+                value = later * earlier if piece == 0 else later + scale * earlier
+            else:
+                held = state[stage - 1, part, :]
+                scale = state[stage - 1, factor_row, :]
+                combined = held * came if piece == 0 else held + scale * came
+                value = jnp.where(ring >= stage, combined, held)
+            state[stage, part, :] = value
+            if stage < 2:
+                step = 1 if stage == 0 else 2
+                following.append(
+                    copy(block(state.at[stage], piece), block(got.at[stage + 1], piece), stage + 1, piece, in_ring(step))
+                )
+        pending = following
+
+    def scatter(start):
+        for k in range(4):
+            for piece, (first_row, count, landing) in enumerate(((k * quarter, quarter, 0), (rows, 8, quarter))):
+                handle = copy(
+                    state.at[2].at[pl.ds(first_row, count), :],
+                    q_got.at[0].at[pl.ds(landing, count), :],
+                    slot_c,
+                    2 * k + piece,
+                    sinks[k],
+                    start=start,
+                    keep=False,
+                    landing=piece,
+                )
+                if not start:
+                    handle.wait_send()
+
+    @pl.when(last_of_ring)
+    def _():
+        scatter(True)
+
+    for k, piece_rows in ((0, (0, quarter)), (1, (quarter, 8))):
+        copy(
+            state.at[2].at[pl.ds(piece_rows[0], piece_rows[1]), :],
+            q_got.at[0].at[pl.ds(piece_rows[0], piece_rows[1]), :],
+            slot_c,
+            k,
+            source,
+            start=False,
+        ).wait_recv()
+    incoming = q_got[0]
+    is_head = group == 0
+    identity = jnp.concatenate(
+        [jnp.zeros((quarter, half), jnp.float32), jnp.ones((8, half), jnp.float32)], axis=0
+    )
+    q_state[0] = jnp.where(is_head, identity, incoming)
+    for level, spread in enumerate(spreads):
+        copy(q_state.at[level], q_got.at[level + 1], 4 + level, 0, order + 8 * spread).wait_recv()
+        held = q_state[level]
+        came = q_got[level + 1]
+        scale = held[quarter : quarter + 1, :]
+        combined = jnp.concatenate([held[:quarter] + scale * came[:quarter], held[quarter:] * came[quarter:]], axis=0)
+        q_state[level + 1] = jnp.where(group >= spread, combined, held)
+    prefix = q_state.at[depth].at[pl.ds(0, quarter), :]
+    spread_copies = [copy(prefix, gathered.at[t - 1], slot_e, t - 1, in_ring(t)) for t in (1, 2, 3)]
+    for handle in spread_copies:
+        handle.wait_recv()
+    scale = state[2, factor_row, :]
+    for t in range(4):
+        owner = (ring - t + 4) % 4
+        band = pl.ds(pl.multiple_of(owner * quarter, quarter), quarter)
+        src = q_state[depth, :quarter, :] if t == 0 else gathered[t - 1]
+        full[band, :] = state[2, band, :] + scale * src
+    near = copy(full, final.at[0], slot_f, 0, order + 1)
+    far = copy(full, final.at[1], slot_f, 1, order + 2)
+    near.wait_recv()
+    far.wait_recv()
+    close = final[0]
+    own = full[...]
+    before_left = final[1]
     offset_left = offset_ref[:, :half]
     offset_right = offset_ref[:, half:]
-    factor_left = factor_ref[0:1, :half]
-    factor_right = factor_ref[0:1, half:]
     early = chip >= 1
     out_ref[:, :half] = jnp.where(
-        first, jnp.where(early, offset_left + factor_left * before_left, offset_left), close
+        first,
+        jnp.where(early, offset_left + factor_ref[0:1, :half] * before_left, offset_left),
+        close,
     )
     out_ref[:, half:] = jnp.where(
-        first, jnp.where(early, offset_right + factor_right * close, offset_right), own
-    )
+        first,
+        jnp.where(early, offset_right + factor_ref[0:1, half:] * close, offset_right),
+        own,
+    )
+    for handle in started:
+        handle.wait_send()
+
+    @pl.when(last_of_ring)
+    def _():
+        scatter(False)
 
 
 def kernel_scan(factor, offset, reverse, ident):
@@ -100,17 +198,23 @@
     packed = jnp.concatenate([offset, spread], axis=0)
     mine = lax.dynamic_slice_in_dim(packed, core * half, half, axis=1)
     other = lax.dynamic_slice_in_dim(packed, (1 - core) * half, half, axis=1)
-    stages = 3 + (size // 2).bit_length() - 1
+    depth = (size // 8).bit_length() - 1
+    quarter = rows // 4
     return pl.pallas_call(
-        functools.partial(scan_kernel, size, reverse),
+        functools.partial(group_kernel, size, reverse, 4),
         out_shape=jax.ShapeDtypeStruct((rows, width), jnp.float32),
         in_specs=[pl.BlockSpec(memory_space=pltpu.VMEM)] * 4,
         out_specs=pl.BlockSpec(memory_space=pltpu.VMEM),
         scratch_shapes=[
-            pltpu.VMEM((stages, rows + 8, half), jnp.float32),
-            pltpu.VMEM((stages - 2, rows + 8, half), jnp.float32),
-            pltpu.SemaphoreType.DMA((stages,)),
-            pltpu.SemaphoreType.DMA((stages,)),
+            pltpu.VMEM((3, rows + 8, half), jnp.float32),
+            pltpu.VMEM((3, rows + 8, half), jnp.float32),
+            pltpu.VMEM((depth + 1, quarter + 8, half), jnp.float32),
+            pltpu.VMEM((depth + 1, quarter + 8, half), jnp.float32),
+            pltpu.VMEM((3, quarter, half), jnp.float32),
+            pltpu.VMEM((rows, half), jnp.float32),
+            pltpu.VMEM((2, rows, half), jnp.float32),
+            pltpu.SemaphoreType.DMA((6 + depth, 8)),
+            pltpu.SemaphoreType.DMA((6 + depth, 8)),
         ],
         compiler_params=pltpu.CompilerParams(collective_id=ident, has_side_effects=True),
     )(mine, other, offset, spread)

time: 177 us -> 161 us (0.910)
  starting transfers between devices: 22.7 us -> 12.1 us
  Pallas kernels: 112 us -> 106 us
    ppermute x4, starting transfers between devices: 22.7 us -> 12.1 us  [shifted(): return lax.ppermute(block, axis, route)]
    pallas_call x2, Pallas kernels: 112 us -> 106 us  [kernel_scan(): pl.pallas_call(functools.partial(group_kernel, size, reverse, 4), out_sha...]
where the time goes in v5:
time: 161 us; the launch traced here: 160 us
  Pallas kernels  106 us (66%)
  matrix products  25.7 us (16%)
  starting transfers between devices  12.1 us (8%)
  other arithmetic  7.05 us (4%)
  waiting for transfers between devices  4.43 us (3%)
  local copies, waits for them, and re-layouts  3.11 us (2%)
    pallas_call x2, Pallas kernels, kernel_scan(): pl.pallas_call(functools.partial(group_kernel, size, reverse, 4), out_sha...  106 us
    dot_general x4, matrix products, backward_block(): lax.dot_general(grad_pre, w_first, (((1,), (1,)), ((), ())), preferred_el...  16.2 us
    ppermute x4, starting transfers between devices, shifted(): return lax.ppermute(block, axis, route)  12.1 us
    dot_general x3, matrix products, finish_block(): jnp.dot(hidden, w_second, preferred_element_type=jnp.float32)  6.85 us
    ppermute x4, waiting for transfers between devices, shifted(): return lax.ppermute(block, axis, route)  4.43 us
  transfers between devices with their start and end apart: 4, of which 2 were waited for; matrix products, arithmetic and copies ran while one was open for 1% of the time, Pallas kernels for 0%

profile of v5, /device:TPU:1, one launch (start us, length us, event | category | flops | bytes accessed | tf_op | source)
XLA Modules:
  0.0 159.8 jit_solution(18253521569546047329)
XLA Ops:
  0.6 0.8 fusion.133
  1.4 0.8 fusion.134
  2.2 1.1 fusion.93
  3.2 3.2 %multiply_reduce_fusion.6 = (f32[128]{0:T(128)S(1)}, f32[128,512]{1,0:T(8,128)S(1)}) fusion(bf16[2,2048,512]{2,1,0:T(8,128)(2,1)} %param.9, bf16[2,512,2048]{2,1,0:T(8,128)(2,1)} %param.8, f32[1,128,512]{2,1,0:T(8,128)} %param.6, f32[512]{0:T(512)S(1)} %bitcast.147, f32[128]{0:T(128)S(1)} %add_rsqrt_fusion.3, f32[512]{0:T(512)S(1)} %bitcast.140), kind=kOutput, calls=%fused_computation.108 | convolution fusion | flops 538640256 | bytes 4985856 | tf_op jit(solution)/shard_map/dot_general | solution.py:232
  6.4 3.0 %fusion.64 = f32[128,512]{1,0:T(8,128)S(1)} fusion(bf16[2,2048,512]{2,1,0:T(8,128)(2,1)} %param.9, bf16[2,512,2048]{2,1,0:T(8,128)(2,1)} %param.8, f32[128,512]{1,0:T(8,128)S(1)} %get-tuple-element.17, f32[512]{0:T(512)S(1)} %bitcast.151, f32[128]{0:T(128)S(1)} %add_rsqrt_fusion.2, f32[512]{0:T(512)S(1)} %bitcast.144), kind=kOutput, calls=%fused_computation.58 | convolution fusion | flops 538509312 | bytes 4985344 | tf_op jit(solution)/shard_map/dot_general | solution.py:232
  9.5 4.5 %collective-permute-start = (f32[128,512]{1,0:T(8,128)S(1)}, f32[128,512]{1,0:T(8,128)S(1)}, u32[]{:S(2)}, u32[]{:S(2)}) collective-permute-start(f32[128,512]{1,0:T(8,128)S(1)} %fusion.64), channel_id=1, source_target_pairs={{0,1},{1,2},{2,3},{3,4},{4,5},{5,6},{6,7},{7,8},{8,9},{9,10},{10,1... | collective-permute-start | bytes 786440 | tf_op jit(solution)/shard_map/ppermute | solution.py:14
  14.0 1.9 %collective-permute-start.1 = (f32[512]{0:T(512)S(1)}, f32[512]{0:T(512)S(1)}, u32[]{:S(2)}, u32[]{:S(2)}) collective-permute-start(f32[512]{0:T(512)S(1)} %reduce_prod.9), channel_id=1, source_target_pairs={{0,1},{1,2},{2,3},{3,4},{4,5},{5,6},{6,7},{7,8},{8,9},{9,10},{10,1... | collective-permute-start | bytes 6152 | tf_op jit(solution)/shard_map/ppermute | solution.py:14
  16.0 1.3 collective-permute-done
  18.2 57.9 %shard_map.77 = f32[128,512]{1,0:T(8,128)} custom-call(f32[136,256]{1,0:T(8,128)} %get-tuple-element.7.mine_ref, f32[136,256]{1,0:T(8,128)} %get-tuple-element.6.other_ref, f32[128,512]{1,0:T(8,128)} %copy-done.2, f32[8,512]{1,0:T(8,128)} %copy-done.6), custom_call_target="tpu_custom_call" | custom-call | tf_op jit(solution)/shard_map/pallas_call | solution.py:203
  76.1 1.2 multiply_reduce_fusion.5
  77.3 2.2 %fusion.30 = f32[128,2048]{1,0:T(8,128)S(1)} fusion(bf16[2,512,2048]{2,1,0:T(8,128)(2,1)} %param.8, f32[128,512]{1,0:T(8,128)S(1)} %get-tuple-element.3, f32[512]{0:T(512)S(1)} %bitcast.148, f32[128]{0:T(128)S(1)} %get-tuple-element.13), kind=kOutput, calls=%fused_computation.34 | convolution fusion | flops 268632064 | bytes 3410432 | tf_op jit(solution)/shard_map/dot_general | solution.py:226
  80.2 1.5 copy-done
  82.2 3.9 %multiply_reduce_fusion.3 = (f32[128]{0:T(128)S(1)}, f32[128,512]{1,0:T(8,128)S(1)}) fusion(f32[128,512]{1,0:T(8,128)S(1)} %get-tuple-element.19, f32[512]{0:T(512)S(1)} %bitcast.153, bf16[2,512,2048]{2,1,0:T(8,128)(2,1)} %param.8, bf16[2,2048,512]{2,1,0:T(8,128)(2,1)} %param.9, f32[128,2048]{1,0:T(8,128)S(1)} %fusion.16, f32[1,128,512]{2,1,0:T(8,128)S(1)} %copy-done.3), kind=kOutput, calls=%fused_computation.101 | convolution fusion | flops 539492224 | bytes 6031872 | tf_op jit(solution)/shard_map/dot_general | solution.py:244
  86.2 4.5 %multiply_reduce_fusion.2 = (f32[128]{0:T(128)S(1)}, f32[128,512]{1,0:T(8,128)}) fusion(f32[128,512]{1,0:T(8,128)S(1)} %get-tuple-element.3, f32[512]{0:T(512)S(1)} %bitcast.149, bf16[2,512,2048]{2,1,0:T(8,128)(2,1)} %param.8, bf16[2,2048,512]{2,1,0:T(8,128)(2,1)} %param.9, f32[128,2048]{1,0:T(8,128)S(1)} %fusion.30, f32[128,512]{1,0:T(8,128)S(1)} %fusion.91), kind=kOutput, calls=%fused_computation.100 | convolution fusion | flops 539492224 | bytes 6031872 | tf_op jit(solution)/shard_map/dot_general | solution.py:244
  90.7 1.1 multiply_subtract_fusion.1
  91.8 3.8 %collective-permute-start.2 = (f32[128,512]{1,0:T(8,128)S(1)}, f32[128,512]{1,0:T(8,128)S(1)}, u32[]{:S(2)}, u32[]{:S(2)}) collective-permute-start(f32[128,512]{1,0:T(8,128)S(1)} %multiply_subtract_fusion.1), channel_id=1, source_target_pairs={{1,0},{2,1},{3,2},{4,3},{5,4},{6,5},{7,6},{8,7},{9,8},{10,9},{11,1... | collective-permute-start | bytes 786440 | tf_op jit(solution)/shard_map/ppermute | solution.py:14
  95.6 1.9 %collective-permute-start.3 = (f32[512]{0:T(512)S(1)}, f32[512]{0:T(512)S(1)}, u32[]{:S(2)}, u32[]{:S(2)}) collective-permute-start(f32[512]{0:T(512)S(1)} %reduce_prod.9), channel_id=1, source_target_pairs={{1,0},{2,1},{3,2},{4,3},{5,4},{6,5},{7,6},{8,7},{9,8},{10,9},{11,1... | collective-permute-start | bytes 6152 | tf_op jit(solution)/shard_map/ppermute | solution.py:14
  97.5 0.8 pad_maximum_fusion
  98.3 3.1 %collective-permute-done.2 = f32[128,512]{1,0:T(8,128)S(1)} collective-permute-done((f32[128,512]{1,0:T(8,128)S(1)}, f32[128,512]{1,0:T(8,128)S(1)}, u32[]{:S(2)}, u32[]{:S(2)}) %collective-permute-start.2) | collective-permute-done | bytes 262176 | tf_op jit(solution)/shard_map/ppermute | solution.py:14
  101.5 0.8 fusion.95
  102.3 48.5 %shard_map.78 = f32[128,512]{1,0:T(8,128)} custom-call(f32[136,256]{1,0:T(8,128)} %get-tuple-element.5.mine_ref, f32[136,256]{1,0:T(8,128)} %get-tuple-element.4.other_ref, f32[128,512]{1,0:T(8,128)} %copy-done.1, f32[8,512]{1,0:T(8,128)} %copy-done.7), custom_call_target="tpu_custom_call" | custom-call | tf_op jit(solution)/shard_map/pallas_call | solution.py:203
  150.8 4.0 %multiply_reduce_fusion.1 = (f32[128]{0:T(128)S(1)}, f32[128,512]{1,0:T(8,128)S(1)}) fusion(f32[128,512]{1,0:T(8,128)S(1)} %get-tuple-element.19, f32[512]{0:T(512)S(1)} %bitcast.154, bf16[2,512,2048]{2,1,0:T(8,128)(2,1)} %param.8, bf16[2,2048,512]{2,1,0:T(8,128)(2,1)} %param.9, f32[128,2048]{1,0:T(8,128)S(1)} %fusion.16, f32[128,512]{1,0:T(8,128)} %shard_map.78, ...), kind=kOutput, calls=%fused_computation.98 | convolution fusion | flops 539557760 | bytes 6294016 | tf_op jit(solution)/shard_map/dot_general | solution.py:244
  155.0 3.9 %multiply_reduce_fusion = (f32[128]{0:T(128)S(1)}, f32[128,512]{1,0:T(8,128)S(1)}) fusion(f32[128,512]{1,0:T(8,128)S(1)} %get-tuple-element.3, f32[512]{0:T(512)S(1)} %bitcast.150, bf16[2,512,2048]{2,1,0:T(8,128)(2,1)} %param.8, bf16[2,2048,512]{2,1,0:T(8,128)(2,1)} %param.9, f32[128,2048]{1,0:T(8,128)S(1)} %fusion.30, f32[128,512]{1,0:T(8,128)S(1)} %multiply_subtract_fusion), kind=kOutput, calls=%fused_computation.96 | convolution fusion | flops 539492224 | bytes 6031872 | tf_op jit(solution)/shard_map/dot_general | solution.py:244
  159.0 0.8 pad_maximum_fusion.1
  (40 shorter events, 2.5 us)
Async XLA Ops:
  6.4 7.6 %copy-start.8 = (f32[2,512]{1,0:T(2,128)S(1)}, f32[2,512]{1,0:T(2,128)}, u32[]{:S(2)}) copy-start(f32[2,512]{1,0:T(2,128)} %param.11) | copy-start | bytes 12292
  6.4 10.9 %copy-start.4 = (f32[1,128,512]{2,1,0:T(8,128)S(1)}, f32[1,128,512]{2,1,0:T(8,128)}, u32[]{:S(2)}) copy-start(f32[1,128,512]{2,1,0:T(8,128)} %param.6) | copy-start | bytes 786436
  9.5 7.8 %collective-permute-start = (f32[128,512]{1,0:T(8,128)S(1)}, f32[128,512]{1,0:T(8,128)S(1)}, u32[]{:S(2)}, u32[]{:S(2)}) collective-permute-start(f32[128,512]{1,0:T(8,128)S(1)} %fusion.64), channel_id=1, source_target_pairs={{0,1},{1,2},{2,3},{3,4},{4,5},{5,6},{6,7},{7,8},{8,9},{9,10},{10,1... | collective-permute-start | bytes 786440 | tf_op jit(solution)/shard_map/ppermute | solution.py:14
  14.0 3.3 %collective-permute-start.1 = (f32[512]{0:T(512)S(1)}, f32[512]{0:T(512)S(1)}, u32[]{:S(2)}, u32[]{:S(2)}) collective-permute-start(f32[512]{0:T(512)S(1)} %reduce_prod.9), channel_id=1, source_target_pairs={{0,1},{1,2},{2,3},{3,4},{4,5},{5,6},{6,7},{7,8},{8,9},{9,10},{10,1... | collective-permute-start | bytes 6152 | tf_op jit(solution)/shard_map/ppermute | solution.py:14
  17.4 0.8 copy-start.2
  17.4 0.8 copy-start.6
  76.0 3.4 %copy-start.9 = (bf16[2,2048,512]{2,1,0:T(8,128)(2,1)S(1)}, bf16[2,2048,512]{2,1,0:T(8,128)(2,1)}, u32[]{:S(2)}) copy-start(bf16[2,2048,512]{2,1,0:T(8,128)(2,1)} %param.9) | copy-start | bytes 12582916
  79.5 2.2 %copy-start = (bf16[2,512,2048]{2,1,0:T(8,128)(2,1)S(1)}, bf16[2,512,2048]{2,1,0:T(8,128)(2,1)}, u32[]{:S(2)}) copy-start(bf16[2,512,2048]{2,1,0:T(8,128)(2,1)} %param.8) | copy-start | bytes 12582916
  79.5 2.7 %copy-start.3 = (f32[1,128,512]{2,1,0:T(8,128)S(1)}, f32[1,128,512]{2,1,0:T(8,128)}, u32[]{:S(2)}) copy-start(f32[1,128,512]{2,1,0:T(8,128)} %param.7) | copy-start | bytes 786436
  91.8 9.7 %collective-permute-start.2 = (f32[128,512]{1,0:T(8,128)S(1)}, f32[128,512]{1,0:T(8,128)S(1)}, u32[]{:S(2)}, u32[]{:S(2)}) collective-permute-start(f32[128,512]{1,0:T(8,128)S(1)} %multiply_subtract_fusion.1), channel_id=1, source_target_pairs={{1,0},{2,1},{3,2},{4,3},{5,4},{6,5},{7,6},{8,7},{9,8},{10,9},{11,1... | collective-permute-start | bytes 786440 | tf_op jit(solution)/shard_map/ppermute | solution.py:14
  95.6 5.9 %collective-permute-start.3 = (f32[512]{0:T(512)S(1)}, f32[512]{0:T(512)S(1)}, u32[]{:S(2)}, u32[]{:S(2)}) collective-permute-start(f32[512]{0:T(512)S(1)} %reduce_prod.9), channel_id=1, source_target_pairs={{1,0},{2,1},{3,2},{4,3},{5,4},{6,5},{7,6},{8,7},{9,8},{10,9},{11,1... | collective-permute-start | bytes 6152 | tf_op jit(solution)/shard_map/ppermute | solution.py:14
  101.5 0.8 copy-start.1
  101.5 0.8 copy-start.7
  150.8 4.0 %copy-start.5 = (f32[128,512]{1,0:T(8,128)S(1)}, f32[128,512]{1,0:T(8,128)}, u32[]{:S(2)}) copy-start(f32[128,512]{1,0:T(8,128)} %shard_map.78) | copy-start | bytes 786436

commit v6 on v5

--- a/solution.py
+++ b/solution.py
@@ -17,7 +17,7 @@
 MESH = pl.DeviceIdType.MESH
 
 
-def group_kernel(size, reverse, pieces, mine_ref, other_ref, offset_ref, factor_ref, out_ref, got, state, q_got, q_state, gathered, full, final, sends, recvs):
+def group_kernel(size, reverse, pieces, mine_ref, other_ref, offset_ref, factor_ref, out_ref, got, state, q_got, q_state, gathered, final, sends, recvs):
     position = lax.axis_index("depth")
     order = size - 1 - position if reverse else position
     core, chip = (order % 2, order // 2)
@@ -28,13 +28,15 @@
     quarter = rows // 4
     step_rows = rows // pieces
     spans = [(rows, 8)] + [(k * step_rows, step_rows) for k in range(pieces)]
-    spreads = []
-    distance = 1
-    while distance < groups:
-        spreads.append(distance)
-        distance *= 2
-    depth = len(spreads)
-    slot_c, slot_e, slot_f = (3, 4 + depth, 5 + depth)
+    levels = []
+    width_now = 1
+    while width_now < groups:
+        ks = [k for k in (1, 2, 3) if k * width_now < groups]
+        levels.append((width_now, ks))
+        width_now *= len(ks) + 1
+    links = [(level, k) for level, (_, ks) in enumerate(levels) for k in ks]
+    slot_c, slot_e, slot_f = (3, 4 + len(levels), 5 + len(levels))
+    index = order % 8
 
     def device(q):
         q = lax.rem(q + 2 * size, size)
@@ -49,8 +51,10 @@
     targets = [partner, in_ring(1), in_ring(-1), in_ring(2), in_ring(-2)]
     targets += [order + 8 + 2 * (k - ring) for k in range(4)]
     targets += [order - 8 + 2 * (k - ring) for k in range(4)]
-    targets += [order + 8 * s for s in spreads] + [order - 8 * s for s in spreads]
-    targets += [in_ring(t) for t in (1, 2, 3)] + [in_ring(-t) for t in (1, 2, 3)]
+    for spread_width, ks in levels:
+        targets += [order + 8 * k * spread_width for k in ks] + [order - 8 * k * spread_width for k in ks]
+    targets += [order - index + (index + t) % 8 for t in range(1, 8)]
+    targets += [order - index + (index - t + 8) % 8 for t in range(1, 8)]
     targets += [order + 1, order - 1, order + 2, order - 2]
     barrier = pltpu.get_barrier_semaphore()
     for target in targets:
@@ -108,6 +112,9 @@
                 )
         pending = following
 
+    near = copy(state.at[2], final.at[0], slot_f, 0, order + 1)
+    far = copy(state.at[2], final.at[1], slot_f, 1, order + 2)
+
     def scatter(start):
         for k in range(4):
             for piece, (first_row, count, landing) in enumerate(((k * quarter, quarter, 0), (rows, 8, quarter))):
@@ -143,43 +150,44 @@
         [jnp.zeros((quarter, half), jnp.float32), jnp.ones((8, half), jnp.float32)], axis=0
     )
     q_state[0] = jnp.where(is_head, identity, incoming)
-    for level, spread in enumerate(spreads):
-        copy(q_state.at[level], q_got.at[level + 1], 4 + level, 0, order + 8 * spread).wait_recv()
+    landing = 1
+    for level, (spread_width, ks) in enumerate(levels):
+        arrivals = []
+        for k in ks:
+            arrivals.append((k, copy(q_state.at[level], q_got.at[landing], 4 + level, k - 1, order + 8 * k * spread_width), landing))
+            landing += 1
         held = q_state[level]
-        came = q_got[level + 1]
-        scale = held[quarter : quarter + 1, :]
-        combined = jnp.concatenate([held[:quarter] + scale * came[:quarter], held[quarter:] * came[quarter:]], axis=0)
-        q_state[level + 1] = jnp.where(group >= spread, combined, held)
+        for k, handle, spot in arrivals:
+            handle.wait_recv()
+            came = q_got[spot]
+            scale = held[quarter : quarter + 1, :]
+            combined = jnp.concatenate([held[:quarter] + scale * came[:quarter], held[quarter:] * came[quarter:]], axis=0)
+            held = jnp.where(group >= k * spread_width, combined, held)
+        q_state[level + 1] = held
+    depth = len(levels)
     prefix = q_state.at[depth].at[pl.ds(0, quarter), :]
-    spread_copies = [copy(prefix, gathered.at[t - 1], slot_e, t - 1, in_ring(t)) for t in (1, 2, 3)]
+    spread_copies = [copy(prefix, gathered.at[t - 1], slot_e, t - 1, order - index + (index + t) % 8) for t in range(1, 8)]
+    near.wait_recv()
+    far.wait_recv()
     for handle in spread_copies:
         handle.wait_recv()
-    scale = state[2, factor_row, :]
-    for t in range(4):
-        owner = (ring - t + 4) % 4
-        band = pl.ds(pl.multiple_of(owner * quarter, quarter), quarter)
-        src = q_state[depth, :quarter, :] if t == 0 else gathered[t - 1]
-        full[band, :] = state[2, band, :] + scale * src
-    near = copy(full, final.at[0], slot_f, 0, order + 1)
-    far = copy(full, final.at[1], slot_f, 1, order + 2)
-    near.wait_recv()
-    far.wait_recv()
-    close = final[0]
-    own = full[...]
-    before_left = final[1]
-    offset_left = offset_ref[:, :half]
-    offset_right = offset_ref[:, half:]
-    early = chip >= 1
-    out_ref[:, :half] = jnp.where(
-        first,
-        jnp.where(early, offset_left + factor_ref[0:1, :half] * before_left, offset_left),
-        close,
-    )
-    out_ref[:, half:] = jnp.where(
-        first,
-        jnp.where(early, offset_right + factor_ref[0:1, half:] * close, offset_right),
-        own,
-    )
+    at_start = ring == 0
+    for t in range(8):
+        owner = (index - t + 8) % 8
+        owner_ring, owner_core = (owner // 2, owner % 2)
+        band = pl.ds(pl.multiple_of(owner_ring * quarter, quarter), quarter)
+        cols = pl.ds(pl.multiple_of(owner_core * half, half), half)
+        piece = q_state[depth, :quarter, :] if t == 0 else gathered[t - 1]
+        left_side = owner_core == 0
+        close = final[0, band, :]
+        before = jnp.where(left_side, final[1, band, :], close)
+        before_scale = jnp.where(left_side, final[1, factor_row, :], final[0, factor_row, :])
+        behind = jnp.where(at_start, piece, before + before_scale * piece)
+        tail = offset_ref[band, cols] + factor_ref[0:1, cols] * behind
+        current = jnp.where(left_side, close, state[2, band, :])
+        current_scale = jnp.where(left_side, final[0, factor_row, :], state[2, factor_row, :])
+        head = current + current_scale * piece
+        out_ref[band, cols] = jnp.where(first, tail, head)
     for handle in started:
         handle.wait_send()
 
@@ -198,7 +206,15 @@
     packed = jnp.concatenate([offset, spread], axis=0)
     mine = lax.dynamic_slice_in_dim(packed, core * half, half, axis=1)
     other = lax.dynamic_slice_in_dim(packed, (1 - core) * half, half, axis=1)
-    depth = (size // 8).bit_length() - 1
+    groups = size // 8
+    links = 0
+    levels = 0
+    width_now = 1
+    while width_now < groups:
+        ks = [k for k in (1, 2, 3) if k * width_now < groups]
+        links += len(ks)
+        levels += 1
+        width_now *= len(ks) + 1
     quarter = rows // 4
     return pl.pallas_call(
         functools.partial(group_kernel, size, reverse, 4),
@@ -208,13 +224,12 @@
         scratch_shapes=[
             pltpu.VMEM((3, rows + 8, half), jnp.float32),
             pltpu.VMEM((3, rows + 8, half), jnp.float32),
-            pltpu.VMEM((depth + 1, quarter + 8, half), jnp.float32),
-            pltpu.VMEM((depth + 1, quarter + 8, half), jnp.float32),
-            pltpu.VMEM((3, quarter, half), jnp.float32),
-            pltpu.VMEM((rows, half), jnp.float32),
-            pltpu.VMEM((2, rows, half), jnp.float32),
-            pltpu.SemaphoreType.DMA((6 + depth, 8)),
-            pltpu.SemaphoreType.DMA((6 + depth, 8)),
+            pltpu.VMEM((links + 1, quarter + 8, half), jnp.float32),
+            pltpu.VMEM((levels + 1, quarter + 8, half), jnp.float32),
+            pltpu.VMEM((7, quarter, half), jnp.float32),
+            pltpu.VMEM((2, rows + 8, half), jnp.float32),
+            pltpu.SemaphoreType.DMA((6 + levels, 8)),
+            pltpu.SemaphoreType.DMA((6 + levels, 8)),
         ],
         compiler_params=pltpu.CompilerParams(collective_id=ident, has_side_effects=True),
     )(mine, other, offset, spread)

time: 161 us -> 162 us (level)
  Pallas kernels: 106 us -> 110 us
  starting transfers between devices: 12.1 us -> 10.4 us
    pallas_call x2, Pallas kernels: 106 us -> 110 us  [kernel_scan(): pl.pallas_call(functools.partial(group_kernel, size, reverse, 4), out_sha...]
    ppermute x4, starting transfers between devices: 12.1 us -> 10.4 us  [shifted(): return lax.ppermute(block, axis, route)]
where the time goes in v6:
time: 162 us; the launch traced here: 161 us
  Pallas kernels  110 us (68%)
  matrix products  25.7 us (16%)
  starting transfers between devices  10.4 us (6%)
  other arithmetic  7.05 us (4%)
  waiting for transfers between devices  4.14 us (3%)
  local copies, waits for them, and re-layouts  3.12 us (2%)
    pallas_call x2, Pallas kernels, kernel_scan(): pl.pallas_call(functools.partial(group_kernel, size, reverse, 4), out_sha...  110 us
    dot_general x4, matrix products, backward_block(): lax.dot_general(grad_pre, w_first, (((1,), (1,)), ((), ())), preferred_el...  16.2 us
    ppermute x4, starting transfers between devices, shifted(): return lax.ppermute(block, axis, route)  10.4 us
    dot_general x3, matrix products, finish_block(): jnp.dot(hidden, w_second, preferred_element_type=jnp.float32)  6.85 us
    ppermute x4, waiting for transfers between devices, shifted(): return lax.ppermute(block, axis, route)  4.14 us
  transfers between devices with their start and end apart: 4, of which 2 were waited for; matrix products, arithmetic and copies ran while one was open for 1% of the time, Pallas kernels for 0%

profile of v6, /device:TPU:1, one launch (start us, length us, event | category | flops | bytes accessed | tf_op | source)
XLA Modules:
  0.0 161.4 jit_solution(15892552007780197223)
XLA Ops:
  0.6 0.8 fusion.133
  1.4 0.8 fusion.134
  2.2 1.1 fusion.93
  3.2 3.2 %multiply_reduce_fusion.6 = (f32[128]{0:T(128)S(1)}, f32[128,512]{1,0:T(8,128)S(1)}) fusion(bf16[2,2048,512]{2,1,0:T(8,128)(2,1)} %param.9, bf16[2,512,2048]{2,1,0:T(8,128)(2,1)} %param.8, f32[1,128,512]{2,1,0:T(8,128)} %param.6, f32[512]{0:T(512)S(1)} %bitcast.147, f32[128]{0:T(128)S(1)} %add_rsqrt_fusion.3, f32[512]{0:T(512)S(1)} %bitcast.140), kind=kOutput, calls=%fused_computation.108 | convolution fusion | flops 538640256 | bytes 4985856 | tf_op jit(solution)/shard_map/dot_general | solution.py:247
  6.4 3.0 %fusion.64 = f32[128,512]{1,0:T(8,128)S(1)} fusion(bf16[2,2048,512]{2,1,0:T(8,128)(2,1)} %param.9, bf16[2,512,2048]{2,1,0:T(8,128)(2,1)} %param.8, f32[128,512]{1,0:T(8,128)S(1)} %get-tuple-element.17, f32[512]{0:T(512)S(1)} %bitcast.151, f32[128]{0:T(128)S(1)} %add_rsqrt_fusion.2, f32[512]{0:T(512)S(1)} %bitcast.144), kind=kOutput, calls=%fused_computation.58 | convolution fusion | flops 538509312 | bytes 4985344 | tf_op jit(solution)/shard_map/dot_general | solution.py:247
  9.5 4.5 %collective-permute-start = (f32[128,512]{1,0:T(8,128)S(1)}, f32[128,512]{1,0:T(8,128)S(1)}, u32[]{:S(2)}, u32[]{:S(2)}) collective-permute-start(f32[128,512]{1,0:T(8,128)S(1)} %fusion.64), channel_id=1, source_target_pairs={{0,1},{1,2},{2,3},{3,4},{4,5},{5,6},{6,7},{7,8},{8,9},{9,10},{10,1... | collective-permute-start | bytes 786440 | tf_op jit(solution)/shard_map/ppermute | solution.py:14
  14.0 1.9 %collective-permute-start.1 = (f32[512]{0:T(512)S(1)}, f32[512]{0:T(512)S(1)}, u32[]{:S(2)}, u32[]{:S(2)}) collective-permute-start(f32[512]{0:T(512)S(1)} %reduce_prod.9), channel_id=1, source_target_pairs={{0,1},{1,2},{2,3},{3,4},{4,5},{5,6},{6,7},{7,8},{8,9},{9,10},{10,1... | collective-permute-start | bytes 6152 | tf_op jit(solution)/shard_map/ppermute | solution.py:14
  16.0 1.3 collective-permute-done
  18.2 61.5 %shard_map.77 = f32[128,512]{1,0:T(8,128)} custom-call(f32[136,256]{1,0:T(8,128)} %get-tuple-element.7.mine_ref, f32[136,256]{1,0:T(8,128)} %get-tuple-element.6.other_ref, f32[128,512]{1,0:T(8,128)} %copy-done.2, f32[8,512]{1,0:T(8,128)} %copy-done.6), custom_call_target="tpu_custom_call" | custom-call | tf_op jit(solution)/shard_map/pallas_call | solution.py:219
  79.7 1.2 multiply_reduce_fusion.5
  80.9 2.2 %fusion.30 = f32[128,2048]{1,0:T(8,128)S(1)} fusion(bf16[2,512,2048]{2,1,0:T(8,128)(2,1)} %param.8, f32[128,512]{1,0:T(8,128)S(1)} %get-tuple-element.3, f32[512]{0:T(512)S(1)} %bitcast.148, f32[128]{0:T(128)S(1)} %get-tuple-element.13), kind=kOutput, calls=%fused_computation.34 | convolution fusion | flops 268632064 | bytes 3410432 | tf_op jit(solution)/shard_map/dot_general | solution.py:241
  83.8 1.5 copy-done
  85.8 3.9 %multiply_reduce_fusion.3 = (f32[128]{0:T(128)S(1)}, f32[128,512]{1,0:T(8,128)S(1)}) fusion(f32[128,512]{1,0:T(8,128)S(1)} %get-tuple-element.19, f32[512]{0:T(512)S(1)} %bitcast.153, bf16[2,512,2048]{2,1,0:T(8,128)(2,1)} %param.8, bf16[2,2048,512]{2,1,0:T(8,128)(2,1)} %param.9, f32[128,2048]{1,0:T(8,128)S(1)} %fusion.16, f32[1,128,512]{2,1,0:T(8,128)S(1)} %copy-done.3), kind=kOutput, calls=%fused_computation.101 | convolution fusion | flops 539492224 | bytes 6031872 | tf_op jit(solution)/shard_map/dot_general | solution.py:259
  89.8 4.5 %multiply_reduce_fusion.2 = (f32[128]{0:T(128)S(1)}, f32[128,512]{1,0:T(8,128)}) fusion(f32[128,512]{1,0:T(8,128)S(1)} %get-tuple-element.3, f32[512]{0:T(512)S(1)} %bitcast.149, bf16[2,512,2048]{2,1,0:T(8,128)(2,1)} %param.8, bf16[2,2048,512]{2,1,0:T(8,128)(2,1)} %param.9, f32[128,2048]{1,0:T(8,128)S(1)} %fusion.30, f32[128,512]{1,0:T(8,128)S(1)} %fusion.91), kind=kOutput, calls=%fused_computation.100 | convolution fusion | flops 539492224 | bytes 6031872 | tf_op jit(solution)/shard_map/dot_general | solution.py:259
  94.3 1.1 multiply_subtract_fusion.1
  95.4 2.1 %collective-permute-start.2 = (f32[128,512]{1,0:T(8,128)S(1)}, f32[128,512]{1,0:T(8,128)S(1)}, u32[]{:S(2)}, u32[]{:S(2)}) collective-permute-start(f32[128,512]{1,0:T(8,128)S(1)} %multiply_subtract_fusion.1), channel_id=1, source_target_pairs={{1,0},{2,1},{3,2},{4,3},{5,4},{6,5},{7,6},{8,7},{9,8},{10,9},{11,1... | collective-permute-start | bytes 786440 | tf_op jit(solution)/shard_map/ppermute | solution.py:14
  97.5 1.9 %collective-permute-start.3 = (f32[512]{0:T(512)S(1)}, f32[512]{0:T(512)S(1)}, u32[]{:S(2)}, u32[]{:S(2)}) collective-permute-start(f32[512]{0:T(512)S(1)} %reduce_prod.9), channel_id=1, source_target_pairs={{1,0},{2,1},{3,2},{4,3},{5,4},{6,5},{7,6},{8,7},{9,8},{10,9},{11,1... | collective-permute-start | bytes 6152 | tf_op jit(solution)/shard_map/ppermute | solution.py:14
  99.4 0.8 pad_maximum_fusion
  100.3 2.8 %collective-permute-done.2 = f32[128,512]{1,0:T(8,128)S(1)} collective-permute-done((f32[128,512]{1,0:T(8,128)S(1)}, f32[128,512]{1,0:T(8,128)S(1)}, u32[]{:S(2)}, u32[]{:S(2)}) %collective-permute-start.2) | collective-permute-done | bytes 262176 | tf_op jit(solution)/shard_map/ppermute | solution.py:14
  103.2 0.8 fusion.95
  103.9 48.4 %shard_map.78 = f32[128,512]{1,0:T(8,128)} custom-call(f32[136,256]{1,0:T(8,128)} %get-tuple-element.5.mine_ref, f32[136,256]{1,0:T(8,128)} %get-tuple-element.4.other_ref, f32[128,512]{1,0:T(8,128)} %copy-done.1, f32[8,512]{1,0:T(8,128)} %copy-done.7), custom_call_target="tpu_custom_call" | custom-call | tf_op jit(solution)/shard_map/pallas_call | solution.py:219
  152.4 4.0 %multiply_reduce_fusion.1 = (f32[128]{0:T(128)S(1)}, f32[128,512]{1,0:T(8,128)S(1)}) fusion(f32[128,512]{1,0:T(8,128)S(1)} %get-tuple-element.19, f32[512]{0:T(512)S(1)} %bitcast.154, bf16[2,512,2048]{2,1,0:T(8,128)(2,1)} %param.8, bf16[2,2048,512]{2,1,0:T(8,128)(2,1)} %param.9, f32[128,2048]{1,0:T(8,128)S(1)} %fusion.16, f32[128,512]{1,0:T(8,128)} %shard_map.78, ...), kind=kOutput, calls=%fused_computation.98 | convolution fusion | flops 539557760 | bytes 6294016 | tf_op jit(solution)/shard_map/dot_general | solution.py:259
  156.5 3.9 %multiply_reduce_fusion = (f32[128]{0:T(128)S(1)}, f32[128,512]{1,0:T(8,128)S(1)}) fusion(f32[128,512]{1,0:T(8,128)S(1)} %get-tuple-element.3, f32[512]{0:T(512)S(1)} %bitcast.150, bf16[2,512,2048]{2,1,0:T(8,128)(2,1)} %param.8, bf16[2,2048,512]{2,1,0:T(8,128)(2,1)} %param.9, f32[128,2048]{1,0:T(8,128)S(1)} %fusion.30, f32[128,512]{1,0:T(8,128)S(1)} %multiply_subtract_fusion), kind=kOutput, calls=%fused_computation.96 | convolution fusion | flops 539492224 | bytes 6031872 | tf_op jit(solution)/shard_map/dot_general | solution.py:259
  160.5 0.8 pad_maximum_fusion.1
  (40 shorter events, 2.5 us)
Async XLA Ops:
  6.4 7.6 %copy-start.8 = (f32[2,512]{1,0:T(2,128)S(1)}, f32[2,512]{1,0:T(2,128)}, u32[]{:S(2)}) copy-start(f32[2,512]{1,0:T(2,128)} %param.11) | copy-start | bytes 12292
  6.4 10.9 %copy-start.4 = (f32[1,128,512]{2,1,0:T(8,128)S(1)}, f32[1,128,512]{2,1,0:T(8,128)}, u32[]{:S(2)}) copy-start(f32[1,128,512]{2,1,0:T(8,128)} %param.6) | copy-start | bytes 786436
  9.5 7.8 %collective-permute-start = (f32[128,512]{1,0:T(8,128)S(1)}, f32[128,512]{1,0:T(8,128)S(1)}, u32[]{:S(2)}, u32[]{:S(2)}) collective-permute-start(f32[128,512]{1,0:T(8,128)S(1)} %fusion.64), channel_id=1, source_target_pairs={{0,1},{1,2},{2,3},{3,4},{4,5},{5,6},{6,7},{7,8},{8,9},{9,10},{10,1... | collective-permute-start | bytes 786440 | tf_op jit(solution)/shard_map/ppermute | solution.py:14
  14.0 3.3 %collective-permute-start.1 = (f32[512]{0:T(512)S(1)}, f32[512]{0:T(512)S(1)}, u32[]{:S(2)}, u32[]{:S(2)}) collective-permute-start(f32[512]{0:T(512)S(1)} %reduce_prod.9), channel_id=1, source_target_pairs={{0,1},{1,2},{2,3},{3,4},{4,5},{5,6},{6,7},{7,8},{8,9},{9,10},{10,1... | collective-permute-start | bytes 6152 | tf_op jit(solution)/shard_map/ppermute | solution.py:14
  17.4 0.8 copy-start.2
  17.4 0.8 copy-start.6
  79.7 3.4 %copy-start.9 = (bf16[2,2048,512]{2,1,0:T(8,128)(2,1)S(1)}, bf16[2,2048,512]{2,1,0:T(8,128)(2,1)}, u32[]{:S(2)}) copy-start(bf16[2,2048,512]{2,1,0:T(8,128)(2,1)} %param.9) | copy-start | bytes 12582916
  83.1 2.2 %copy-start = (bf16[2,512,2048]{2,1,0:T(8,128)(2,1)S(1)}, bf16[2,512,2048]{2,1,0:T(8,128)(2,1)}, u32[]{:S(2)}) copy-start(bf16[2,512,2048]{2,1,0:T(8,128)(2,1)} %param.8) | copy-start | bytes 12582916
  83.1 2.7 %copy-start.3 = (f32[1,128,512]{2,1,0:T(8,128)S(1)}, f32[1,128,512]{2,1,0:T(8,128)}, u32[]{:S(2)}) copy-start(f32[1,128,512]{2,1,0:T(8,128)} %param.7) | copy-start | bytes 786436
  95.4 7.7 %collective-permute-start.2 = (f32[128,512]{1,0:T(8,128)S(1)}, f32[128,512]{1,0:T(8,128)S(1)}, u32[]{:S(2)}, u32[]{:S(2)}) collective-permute-start(f32[128,512]{1,0:T(8,128)S(1)} %multiply_subtract_fusion.1), channel_id=1, source_target_pairs={{1,0},{2,1},{3,2},{4,3},{5,4},{6,5},{7,6},{8,7},{9,8},{10,9},{11,1... | collective-permute-start | bytes 786440 | tf_op jit(solution)/shard_map/ppermute | solution.py:14
  97.5 5.7 %collective-permute-start.3 = (f32[512]{0:T(512)S(1)}, f32[512]{0:T(512)S(1)}, u32[]{:S(2)}, u32[]{:S(2)}) collective-permute-start(f32[512]{0:T(512)S(1)} %reduce_prod.9), channel_id=1, source_target_pairs={{1,0},{2,1},{3,2},{4,3},{5,4},{6,5},{7,6},{8,7},{9,8},{10,9},{11,1... | collective-permute-start | bytes 6152 | tf_op jit(solution)/shard_map/ppermute | solution.py:14
  103.1 0.8 copy-start.1
  103.2 0.8 copy-start.7
  152.4 4.0 %copy-start.5 = (f32[128,512]{1,0:T(8,128)S(1)}, f32[128,512]{1,0:T(8,128)}, u32[]{:S(2)}) copy-start(f32[128,512]{1,0:T(8,128)} %shard_map.78) | copy-start | bytes 786436

commit v7 on v6

--- a/solution.py
+++ b/solution.py
@@ -17,12 +17,12 @@
 MESH = pl.DeviceIdType.MESH
 
 
-def group_kernel(size, reverse, pieces, mine_ref, other_ref, offset_ref, factor_ref, out_ref, got, state, q_got, q_state, gathered, final, sends, recvs):
+def group_kernel(size, reverse, pieces, mine_ref, other_ref, out_ref, got, state, q_got, q_state, gathered, final, pair, sends, recvs):
     position = lax.axis_index("depth")
     order = size - 1 - position if reverse else position
     core, chip = (order % 2, order // 2)
     ring, group = (chip % 4, chip // 4)
-    rows = offset_ref.shape[0]
+    rows = out_ref.shape[0]
     half = mine_ref.shape[1]
     groups = size // 8
     quarter = rows // 4
@@ -55,7 +55,7 @@
         targets += [order + 8 * k * spread_width for k in ks] + [order - 8 * k * spread_width for k in ks]
     targets += [order - index + (index + t) % 8 for t in range(1, 8)]
     targets += [order - index + (index - t + 8) % 8 for t in range(1, 8)]
-    targets += [order + 1, order - 1, order + 2, order - 2]
+    targets += [order + 1, order - 1, order + 2, order - 2, order + 3, order - 3]
     barrier = pltpu.get_barrier_semaphore()
     for target in targets:
         pl.semaphore_signal(barrier, inc=1, device_id=device(target), device_id_type=MESH)
@@ -112,8 +112,8 @@
                 )
         pending = following
 
-    near = copy(state.at[2], final.at[0], slot_f, 0, order + 1)
-    far = copy(state.at[2], final.at[1], slot_f, 1, order + 2)
+    sides = [copy(state.at[2], final.at[k], slot_f, k, order + 1 + k) for k in range(3)]
+    sides.append(copy(mine_ref, pair, slot_f, 3, partner))
 
     def scatter(start):
         for k in range(4):
@@ -167,27 +167,26 @@
     depth = len(levels)
     prefix = q_state.at[depth].at[pl.ds(0, quarter), :]
     spread_copies = [copy(prefix, gathered.at[t - 1], slot_e, t - 1, order - index + (index + t) % 8) for t in range(1, 8)]
-    near.wait_recv()
-    far.wait_recv()
-    for handle in spread_copies:
+    for handle in sides + spread_copies:
         handle.wait_recv()
     at_start = ring == 0
     for t in range(8):
         owner = (index - t + 8) % 8
         owner_ring, owner_core = (owner // 2, owner % 2)
         band = pl.ds(pl.multiple_of(owner_ring * quarter, quarter), quarter)
-        cols = pl.ds(pl.multiple_of(owner_core * half, half), half)
         piece = q_state[depth, :quarter, :] if t == 0 else gathered[t - 1]
         left_side = owner_core == 0
-        close = final[0, band, :]
-        before = jnp.where(left_side, final[1, band, :], close)
-        before_scale = jnp.where(left_side, final[1, factor_row, :], final[0, factor_row, :])
+        low = jnp.where(first, final[1, band, :], final[2, band, :])
+        low_scale = jnp.where(first, final[1, factor_row, :], final[2, factor_row, :])
+        high = jnp.where(first, final[0, band, :], final[1, band, :])
+        high_scale = jnp.where(first, final[0, factor_row, :], final[1, factor_row, :])
+        before = jnp.where(left_side, low, high)
+        before_scale = jnp.where(left_side, low_scale, high_scale)
         behind = jnp.where(at_start, piece, before + before_scale * piece)
-        tail = offset_ref[band, cols] + factor_ref[0:1, cols] * behind
-        current = jnp.where(left_side, close, state[2, band, :])
-        current_scale = jnp.where(left_side, final[0, factor_row, :], state[2, factor_row, :])
-        head = current + current_scale * piece
-        out_ref[band, cols] = jnp.where(first, tail, head)
+        element = jnp.where(left_side, pair[band, :], got[0, band, :])
+        element_scale = jnp.where(left_side, pair[factor_row, :], got[0, factor_row, :])
+        cols = pl.ds(pl.multiple_of(owner_core * half, half), half)
+        out_ref[band, cols] = jnp.where(first, behind, element + element_scale * behind)
     for handle in started:
         handle.wait_send()
 
@@ -219,7 +218,7 @@
     return pl.pallas_call(
         functools.partial(group_kernel, size, reverse, 4),
         out_shape=jax.ShapeDtypeStruct((rows, width), jnp.float32),
-        in_specs=[pl.BlockSpec(memory_space=pltpu.VMEM)] * 4,
+        in_specs=[pl.BlockSpec(memory_space=pltpu.VMEM)] * 2,
         out_specs=pl.BlockSpec(memory_space=pltpu.VMEM),
         scratch_shapes=[
             pltpu.VMEM((3, rows + 8, half), jnp.float32),
@@ -227,12 +226,13 @@
             pltpu.VMEM((links + 1, quarter + 8, half), jnp.float32),
             pltpu.VMEM((levels + 1, quarter + 8, half), jnp.float32),
             pltpu.VMEM((7, quarter, half), jnp.float32),
-            pltpu.VMEM((2, rows + 8, half), jnp.float32),
+            pltpu.VMEM((3, rows + 8, half), jnp.float32),
+            pltpu.VMEM((rows + 8, half), jnp.float32),
             pltpu.SemaphoreType.DMA((6 + levels, 8)),
             pltpu.SemaphoreType.DMA((6 + levels, 8)),
         ],
         compiler_params=pltpu.CompilerParams(collective_id=ident, has_side_effects=True),
-    )(mine, other, offset, spread)
+    )(mine, other)
 
 
 def prepare_block(state, w_first, gain_row):
@@ -305,24 +305,18 @@
     position = lax.axis_index("depth")
     devices = lax.axis_size("depth")
     factor = jnp.prod(decay, axis=0)
-    at_first = position == 0
-    at_last = position == devices - 1
-    factor_before = shifted(factor, "depth", 1)
-    factor_after = shifted(factor, "depth", -1)
     guess_state = state_guess[0]
+    guess_adjoint = adjoint_guess[0]
+    next_guess = shifted(guess_state, "depth", -1)
+    prev_guess = shifted(guess_adjoint, "depth", 1)
     end_state, _, _, _ = relax_forward(guess_state, w_in, w_out, norm_gain, decay, True)
-    end_before = shifted(end_state, "depth", 1)
-    resid = jnp.where(at_first, jnp.zeros_like(guess_state), end_before - guess_state)
-    correction = kernel_scan(factor_before, resid, False, 0)
+    correction = kernel_scan(factor, end_state - next_guess, False, 0)
     start = guess_state + correction
     _, states, inverses, preacts = relax_forward(start, w_in, w_out, norm_gain, decay, False)
-    guess_adjoint = adjoint_guess[0]
     first_adjoint, _ = relax_backward(
         guess_adjoint, states, inverses, preacts, w_in, w_out, norm_gain, decay
     )
-    first_after = shifted(first_adjoint, "depth", -1)
-    rho = jnp.where(at_last, jnp.zeros_like(guess_adjoint), first_after - guess_adjoint)
-    eps = kernel_scan(factor_after, rho, True, 1)
+    eps = kernel_scan(factor, first_adjoint - prev_guess, True, 1)
     head = guess_adjoint + eps
     _, lambdas = relax_backward(head, states, inverses, preacts, w_in, w_out, norm_gain, decay)
     return (jnp.stack(states), jnp.stack(lambdas))

time: 162 us -> 158 us (0.975)
  waiting for transfers between devices: 4.14 us -> 0.01 us
  Pallas kernels: 110 us -> 114 us
  starting transfers between devices: 10.4 us -> 7.12 us
    pallas_call x2, Pallas kernels: 110 us -> 114 us  [kernel_scan(): pl.pallas_call(functools.partial(group_kernel, size, reverse, 4), out_sha...]
    ppermute x4 -> x2, waiting for transfers between devices: 4.14 us -> 0.01 us  [shifted(): return lax.ppermute(block, axis, route)]
    ppermute x4 -> x2, starting transfers between devices: 10.4 us -> 7.12 us  [shifted(): return lax.ppermute(block, axis, route)]
  transfers between devices with their start and end apart: 4 -> 2, of which waited for: 2 -> 0; matrix products, arithmetic and copies ran while one was open for 1% -> 14% of each run, Pallas kernels for 0% -> 40%
where the time goes in v7:
time: 158 us; the launch traced here: 157 us
  Pallas kernels  114 us (72%)
  matrix products  25.1 us (16%)
  starting transfers between devices  7.12 us (5%)
  other arithmetic  6.34 us (4%)
  local copies, waits for them, and re-layouts  3.1 us (2%)
    pallas_call x2, Pallas kernels, kernel_scan(): pl.pallas_call(functools.partial(group_kernel, size, reverse, 4), out_sha...  114 us
    dot_general x4, matrix products, backward_block(): lax.dot_general(grad_pre, w_first, (((1,), (1,)), ((), ())), preferred_el...  15.6 us
    ppermute x2, starting transfers between devices, shifted(): return lax.ppermute(block, axis, route)  7.12 us
    dot_general x3, matrix products, finish_block(): jnp.dot(hidden, w_second, preferred_element_type=jnp.float32)  6.84 us
  transfers between devices with their start and end apart: 2, of which 0 were waited for; matrix products, arithmetic and copies ran while one was open for 14% of the time, Pallas kernels for 40%

profile of v7, /device:TPU:1, one launch (start us, length us, event | category | flops | bytes accessed | tf_op | source)
XLA Modules:
  0.0 156.9 jit_solution(6676553582497423052)
XLA Ops:
  0.6 4.5 %collective-permute-start.1 = (f32[128,512]{1,0:T(8,128)}, f32[128,512]{1,0:T(8,128)}, u32[]{:S(2)}, u32[]{:S(2)}) collective-permute-start(f32[128,512]{1,0:T(8,128)} %bitcast.127), channel_id=1, source_target_pairs={{0,1},{1,2},{2,3},{3,4},{4,5},{5,6},{6,7},{7,8},{8,9},{9,10},{10,1... | collective-permute-start | bytes 786440 | tf_op jit(solution)/shard_map/ppermute | solution.py:14
  5.1 2.6 %collective-permute-start = (f32[128,512]{1,0:T(8,128)}, f32[128,512]{1,0:T(8,128)S(1)}, u32[]{:S(2)}, u32[]{:S(2)}) collective-permute-start(f32[128,512]{1,0:T(8,128)} %bitcast.128), channel_id=1, source_target_pairs={{1,0},{2,1},{3,2},{4,3},{5,4},{6,5},{7,6},{8,7},{9,8},{10,9},{11,1... | collective-permute-start | bytes 786440 | tf_op jit(solution)/shard_map/ppermute | solution.py:14
  7.8 1.1 multiply_reduce_fusion.7
  8.8 0.8 fusion.137
  9.6 0.8 fusion.136
  10.4 3.2 %multiply_reduce_fusion.6 = (f32[128]{0:T(128)S(1)}, f32[128,512]{1,0:T(8,128)S(1)}) fusion(bf16[2,2048,512]{2,1,0:T(8,128)(2,1)} %param.9, bf16[2,512,2048]{2,1,0:T(8,128)(2,1)} %param.8, f32[1,128,512]{2,1,0:T(8,128)} %param.6, f32[512]{0:T(512)S(1)} %bitcast.136, f32[128]{0:T(128)S(1)} %add_rsqrt_fusion.3, f32[512]{0:T(512)S(1)} %bitcast.129), kind=kOutput, calls=%fused_computation.98 | convolution fusion | flops 538640256 | bytes 4985856 | tf_op jit(solution)/shard_map/dot_general | solution.py:247
  13.7 3.0 %fusion.70 = f32[128,512]{1,0:T(8,128)S(1)} fusion(f32[128,512]{1,0:T(8,128)S(1)} %collective-permute-done, bf16[2,2048,512]{2,1,0:T(8,128)(2,1)} %param.9, bf16[2,512,2048]{2,1,0:T(8,128)(2,1)} %param.8, f32[128,512]{1,0:T(8,128)S(1)} %get-tuple-element.17, f32[512]{0:T(512)S(1)} %bitcast.140, f32[128]{0:T(128)S(1)} %add_rsqrt_fusion.2, f32[512]{0:T(512)S(1)} %bitcast.133), kind=kOutput, calls=%fused_computation.60 | convolution fusion | flops 538574848 | bytes 5247488 | tf_op jit(solution)/shard_map/dot_general | solution.py:247
  16.7 0.7 fusion.98
  17.5 63.4 %shard_map.77 = f32[128,512]{1,0:T(8,128)} custom-call(f32[136,256]{1,0:T(8,128)} %get-tuple-element.7.mine_ref, f32[136,256]{1,0:T(8,128)} %get-tuple-element.6.other_ref), custom_call_target="tpu_custom_call" | custom-call | tf_op jit(solution)/shard_map/pallas_call | solution.py:218
  80.8 1.2 multiply_reduce_fusion.5
  82.1 2.2 %fusion.30 = f32[128,2048]{1,0:T(8,128)S(1)} fusion(bf16[2,512,2048]{2,1,0:T(8,128)(2,1)} %param.8, f32[128,512]{1,0:T(8,128)S(1)} %get-tuple-element.3, f32[512]{0:T(512)S(1)} %bitcast.137, f32[128]{0:T(128)S(1)} %get-tuple-element.13), kind=kOutput, calls=%fused_computation.34 | convolution fusion | flops 268632064 | bytes 3410432 | tf_op jit(solution)/shard_map/dot_general | solution.py:241
  84.3 0.6 multiply_reduce_fusion.4
  84.9 1.5 copy-done
  86.5 0.5 fusion.16
  87.0 3.9 %multiply_reduce_fusion.3 = (f32[128]{0:T(128)S(1)}, f32[128,512]{1,0:T(8,128)S(1)}) fusion(f32[128,512]{1,0:T(8,128)S(1)} %get-tuple-element.19, f32[512]{0:T(512)S(1)} %bitcast.142, bf16[2,512,2048]{2,1,0:T(8,128)(2,1)} %param.8, bf16[2,2048,512]{2,1,0:T(8,128)(2,1)} %param.9, f32[128,2048]{1,0:T(8,128)S(1)} %fusion.16, f32[1,128,512]{2,1,0:T(8,128)S(1)} %copy-done.1), kind=kOutput, calls=%fused_computation.92 | convolution fusion | flops 539492224 | bytes 6031872 | tf_op jit(solution)/shard_map/dot_general | solution.py:259
  91.0 3.9 %multiply_reduce_fusion.2 = (f32[128]{0:T(128)S(1)}, f32[128,512]{1,0:T(8,128)S(1)}) fusion(f32[128,512]{1,0:T(8,128)S(1)} %get-tuple-element.3, f32[512]{0:T(512)S(1)} %bitcast.138, bf16[2,512,2048]{2,1,0:T(8,128)(2,1)} %param.8, bf16[2,2048,512]{2,1,0:T(8,128)(2,1)} %param.9, f32[128,2048]{1,0:T(8,128)S(1)} %fusion.30, ...), kind=kOutput, calls=%fused_computation.90 | convolution fusion | flops 539492224 | bytes 6031872 | tf_op jit(solution)/shard_map/dot_general | solution.py:259
  94.9 1.1 subtract_subtract_fusion
  96.0 0.7 fusion.96
  96.7 51.0 %shard_map.78 = f32[128,512]{1,0:T(8,128)} custom-call(f32[136,256]{1,0:T(8,128)} %get-tuple-element.5.mine_ref, f32[136,256]{1,0:T(8,128)} %get-tuple-element.4.other_ref), custom_call_target="tpu_custom_call" | custom-call | tf_op jit(solution)/shard_map/pallas_call | solution.py:218
  147.7 4.0 %multiply_reduce_fusion.1 = (f32[128]{0:T(128)S(1)}, f32[128,512]{1,0:T(8,128)S(1)}) fusion(f32[128,512]{1,0:T(8,128)S(1)} %get-tuple-element.19, f32[512]{0:T(512)S(1)} %bitcast.143, bf16[2,512,2048]{2,1,0:T(8,128)(2,1)} %param.8, bf16[2,2048,512]{2,1,0:T(8,128)(2,1)} %param.9, f32[128,2048]{1,0:T(8,128)S(1)} %fusion.16, f32[128,512]{1,0:T(8,128)} %shard_map.78, ...), kind=kOutput, calls=%fused_computation.88 | convolution fusion | flops 539557760 | bytes 6294016 | tf_op jit(solution)/shard_map/dot_general | solution.py:259
  151.7 0.1 multiply_subtract_fusion
  151.9 3.9 %multiply_reduce_fusion = (f32[128]{0:T(128)S(1)}, f32[128,512]{1,0:T(8,128)S(1)}) fusion(f32[128,512]{1,0:T(8,128)S(1)} %get-tuple-element.3, f32[512]{0:T(512)S(1)} %bitcast.139, bf16[2,512,2048]{2,1,0:T(8,128)(2,1)} %param.8, bf16[2,2048,512]{2,1,0:T(8,128)(2,1)} %param.9, f32[128,2048]{1,0:T(8,128)S(1)} %fusion.30, f32[128,512]{1,0:T(8,128)S(1)} %multiply_subtract_fusion), kind=kOutput, calls=%fused_computation.86 | convolution fusion | flops 539492224 | bytes 6031872 | tf_op jit(solution)/shard_map/dot_general | solution.py:259
  155.7 0.1 subtract_bitcast_fusion
  155.9 1.0 pad_maximum_fusion
  (24 shorter events, 0.3 us)
Async XLA Ops:
  0.6 94.2 %collective-permute-start.1 = (f32[128,512]{1,0:T(8,128)}, f32[128,512]{1,0:T(8,128)}, u32[]{:S(2)}, u32[]{:S(2)}) collective-permute-start(f32[128,512]{1,0:T(8,128)} %bitcast.127), channel_id=1, source_target_pairs={{0,1},{1,2},{2,3},{3,4},{4,5},{5,6},{6,7},{7,8},{8,9},{9,10},{10,1... | collective-permute-start | bytes 786440 | tf_op jit(solution)/shard_map/ppermute | solution.py:14
  5.1 8.5 %collective-permute-start = (f32[128,512]{1,0:T(8,128)}, f32[128,512]{1,0:T(8,128)S(1)}, u32[]{:S(2)}, u32[]{:S(2)}) collective-permute-start(f32[128,512]{1,0:T(8,128)} %bitcast.128), channel_id=1, source_target_pairs={{1,0},{2,1},{3,2},{4,3},{5,4},{6,5},{7,6},{8,7},{9,8},{10,9},{11,1... | collective-permute-start | bytes 786440 | tf_op jit(solution)/shard_map/ppermute | solution.py:14
  10.4 3.2 %copy-start.4 = (f32[2,512]{1,0:T(2,128)S(1)}, f32[2,512]{1,0:T(2,128)}, u32[]{:S(2)}) copy-start(f32[2,512]{1,0:T(2,128)} %param.11) | copy-start | bytes 12292
  13.7 67.2 %copy-start.2 = (f32[1,128,512]{2,1,0:T(8,128)S(1)}, f32[1,128,512]{2,1,0:T(8,128)}, u32[]{:S(2)}) copy-start(f32[1,128,512]{2,1,0:T(8,128)} %param.6) | copy-start | bytes 786436
  80.8 3.4 %copy-start.5 = (bf16[2,2048,512]{2,1,0:T(8,128)(2,1)S(1)}, bf16[2,2048,512]{2,1,0:T(8,128)(2,1)}, u32[]{:S(2)}) copy-start(bf16[2,2048,512]{2,1,0:T(8,128)(2,1)} %param.9) | copy-start | bytes 12582916
  84.3 2.2 %copy-start = (bf16[2,512,2048]{2,1,0:T(8,128)(2,1)S(1)}, bf16[2,512,2048]{2,1,0:T(8,128)(2,1)}, u32[]{:S(2)}) copy-start(bf16[2,512,2048]{2,1,0:T(8,128)(2,1)} %param.8) | copy-start | bytes 12582916
  84.3 2.7 %copy-start.1 = (f32[1,128,512]{2,1,0:T(8,128)S(1)}, f32[1,128,512]{2,1,0:T(8,128)}, u32[]{:S(2)}) copy-start(f32[1,128,512]{2,1,0:T(8,128)} %param.7) | copy-start | bytes 786436
  147.7 4.0 %copy-start.3 = (f32[128,512]{1,0:T(8,128)S(1)}, f32[128,512]{1,0:T(8,128)}, u32[]{:S(2)}) copy-start(f32[128,512]{1,0:T(8,128)} %shard_map.78) | copy-start | bytes 786436

commit v8 on v7

--- a/solution.py
+++ b/solution.py
@@ -15,6 +15,17 @@
 
 
 MESH = pl.DeviceIdType.MESH
+
+
+def radices(groups):
+    along_z = min(groups, 8)
+    out = []
+    for part in (along_z, groups // along_z):
+        while part > 1:
+            step = 4 if part % 4 == 0 else 2
+            out.append(step)
+            part //= step
+    return out
 
 
 def group_kernel(size, reverse, pieces, mine_ref, other_ref, out_ref, got, state, q_got, q_state, gathered, final, pair, sends, recvs):
@@ -30,10 +41,9 @@
     spans = [(rows, 8)] + [(k * step_rows, step_rows) for k in range(pieces)]
     levels = []
     width_now = 1
-    while width_now < groups:
-        ks = [k for k in (1, 2, 3) if k * width_now < groups]
-        levels.append((width_now, ks))
-        width_now *= len(ks) + 1
+    for step in radices(groups):
+        levels.append((width_now, list(range(1, step))))
+        width_now *= step
     links = [(level, k) for level, (_, ks) in enumerate(levels) for k in ks]
     slot_c, slot_e, slot_f = (3, 4 + len(levels), 5 + len(levels))
     index = order % 8
@@ -48,13 +58,11 @@
     partner = order + 1 - 2 * core
     source = order - 8 + 2 * (3 - ring)
     sinks = [order + 8 + 2 * (k - 3) for k in range(4)]
-    targets = [partner, in_ring(1), in_ring(-1), in_ring(2), in_ring(-2)]
-    targets += [order + 8 + 2 * (k - ring) for k in range(4)]
+    targets = [order + 8 + 2 * (k - ring) for k in range(4)]
     targets += [order - 8 + 2 * (k - ring) for k in range(4)]
     for spread_width, ks in levels:
         targets += [order + 8 * k * spread_width for k in ks] + [order - 8 * k * spread_width for k in ks]
     targets += [order - index + (index + t) % 8 for t in range(1, 8)]
-    targets += [order - index + (index - t + 8) % 8 for t in range(1, 8)]
     targets += [order + 1, order - 1, order + 2, order - 2, order + 3, order - 3]
     barrier = pltpu.get_barrier_semaphore()
     for target in targets:
@@ -206,14 +214,8 @@
     mine = lax.dynamic_slice_in_dim(packed, core * half, half, axis=1)
     other = lax.dynamic_slice_in_dim(packed, (1 - core) * half, half, axis=1)
     groups = size // 8
-    links = 0
-    levels = 0
-    width_now = 1
-    while width_now < groups:
-        ks = [k for k in (1, 2, 3) if k * width_now < groups]
-        links += len(ks)
-        levels += 1
-        width_now *= len(ks) + 1
+    links = sum(step - 1 for step in radices(groups))
+    levels = len(radices(groups))
     quarter = rows // 4
     return pl.pallas_call(
         functools.partial(group_kernel, size, reverse, 4),

time: 158 us -> 154 us (0.975)
  Pallas kernels: 114 us -> 109 us
    pallas_call x2, Pallas kernels: 114 us -> 109 us  [kernel_scan(): pl.pallas_call(functools.partial(group_kernel, size, reverse, 4), out_sha...]
where the time goes in v8:
time: 154 us; the launch traced here: 152 us
  Pallas kernels  109 us (71%)
  matrix products  25.1 us (16%)
  starting transfers between devices  7.12 us (5%)
  other arithmetic  6.34 us (4%)
  local copies, waits for them, and re-layouts  3.1 us (2%)
    pallas_call x2, Pallas kernels, kernel_scan(): pl.pallas_call(functools.partial(group_kernel, size, reverse, 4), out_sha...  109 us
    dot_general x4, matrix products, backward_block(): lax.dot_general(grad_pre, w_first, (((1,), (1,)), ((), ())), preferred_el...  15.6 us
    ppermute x2, starting transfers between devices, shifted(): return lax.ppermute(block, axis, route)  7.12 us
    dot_general x3, matrix products, finish_block(): jnp.dot(hidden, w_second, preferred_element_type=jnp.float32)  6.84 us
  transfers between devices with their start and end apart: 2, of which 0 were waited for; matrix products, arithmetic and copies ran while one was open for 14% of the time, Pallas kernels for 40%

profile of v8, /device:TPU:1, one launch (start us, length us, event | category | flops | bytes accessed | tf_op | source)
XLA Modules:
  0.0 151.6 jit_solution(10312953648614544847)
XLA Ops:
  0.6 4.5 %collective-permute-start.1 = (f32[128,512]{1,0:T(8,128)}, f32[128,512]{1,0:T(8,128)}, u32[]{:S(2)}, u32[]{:S(2)}) collective-permute-start(f32[128,512]{1,0:T(8,128)} %bitcast.127), channel_id=1, source_target_pairs={{0,1},{1,2},{2,3},{3,4},{4,5},{5,6},{6,7},{7,8},{8,9},{9,10},{10,1... | collective-permute-start | bytes 786440 | tf_op jit(solution)/shard_map/ppermute | solution.py:14
  5.1 2.6 %collective-permute-start = (f32[128,512]{1,0:T(8,128)}, f32[128,512]{1,0:T(8,128)S(1)}, u32[]{:S(2)}, u32[]{:S(2)}) collective-permute-start(f32[128,512]{1,0:T(8,128)} %bitcast.128), channel_id=1, source_target_pairs={{1,0},{2,1},{3,2},{4,3},{5,4},{6,5},{7,6},{8,7},{9,8},{10,9},{11,1... | collective-permute-start | bytes 786440 | tf_op jit(solution)/shard_map/ppermute | solution.py:14
  7.8 1.1 multiply_reduce_fusion.7
  8.8 0.8 fusion.137
  9.6 0.8 fusion.136
  10.4 3.2 %multiply_reduce_fusion.6 = (f32[128]{0:T(128)S(1)}, f32[128,512]{1,0:T(8,128)S(1)}) fusion(bf16[2,2048,512]{2,1,0:T(8,128)(2,1)} %param.9, bf16[2,512,2048]{2,1,0:T(8,128)(2,1)} %param.8, f32[1,128,512]{2,1,0:T(8,128)} %param.6, f32[512]{0:T(512)S(1)} %bitcast.136, f32[128]{0:T(128)S(1)} %add_rsqrt_fusion.3, f32[512]{0:T(512)S(1)} %bitcast.129), kind=kOutput, calls=%fused_computation.98 | convolution fusion | flops 538640256 | bytes 4985856 | tf_op jit(solution)/shard_map/dot_general | solution.py:249
  13.7 3.0 %fusion.70 = f32[128,512]{1,0:T(8,128)S(1)} fusion(f32[128,512]{1,0:T(8,128)S(1)} %collective-permute-done, bf16[2,2048,512]{2,1,0:T(8,128)(2,1)} %param.9, bf16[2,512,2048]{2,1,0:T(8,128)(2,1)} %param.8, f32[128,512]{1,0:T(8,128)S(1)} %get-tuple-element.17, f32[512]{0:T(512)S(1)} %bitcast.140, f32[128]{0:T(128)S(1)} %add_rsqrt_fusion.2, f32[512]{0:T(512)S(1)} %bitcast.133), kind=kOutput, calls=%fused_computation.60 | convolution fusion | flops 538574848 | bytes 5247488 | tf_op jit(solution)/shard_map/dot_general | solution.py:249
  16.7 0.7 fusion.98
  17.5 61.0 %shard_map.77 = f32[128,512]{1,0:T(8,128)} custom-call(f32[136,256]{1,0:T(8,128)} %get-tuple-element.7.mine_ref, f32[136,256]{1,0:T(8,128)} %get-tuple-element.6.other_ref), custom_call_target="tpu_custom_call" | custom-call | tf_op jit(solution)/shard_map/pallas_call | solution.py:220
  78.5 1.2 multiply_reduce_fusion.5
  79.7 2.2 %fusion.30 = f32[128,2048]{1,0:T(8,128)S(1)} fusion(bf16[2,512,2048]{2,1,0:T(8,128)(2,1)} %param.8, f32[128,512]{1,0:T(8,128)S(1)} %get-tuple-element.3, f32[512]{0:T(512)S(1)} %bitcast.137, f32[128]{0:T(128)S(1)} %get-tuple-element.13), kind=kOutput, calls=%fused_computation.34 | convolution fusion | flops 268632064 | bytes 3410432 | tf_op jit(solution)/shard_map/dot_general | solution.py:243
  81.9 0.6 multiply_reduce_fusion.4
  82.6 1.5 %copy-done = bf16[2,512,2048]{2,1,0:T(8,128)(2,1)S(1)} copy-done((bf16[2,512,2048]{2,1,0:T(8,128)(2,1)S(1)}, bf16[2,512,2048]{2,1,0:T(8,128)(2,1)}, u32[]{:S(2)}) %copy-start) | copy-done | bytes 4194328
  84.1 0.5 fusion.16
  84.6 3.9 %multiply_reduce_fusion.3 = (f32[128]{0:T(128)S(1)}, f32[128,512]{1,0:T(8,128)S(1)}) fusion(f32[128,512]{1,0:T(8,128)S(1)} %get-tuple-element.19, f32[512]{0:T(512)S(1)} %bitcast.142, bf16[2,512,2048]{2,1,0:T(8,128)(2,1)} %param.8, bf16[2,2048,512]{2,1,0:T(8,128)(2,1)} %param.9, f32[128,2048]{1,0:T(8,128)S(1)} %fusion.16, f32[1,128,512]{2,1,0:T(8,128)S(1)} %copy-done.1), kind=kOutput, calls=%fused_computation.92 | convolution fusion | flops 539492224 | bytes 6031872 | tf_op jit(solution)/shard_map/dot_general | solution.py:261
  88.6 3.9 %multiply_reduce_fusion.2 = (f32[128]{0:T(128)S(1)}, f32[128,512]{1,0:T(8,128)S(1)}) fusion(f32[128,512]{1,0:T(8,128)S(1)} %get-tuple-element.3, f32[512]{0:T(512)S(1)} %bitcast.138, bf16[2,512,2048]{2,1,0:T(8,128)(2,1)} %param.8, bf16[2,2048,512]{2,1,0:T(8,128)(2,1)} %param.9, f32[128,2048]{1,0:T(8,128)S(1)} %fusion.30, ...), kind=kOutput, calls=%fused_computation.90 | convolution fusion | flops 539492224 | bytes 6031872 | tf_op jit(solution)/shard_map/dot_general | solution.py:261
  92.5 1.1 subtract_subtract_fusion
  93.6 0.7 fusion.96
  94.3 48.1 %shard_map.78 = f32[128,512]{1,0:T(8,128)} custom-call(f32[136,256]{1,0:T(8,128)} %get-tuple-element.5.mine_ref, f32[136,256]{1,0:T(8,128)} %get-tuple-element.4.other_ref), custom_call_target="tpu_custom_call" | custom-call | tf_op jit(solution)/shard_map/pallas_call | solution.py:220
  142.4 4.0 %multiply_reduce_fusion.1 = (f32[128]{0:T(128)S(1)}, f32[128,512]{1,0:T(8,128)S(1)}) fusion(f32[128,512]{1,0:T(8,128)S(1)} %get-tuple-element.19, f32[512]{0:T(512)S(1)} %bitcast.143, bf16[2,512,2048]{2,1,0:T(8,128)(2,1)} %param.8, bf16[2,2048,512]{2,1,0:T(8,128)(2,1)} %param.9, f32[128,2048]{1,0:T(8,128)S(1)} %fusion.16, f32[128,512]{1,0:T(8,128)} %shard_map.78, ...), kind=kOutput, calls=%fused_computation.88 | convolution fusion | flops 539557760 | bytes 6294016 | tf_op jit(solution)/shard_map/dot_general | solution.py:261
  146.4 0.1 multiply_subtract_fusion
  146.6 3.9 %multiply_reduce_fusion = (f32[128]{0:T(128)S(1)}, f32[128,512]{1,0:T(8,128)S(1)}) fusion(f32[128,512]{1,0:T(8,128)S(1)} %get-tuple-element.3, f32[512]{0:T(512)S(1)} %bitcast.139, bf16[2,512,2048]{2,1,0:T(8,128)(2,1)} %param.8, bf16[2,2048,512]{2,1,0:T(8,128)(2,1)} %param.9, f32[128,2048]{1,0:T(8,128)S(1)} %fusion.30, f32[128,512]{1,0:T(8,128)S(1)} %multiply_subtract_fusion), kind=kOutput, calls=%fused_computation.86 | convolution fusion | flops 539492224 | bytes 6031872 | tf_op jit(solution)/shard_map/dot_general | solution.py:261
  150.4 0.1 subtract_bitcast_fusion
  150.6 1.0 pad_maximum_fusion
  (24 shorter events, 0.3 us)
Async XLA Ops:
  0.6 91.9 %collective-permute-start.1 = (f32[128,512]{1,0:T(8,128)}, f32[128,512]{1,0:T(8,128)}, u32[]{:S(2)}, u32[]{:S(2)}) collective-permute-start(f32[128,512]{1,0:T(8,128)} %bitcast.127), channel_id=1, source_target_pairs={{0,1},{1,2},{2,3},{3,4},{4,5},{5,6},{6,7},{7,8},{8,9},{9,10},{10,1... | collective-permute-start | bytes 786440 | tf_op jit(solution)/shard_map/ppermute | solution.py:14
  5.1 8.5 %collective-permute-start = (f32[128,512]{1,0:T(8,128)}, f32[128,512]{1,0:T(8,128)S(1)}, u32[]{:S(2)}, u32[]{:S(2)}) collective-permute-start(f32[128,512]{1,0:T(8,128)} %bitcast.128), channel_id=1, source_target_pairs={{1,0},{2,1},{3,2},{4,3},{5,4},{6,5},{7,6},{8,7},{9,8},{10,9},{11,1... | collective-permute-start | bytes 786440 | tf_op jit(solution)/shard_map/ppermute | solution.py:14
  10.4 3.2 %copy-start.4 = (f32[2,512]{1,0:T(2,128)S(1)}, f32[2,512]{1,0:T(2,128)}, u32[]{:S(2)}) copy-start(f32[2,512]{1,0:T(2,128)} %param.11) | copy-start | bytes 12292
  13.7 64.8 %copy-start.2 = (f32[1,128,512]{2,1,0:T(8,128)S(1)}, f32[1,128,512]{2,1,0:T(8,128)}, u32[]{:S(2)}) copy-start(f32[1,128,512]{2,1,0:T(8,128)} %param.6) | copy-start | bytes 786436
  78.5 3.4 %copy-start.5 = (bf16[2,2048,512]{2,1,0:T(8,128)(2,1)S(1)}, bf16[2,2048,512]{2,1,0:T(8,128)(2,1)}, u32[]{:S(2)}) copy-start(bf16[2,2048,512]{2,1,0:T(8,128)(2,1)} %param.9) | copy-start | bytes 12582916
  81.9 2.2 %copy-start = (bf16[2,512,2048]{2,1,0:T(8,128)(2,1)S(1)}, bf16[2,512,2048]{2,1,0:T(8,128)(2,1)}, u32[]{:S(2)}) copy-start(bf16[2,512,2048]{2,1,0:T(8,128)(2,1)} %param.8) | copy-start | bytes 12582916
  81.9 2.7 %copy-start.1 = (f32[1,128,512]{2,1,0:T(8,128)S(1)}, f32[1,128,512]{2,1,0:T(8,128)}, u32[]{:S(2)}) copy-start(f32[1,128,512]{2,1,0:T(8,128)} %param.7) | copy-start | bytes 786436
  142.4 4.0 %copy-start.3 = (f32[128,512]{1,0:T(8,128)S(1)}, f32[128,512]{1,0:T(8,128)}, u32[]{:S(2)}) copy-start(f32[128,512]{1,0:T(8,128)} %shard_map.78) | copy-start | bytes 786436

commit v9 on v8

--- a/solution.py
+++ b/solution.py
@@ -28,13 +28,13 @@
     return out
 
 
-def group_kernel(size, reverse, pieces, mine_ref, other_ref, out_ref, got, state, q_got, q_state, gathered, final, pair, sends, recvs):
+def group_kernel(size, reverse, pieces, packed_ref, out_ref, got, state, q_got, q_state, gathered, final, pair, sends, recvs):
     position = lax.axis_index("depth")
     order = size - 1 - position if reverse else position
     core, chip = (order % 2, order // 2)
     ring, group = (chip % 4, chip // 4)
     rows = out_ref.shape[0]
-    half = mine_ref.shape[1]
+    half = packed_ref.shape[1] // 2
     groups = size // 8
     quarter = rows // 4
     step_rows = rows // pieces
@@ -93,6 +93,8 @@
 
     first = core == 0
     factor_row = slice(rows, rows + 1)
+    mine_ref = packed_ref.at[:, pl.ds(pl.multiple_of(core * half, half), half)]
+    other_ref = packed_ref.at[:, pl.ds(pl.multiple_of((1 - core) * half, half), half)]
     pending = [copy(block(other_ref, k), block(got.at[0], k), 0, k, partner) for k in range(pieces + 1)]
     for stage in range(3):
         following = []
@@ -204,15 +206,11 @@
 
 
 def kernel_scan(factor, offset, reverse, ident):
-    size, position = (lax.axis_size("depth"), lax.axis_index("depth"))
+    size = lax.axis_size("depth")
     rows, width = offset.shape
     half = width // 2
-    order = size - 1 - position if reverse else position
-    core = order % 2
     spread = jnp.broadcast_to(factor[None, :], (8, width))
     packed = jnp.concatenate([offset, spread], axis=0)
-    mine = lax.dynamic_slice_in_dim(packed, core * half, half, axis=1)
-    other = lax.dynamic_slice_in_dim(packed, (1 - core) * half, half, axis=1)
     groups = size // 8
     links = sum(step - 1 for step in radices(groups))
     levels = len(radices(groups))
@@ -220,7 +218,7 @@
     return pl.pallas_call(
         functools.partial(group_kernel, size, reverse, 4),
         out_shape=jax.ShapeDtypeStruct((rows, width), jnp.float32),
-        in_specs=[pl.BlockSpec(memory_space=pltpu.VMEM)] * 2,
+        in_specs=[pl.BlockSpec(memory_space=pltpu.VMEM)],
         out_specs=pl.BlockSpec(memory_space=pltpu.VMEM),
         scratch_shapes=[
             pltpu.VMEM((3, rows + 8, half), jnp.float32),
@@ -234,7 +232,7 @@
             pltpu.SemaphoreType.DMA((6 + levels, 8)),
         ],
         compiler_params=pltpu.CompilerParams(collective_id=ident, has_side_effects=True),
-    )(mine, other)
+    )(packed)
 
 
 def prepare_block(state, w_first, gain_row):
@@ -304,8 +302,6 @@
 
 
 def shards(state_guess, adjoint_guess, w_in, w_out, norm_gain, decay):
-    position = lax.axis_index("depth")
-    devices = lax.axis_size("depth")
     factor = jnp.prod(decay, axis=0)
     guess_state = state_guess[0]
     guess_adjoint = adjoint_guess[0]

time: 154 us -> 153 us (level)
  no operation moved by 1% of the time
where the time goes in v9:
time: 153 us; the launch traced here: 152 us
  Pallas kernels  109 us (71%)
  matrix products  25.1 us (16%)
  starting transfers between devices  7.12 us (5%)
  other arithmetic  6.33 us (4%)
  local copies, waits for them, and re-layouts  3.1 us (2%)
    pallas_call x2, Pallas kernels, kernel_scan(): pl.pallas_call(functools.partial(group_kernel, size, reverse, 4), out_sha...  109 us
    dot_general x4, matrix products, backward_block(): lax.dot_general(grad_pre, w_first, (((1,), (1,)), ((), ())), preferred_el...  15.6 us
    ppermute x2, starting transfers between devices, shifted(): return lax.ppermute(block, axis, route)  7.12 us
    dot_general x3, matrix products, finish_block(): jnp.dot(hidden, w_second, preferred_element_type=jnp.float32)  6.85 us
  transfers between devices with their start and end apart: 2, of which 0 were waited for; matrix products, arithmetic and copies ran while one was open for 14% of the time, Pallas kernels for 40%

profile of v9, /device:TPU:1, one launch (start us, length us, event | category | flops | bytes accessed | tf_op | source)
XLA Modules:
  0.0 151.7 jit_solution(4691464359656386322)
XLA Ops:
  0.6 4.5 %collective-permute-start.1 = (f32[128,512]{1,0:T(8,128)}, f32[128,512]{1,0:T(8,128)}, u32[]{:S(2)}, u32[]{:S(2)}) collective-permute-start(f32[128,512]{1,0:T(8,128)} %bitcast.127), channel_id=1, source_target_pairs={{0,1},{1,2},{2,3},{3,4},{4,5},{5,6},{6,7},{7,8},{8,9},{9,10},{10,1... | collective-permute-start | bytes 786440 | tf_op jit(solution)/shard_map/ppermute | solution.py:14
  5.1 2.6 %collective-permute-start = (f32[128,512]{1,0:T(8,128)}, f32[128,512]{1,0:T(8,128)S(1)}, u32[]{:S(2)}, u32[]{:S(2)}) collective-permute-start(f32[128,512]{1,0:T(8,128)} %bitcast.128), channel_id=1, source_target_pairs={{1,0},{2,1},{3,2},{4,3},{5,4},{6,5},{7,6},{8,7},{9,8},{10,9},{11,1... | collective-permute-start | bytes 786440 | tf_op jit(solution)/shard_map/ppermute | solution.py:14
  7.8 1.1 multiply_reduce_fusion.7
  8.8 0.8 fusion.133
  9.6 0.8 fusion.132
  10.4 3.2 %multiply_reduce_fusion.6 = (f32[128]{0:T(128)S(1)}, f32[128,512]{1,0:T(8,128)S(1)}) fusion(bf16[2,2048,512]{2,1,0:T(8,128)(2,1)} %param.9, bf16[2,512,2048]{2,1,0:T(8,128)(2,1)} %param.8, f32[1,128,512]{2,1,0:T(8,128)} %param.6, f32[512]{0:T(512)S(1)} %bitcast.136, f32[128]{0:T(128)S(1)} %add_rsqrt_fusion.3, f32[512]{0:T(512)S(1)} %bitcast.129), kind=kOutput, calls=%fused_computation.92 | convolution fusion | flops 538640256 | bytes 4985856 | tf_op jit(solution)/shard_map/dot_general | solution.py:247
  13.6 3.0 %fusion.70 = f32[128,512]{1,0:T(8,128)S(1)} fusion(f32[128,512]{1,0:T(8,128)S(1)} %collective-permute-done, bf16[2,2048,512]{2,1,0:T(8,128)(2,1)} %param.9, bf16[2,512,2048]{2,1,0:T(8,128)(2,1)} %param.8, f32[128,512]{1,0:T(8,128)S(1)} %get-tuple-element.13, f32[512]{0:T(512)S(1)} %bitcast.140, f32[128]{0:T(128)S(1)} %add_rsqrt_fusion.2, f32[512]{0:T(512)S(1)} %bitcast.133), kind=kOutput, calls=%fused_computation.60 | convolution fusion | flops 538574848 | bytes 5247488 | tf_op jit(solution)/shard_map/dot_general | solution.py:247
  16.7 0.7 pad_maximum_fusion.3.packed_ref
  17.4 60.4 %shard_map.77 = f32[128,512]{1,0:T(8,128)} custom-call(f32[136,512]{1,0:T(8,128)} %pad_maximum_fusion.3.packed_ref), custom_call_target="tpu_custom_call" | custom-call | tf_op jit(solution)/shard_map/pallas_call | solution.py:218
  77.8 1.2 multiply_reduce_fusion.5
  79.0 2.2 %fusion.30 = f32[128,2048]{1,0:T(8,128)S(1)} fusion(bf16[2,512,2048]{2,1,0:T(8,128)(2,1)} %param.8, f32[128,512]{1,0:T(8,128)S(1)} %get-tuple-element.3, f32[512]{0:T(512)S(1)} %bitcast.137, f32[128]{0:T(128)S(1)} %get-tuple-element.9), kind=kOutput, calls=%fused_computation.34 | convolution fusion | flops 268632064 | bytes 3410432 | tf_op jit(solution)/shard_map/dot_general | solution.py:241
  81.3 0.6 multiply_reduce_fusion.4
  81.9 1.5 %copy-done = bf16[2,512,2048]{2,1,0:T(8,128)(2,1)S(1)} copy-done((bf16[2,512,2048]{2,1,0:T(8,128)(2,1)S(1)}, bf16[2,512,2048]{2,1,0:T(8,128)(2,1)}, u32[]{:S(2)}) %copy-start) | copy-done | bytes 4194328
  83.4 0.5 fusion.16
  83.9 3.9 %multiply_reduce_fusion.3 = (f32[128]{0:T(128)S(1)}, f32[128,512]{1,0:T(8,128)S(1)}) fusion(f32[128,512]{1,0:T(8,128)S(1)} %get-tuple-element.15, f32[512]{0:T(512)S(1)} %bitcast.142, bf16[2,512,2048]{2,1,0:T(8,128)(2,1)} %param.8, bf16[2,2048,512]{2,1,0:T(8,128)(2,1)} %param.9, f32[128,2048]{1,0:T(8,128)S(1)} %fusion.16, f32[1,128,512]{2,1,0:T(8,128)S(1)} %copy-done.1), kind=kOutput, calls=%fused_computation.86 | convolution fusion | flops 539492224 | bytes 6031872 | tf_op jit(solution)/shard_map/dot_general | solution.py:259
  87.9 3.9 %multiply_reduce_fusion.2 = (f32[128]{0:T(128)S(1)}, f32[128,512]{1,0:T(8,128)S(1)}) fusion(f32[128,512]{1,0:T(8,128)S(1)} %get-tuple-element.3, f32[512]{0:T(512)S(1)} %bitcast.138, bf16[2,512,2048]{2,1,0:T(8,128)(2,1)} %param.8, bf16[2,2048,512]{2,1,0:T(8,128)(2,1)} %param.9, f32[128,2048]{1,0:T(8,128)S(1)} %fusion.30, ...), kind=kOutput, calls=%fused_computation.84 | convolution fusion | flops 539492224 | bytes 6031872 | tf_op jit(solution)/shard_map/dot_general | solution.py:259
  91.8 1.1 subtract_subtract_fusion
  92.9 0.7 pad_maximum_fusion.2.packed_ref
  93.7 48.8 %shard_map.78 = f32[128,512]{1,0:T(8,128)} custom-call(f32[136,512]{1,0:T(8,128)} %pad_maximum_fusion.2.packed_ref), custom_call_target="tpu_custom_call" | custom-call | tf_op jit(solution)/shard_map/pallas_call | solution.py:218
  142.5 4.0 %multiply_reduce_fusion.1 = (f32[128]{0:T(128)S(1)}, f32[128,512]{1,0:T(8,128)S(1)}) fusion(f32[128,512]{1,0:T(8,128)S(1)} %get-tuple-element.15, f32[512]{0:T(512)S(1)} %bitcast.143, bf16[2,512,2048]{2,1,0:T(8,128)(2,1)} %param.8, bf16[2,2048,512]{2,1,0:T(8,128)(2,1)} %param.9, f32[128,2048]{1,0:T(8,128)S(1)} %fusion.16, f32[128,512]{1,0:T(8,128)} %shard_map.78, ...), kind=kOutput, calls=%fused_computation.82 | convolution fusion | flops 539557760 | bytes 6294016 | tf_op jit(solution)/shard_map/dot_general | solution.py:259
  146.5 0.1 multiply_subtract_fusion
  146.6 3.9 %multiply_reduce_fusion = (f32[128]{0:T(128)S(1)}, f32[128,512]{1,0:T(8,128)S(1)}) fusion(f32[128,512]{1,0:T(8,128)S(1)} %get-tuple-element.3, f32[512]{0:T(512)S(1)} %bitcast.139, bf16[2,512,2048]{2,1,0:T(8,128)(2,1)} %param.8, bf16[2,2048,512]{2,1,0:T(8,128)(2,1)} %param.9, f32[128,2048]{1,0:T(8,128)S(1)} %fusion.30, f32[128,512]{1,0:T(8,128)S(1)} %multiply_subtract_fusion), kind=kOutput, calls=%fused_computation.80 | convolution fusion | flops 539492224 | bytes 6031872 | tf_op jit(solution)/shard_map/dot_general | solution.py:259
  150.5 0.1 subtract_bitcast_fusion
  150.7 1.0 pad_maximum_fusion
  (24 shorter events, 0.3 us)
Async XLA Ops:
  0.6 91.2 %collective-permute-start.1 = (f32[128,512]{1,0:T(8,128)}, f32[128,512]{1,0:T(8,128)}, u32[]{:S(2)}, u32[]{:S(2)}) collective-permute-start(f32[128,512]{1,0:T(8,128)} %bitcast.127), channel_id=1, source_target_pairs={{0,1},{1,2},{2,3},{3,4},{4,5},{5,6},{6,7},{7,8},{8,9},{9,10},{10,1... | collective-permute-start | bytes 786440 | tf_op jit(solution)/shard_map/ppermute | solution.py:14
  5.1 8.4 %collective-permute-start = (f32[128,512]{1,0:T(8,128)}, f32[128,512]{1,0:T(8,128)S(1)}, u32[]{:S(2)}, u32[]{:S(2)}) collective-permute-start(f32[128,512]{1,0:T(8,128)} %bitcast.128), channel_id=1, source_target_pairs={{1,0},{2,1},{3,2},{4,3},{5,4},{6,5},{7,6},{8,7},{9,8},{10,9},{11,1... | collective-permute-start | bytes 786440 | tf_op jit(solution)/shard_map/ppermute | solution.py:14
  10.4 3.2 %copy-start.4 = (f32[2,512]{1,0:T(2,128)S(1)}, f32[2,512]{1,0:T(2,128)}, u32[]{:S(2)}) copy-start(f32[2,512]{1,0:T(2,128)} %param.11) | copy-start | bytes 12292
  13.6 64.2 %copy-start.2 = (f32[1,128,512]{2,1,0:T(8,128)S(1)}, f32[1,128,512]{2,1,0:T(8,128)}, u32[]{:S(2)}) copy-start(f32[1,128,512]{2,1,0:T(8,128)} %param.6) | copy-start | bytes 786436
  77.8 3.4 %copy-start.5 = (bf16[2,2048,512]{2,1,0:T(8,128)(2,1)S(1)}, bf16[2,2048,512]{2,1,0:T(8,128)(2,1)}, u32[]{:S(2)}) copy-start(bf16[2,2048,512]{2,1,0:T(8,128)(2,1)} %param.9) | copy-start | bytes 12582916
  81.2 2.2 %copy-start = (bf16[2,512,2048]{2,1,0:T(8,128)(2,1)S(1)}, bf16[2,512,2048]{2,1,0:T(8,128)(2,1)}, u32[]{:S(2)}) copy-start(bf16[2,512,2048]{2,1,0:T(8,128)(2,1)} %param.8) | copy-start | bytes 12582916
  81.3 2.7 %copy-start.1 = (f32[1,128,512]{2,1,0:T(8,128)S(1)}, f32[1,128,512]{2,1,0:T(8,128)}, u32[]{:S(2)}) copy-start(f32[1,128,512]{2,1,0:T(8,128)} %param.7) | copy-start | bytes 786436
  142.5 4.0 %copy-start.3 = (f32[128,512]{1,0:T(8,128)S(1)}, f32[128,512]{1,0:T(8,128)}, u32[]{:S(2)}) copy-start(f32[128,512]{1,0:T(8,128)} %shard_map.78) | copy-start | bytes 786436

commit v10 on v9

--- a/solution.py
+++ b/solution.py
@@ -28,7 +28,11 @@
     return out
 
 
-def group_kernel(size, reverse, pieces, packed_ref, out_ref, got, state, q_got, q_state, gathered, final, pair, sends, recvs):
+def group_kernel(size, reverse, pieces, carry, *refs):
+    if carry:
+        packed_ref, carry_ref, out_ref, carry_out, got, state, q_got, q_state, gathered, final, pair, held_carry, sends, recvs = refs
+    else:
+        packed_ref, out_ref, got, state, q_got, q_state, gathered, final, pair, sends, recvs = refs
     position = lax.axis_index("depth")
     order = size - 1 - position if reverse else position
     core, chip = (order % 2, order // 2)
@@ -124,6 +128,8 @@
 
     sides = [copy(state.at[2], final.at[k], slot_f, k, order + 1 + k) for k in range(3)]
     sides.append(copy(mine_ref, pair, slot_f, 3, partner))
+    if carry:
+        sides.append(copy(carry_ref, held_carry, slot_f, 4, order + 1))
 
     def scatter(start):
         for k in range(4):
@@ -197,6 +203,8 @@
         element_scale = jnp.where(left_side, pair[factor_row, :], got[0, factor_row, :])
         cols = pl.ds(pl.multiple_of(owner_core * half, half), half)
         out_ref[band, cols] = jnp.where(first, behind, element + element_scale * behind)
+    if carry:
+        carry_out[...] = held_carry[...]
     for handle in started:
         handle.wait_send()
 
@@ -205,7 +213,7 @@
         scatter(False)
 
 
-def kernel_scan(factor, offset, reverse, ident):
+def kernel_scan(factor, offset, reverse, ident, carried=None):
     size = lax.axis_size("depth")
     rows, width = offset.shape
     half = width // 2
@@ -215,11 +223,15 @@
     links = sum(step - 1 for step in radices(groups))
     levels = len(radices(groups))
     quarter = rows // 4
+    carry = carried is not None
+    result = jax.ShapeDtypeStruct((rows, width), jnp.float32)
+    place = pl.BlockSpec(memory_space=pltpu.VMEM)
+    extra = [pltpu.VMEM((rows, width), jnp.float32)] if carry else []
     return pl.pallas_call(
-        functools.partial(group_kernel, size, reverse, 4),
-        out_shape=jax.ShapeDtypeStruct((rows, width), jnp.float32),
-        in_specs=[pl.BlockSpec(memory_space=pltpu.VMEM)],
-        out_specs=pl.BlockSpec(memory_space=pltpu.VMEM),
+        functools.partial(group_kernel, size, reverse, 4, carry),
+        out_shape=(result, result) if carry else result,
+        in_specs=[place, place] if carry else [place],
+        out_specs=(place, place) if carry else place,
         scratch_shapes=[
             pltpu.VMEM((3, rows + 8, half), jnp.float32),
             pltpu.VMEM((3, rows + 8, half), jnp.float32),
@@ -228,11 +240,14 @@
             pltpu.VMEM((7, quarter, half), jnp.float32),
             pltpu.VMEM((3, rows + 8, half), jnp.float32),
             pltpu.VMEM((rows + 8, half), jnp.float32),
+        ]
+        + extra
+        + [
             pltpu.SemaphoreType.DMA((6 + levels, 8)),
             pltpu.SemaphoreType.DMA((6 + levels, 8)),
         ],
         compiler_params=pltpu.CompilerParams(collective_id=ident, has_side_effects=True),
-    )(packed)
+    )(*((packed, carried) if carry else (packed,)))
 
 
 def prepare_block(state, w_first, gain_row):
@@ -306,9 +321,8 @@
     guess_state = state_guess[0]
     guess_adjoint = adjoint_guess[0]
     next_guess = shifted(guess_state, "depth", -1)
-    prev_guess = shifted(guess_adjoint, "depth", 1)
     end_state, _, _, _ = relax_forward(guess_state, w_in, w_out, norm_gain, decay, True)
-    correction = kernel_scan(factor, end_state - next_guess, False, 0)
+    correction, prev_guess = kernel_scan(factor, end_state - next_guess, False, 0, guess_adjoint)
     start = guess_state + correction
     _, states, inverses, preacts = relax_forward(start, w_in, w_out, norm_gain, decay, False)
     first_adjoint, _ = relax_backward(

time: 153 us -> 154 us (level)
  starting transfers between devices: 7.12 us -> 5.15 us
    ppermute x2 -> x1, starting transfers between devices: 7.12 us -> 5.15 us  [shifted(): return lax.ppermute(block, axis, route)]
  transfers between devices with their start and end apart: 2 -> 1, of which waited for: 0 -> 0; matrix products, arithmetic and copies ran while one was open for 14% -> 4% of each run, Pallas kernels for 40% -> 0%
where the time goes in v10:
time: 154 us; the launch traced here: 152 us
  Pallas kernels  110 us (71%)
  matrix products  25.7 us (17%)
  other arithmetic  6.34 us (4%)
  starting transfers between devices  5.15 us (3%)
  local copies, waits for them, and re-layouts  3.15 us (2%)
    pallas_call x2, Pallas kernels, kernel_scan(): pl.pallas_call(functools.partial(group_kernel, size, reverse, 4, carry),...  110 us
    dot_general x4, matrix products, backward_block(): lax.dot_general(grad_pre, w_first, (((1,), (1,)), ((), ())), preferred_el...  16.3 us
    dot_general x3, matrix products, finish_block(): jnp.dot(hidden, w_second, preferred_element_type=jnp.float32)  6.8 us
    ppermute x1, starting transfers between devices, shifted(): return lax.ppermute(block, axis, route)  5.15 us
  transfers between devices with their start and end apart: 1, of which 0 were waited for; matrix products, arithmetic and copies ran while one was open for 4% of the time, Pallas kernels for 0%

profile of v10, /device:TPU:1, one launch (start us, length us, event | category | flops | bytes accessed | tf_op | source)
XLA Modules:
  0.0 151.5 jit_solution(8924214168564750862)
XLA Ops:
  0.6 5.2 %collective-permute-start = (f32[128,512]{1,0:T(8,128)}, f32[128,512]{1,0:T(8,128)S(1)}, u32[]{:S(2)}, u32[]{:S(2)}) collective-permute-start(f32[128,512]{1,0:T(8,128)} %bitcast.128), channel_id=1, source_target_pairs={{1,0},{2,1},{3,2},{4,3},{5,4},{6,5},{7,6},{8,7},{9,8},{10,9},{11,1... | collective-permute-start | bytes 786440 | tf_op jit(solution)/shard_map/ppermute | solution.py:14
  5.8 1.1 multiply_reduce_fusion.7
  6.9 0.8 fusion.133
  7.6 0.8 fusion.132
  8.4 3.2 %multiply_reduce_fusion.6 = (f32[128]{0:T(128)S(1)}, f32[128,512]{1,0:T(8,128)S(1)}) fusion(bf16[2,2048,512]{2,1,0:T(8,128)(2,1)} %param.9, bf16[2,512,2048]{2,1,0:T(8,128)(2,1)} %param.8, f32[1,128,512]{2,1,0:T(8,128)} %param.6, f32[512]{0:T(512)S(1)} %bitcast.136, f32[128]{0:T(128)S(1)} %add_rsqrt_fusion.3, f32[512]{0:T(512)S(1)} %bitcast.129), kind=kOutput, calls=%fused_computation.92 | convolution fusion | flops 538640256 | bytes 4985856 | tf_op jit(solution)/shard_map/dot_general | solution.py:262
  11.6 3.0 %fusion.70 = f32[128,512]{1,0:T(8,128)S(1)} fusion(f32[128,512]{1,0:T(8,128)S(1)} %collective-permute-done, bf16[2,2048,512]{2,1,0:T(8,128)(2,1)} %param.9, bf16[2,512,2048]{2,1,0:T(8,128)(2,1)} %param.8, f32[128,512]{1,0:T(8,128)S(1)} %get-tuple-element.17, f32[512]{0:T(512)S(1)} %bitcast.140, f32[128]{0:T(128)S(1)} %add_rsqrt_fusion.2, f32[512]{0:T(512)S(1)} %bitcast.133), kind=kOutput, calls=%fused_computation.60 | convolution fusion | flops 538574848 | bytes 5247488 | tf_op jit(solution)/shard_map/dot_general | solution.py:262
  14.7 0.7 pad_maximum_fusion.3.refs_0_
  15.4 61.2 %shard_map.77 = (f32[128,512]{1,0:T(8,128)}, f32[128,512]{1,0:T(8,128)}) custom-call(f32[136,512]{1,0:T(8,128)} %pad_maximum_fusion.3.refs_0_, f32[128,512]{1,0:T(8,128)} %bitcast.126), custom_call_target="tpu_custom_call" | custom-call | tf_op jit(solution)/shard_map/pallas_call | solution.py:230
  76.6 1.2 multiply_reduce_fusion.5
  77.9 2.2 %fusion.30 = f32[128,2048]{1,0:T(8,128)S(1)} fusion(bf16[2,512,2048]{2,1,0:T(8,128)(2,1)} %param.8, f32[128,512]{1,0:T(8,128)S(1)} %get-tuple-element.7, f32[512]{0:T(512)S(1)} %bitcast.137, f32[128]{0:T(128)S(1)} %get-tuple-element.13), kind=kOutput, calls=%fused_computation.34 | convolution fusion | flops 268632064 | bytes 3410432 | tf_op jit(solution)/shard_map/dot_general | solution.py:256
  80.1 0.6 multiply_reduce_fusion.4
  80.7 1.6 %copy-done = bf16[2,512,2048]{2,1,0:T(8,128)(2,1)S(1)} copy-done((bf16[2,512,2048]{2,1,0:T(8,128)(2,1)S(1)}, bf16[2,512,2048]{2,1,0:T(8,128)(2,1)}, u32[]{:S(2)}) %copy-start) | copy-done | bytes 4194328
  82.2 0.5 fusion.16
  82.7 3.9 %multiply_reduce_fusion.3 = (f32[128]{0:T(128)S(1)}, f32[128,512]{1,0:T(8,128)S(1)}) fusion(f32[128,512]{1,0:T(8,128)S(1)} %get-tuple-element.19, f32[512]{0:T(512)S(1)} %bitcast.142, bf16[2,512,2048]{2,1,0:T(8,128)(2,1)} %param.8, bf16[2,2048,512]{2,1,0:T(8,128)(2,1)} %param.9, f32[128,2048]{1,0:T(8,128)S(1)} %fusion.16, f32[1,128,512]{2,1,0:T(8,128)S(1)} %copy-done.1), kind=kOutput, calls=%fused_computation.86 | convolution fusion | flops 539492224 | bytes 6031872 | tf_op jit(solution)/shard_map/dot_general | solution.py:274
  86.6 0.1 multiply_subtract_fusion.1
  86.8 4.5 %multiply_reduce_fusion.2 = (f32[128]{0:T(128)S(1)}, f32[128,512]{1,0:T(8,128)}) fusion(f32[128,512]{1,0:T(8,128)S(1)} %get-tuple-element.7, f32[512]{0:T(512)S(1)} %bitcast.138, bf16[2,512,2048]{2,1,0:T(8,128)(2,1)} %param.8, bf16[2,2048,512]{2,1,0:T(8,128)(2,1)} %param.9, f32[128,2048]{1,0:T(8,128)S(1)} %fusion.30, f32[128,512]{1,0:T(8,128)S(1)} %multiply_subtract_fusion.1), kind=kOutput, calls=%fused_computation.84 | convolution fusion | flops 539492224 | bytes 6031872 | tf_op jit(solution)/shard_map/dot_general | solution.py:274
  91.3 1.1 subtract_subtract_fusion
  92.4 0.7 pad_maximum_fusion.2.refs_0_
  93.1 49.1 %shard_map.78 = f32[128,512]{1,0:T(8,128)} custom-call(f32[136,512]{1,0:T(8,128)} %pad_maximum_fusion.2.refs_0_), custom_call_target="tpu_custom_call" | custom-call | tf_op jit(solution)/shard_map/pallas_call | solution.py:230
  142.3 4.0 %multiply_reduce_fusion.1 = (f32[128]{0:T(128)S(1)}, f32[128,512]{1,0:T(8,128)S(1)}) fusion(f32[128,512]{1,0:T(8,128)S(1)} %get-tuple-element.19, f32[512]{0:T(512)S(1)} %bitcast.143, bf16[2,512,2048]{2,1,0:T(8,128)(2,1)} %param.8, bf16[2,2048,512]{2,1,0:T(8,128)(2,1)} %param.9, f32[128,2048]{1,0:T(8,128)S(1)} %fusion.16, f32[128,512]{1,0:T(8,128)} %shard_map.78, ...), kind=kOutput, calls=%fused_computation.82 | convolution fusion | flops 539557760 | bytes 6294016 | tf_op jit(solution)/shard_map/dot_general | solution.py:274
  146.3 0.1 multiply_subtract_fusion
  146.5 3.9 %multiply_reduce_fusion = (f32[128]{0:T(128)S(1)}, f32[128,512]{1,0:T(8,128)S(1)}) fusion(f32[128,512]{1,0:T(8,128)S(1)} %get-tuple-element.7, f32[512]{0:T(512)S(1)} %bitcast.139, bf16[2,512,2048]{2,1,0:T(8,128)(2,1)} %param.8, bf16[2,2048,512]{2,1,0:T(8,128)(2,1)} %param.9, f32[128,2048]{1,0:T(8,128)S(1)} %fusion.30, f32[128,512]{1,0:T(8,128)S(1)} %multiply_subtract_fusion), kind=kOutput, calls=%fused_computation.80 | convolution fusion | flops 539492224 | bytes 6031872 | tf_op jit(solution)/shard_map/dot_general | solution.py:274
  150.3 0.1 subtract_bitcast_fusion
  150.5 1.0 pad_maximum_fusion
  (24 shorter events, 0.1 us)
Async XLA Ops:
  0.6 11.0 %collective-permute-start = (f32[128,512]{1,0:T(8,128)}, f32[128,512]{1,0:T(8,128)S(1)}, u32[]{:S(2)}, u32[]{:S(2)}) collective-permute-start(f32[128,512]{1,0:T(8,128)} %bitcast.128), channel_id=1, source_target_pairs={{1,0},{2,1},{3,2},{4,3},{5,4},{6,5},{7,6},{8,7},{9,8},{10,9},{11,1... | collective-permute-start | bytes 786440 | tf_op jit(solution)/shard_map/ppermute | solution.py:14
  8.4 3.2 %copy-start.5 = (f32[2,512]{1,0:T(2,128)S(1)}, f32[2,512]{1,0:T(2,128)}, u32[]{:S(2)}) copy-start(f32[2,512]{1,0:T(2,128)} %param.11) | copy-start | bytes 12292
  11.6 65.0 %copy-start.2 = (f32[1,128,512]{2,1,0:T(8,128)S(1)}, f32[1,128,512]{2,1,0:T(8,128)}, u32[]{:S(2)}) copy-start(f32[1,128,512]{2,1,0:T(8,128)} %param.6) | copy-start | bytes 786436
  76.6 3.4 %copy-start.6 = (bf16[2,2048,512]{2,1,0:T(8,128)(2,1)S(1)}, bf16[2,2048,512]{2,1,0:T(8,128)(2,1)}, u32[]{:S(2)}) copy-start(bf16[2,2048,512]{2,1,0:T(8,128)(2,1)} %param.9) | copy-start | bytes 12582916
  80.1 2.2 %copy-start = (bf16[2,512,2048]{2,1,0:T(8,128)(2,1)S(1)}, bf16[2,512,2048]{2,1,0:T(8,128)(2,1)}, u32[]{:S(2)}) copy-start(bf16[2,512,2048]{2,1,0:T(8,128)(2,1)} %param.8) | copy-start | bytes 12582916
  80.1 2.7 %copy-start.1 = (f32[1,128,512]{2,1,0:T(8,128)S(1)}, f32[1,128,512]{2,1,0:T(8,128)}, u32[]{:S(2)}) copy-start(f32[1,128,512]{2,1,0:T(8,128)} %param.7) | copy-start | bytes 786436
  86.8 4.6 %copy-start.4 = (f32[128,512]{1,0:T(8,128)S(1)}, f32[128,512]{1,0:T(8,128)}, u32[]{:S(2)}) copy-start(f32[128,512]{1,0:T(8,128)} %get-tuple-element.5) | copy-start | bytes 786436
  142.3 4.0 %copy-start.3 = (f32[128,512]{1,0:T(8,128)S(1)}, f32[128,512]{1,0:T(8,128)}, u32[]{:S(2)}) copy-start(f32[128,512]{1,0:T(8,128)} %shard_map.78) | copy-start | bytes 786436

commit v11 on v9

--- a/solution.py
+++ b/solution.py
@@ -216,7 +216,7 @@
     levels = len(radices(groups))
     quarter = rows // 4
     return pl.pallas_call(
-        functools.partial(group_kernel, size, reverse, 4),
+        functools.partial(group_kernel, size, reverse, 2),
         out_shape=jax.ShapeDtypeStruct((rows, width), jnp.float32),
         in_specs=[pl.BlockSpec(memory_space=pltpu.VMEM)],
         out_specs=pl.BlockSpec(memory_space=pltpu.VMEM),

time: 153 us -> 155 us (1.013)
  Pallas kernels: 109 us -> 112 us
    pallas_call x2, Pallas kernels: 109 us -> 112 us  [kernel_scan(): pl.pallas_call(functools.partial(group_kernel, size, reverse, 2), out_sha...]
  transfers between devices with their start and end apart: 2 -> 2, of which waited for: 0 -> 0; matrix products, arithmetic and copies ran while one was open for 14% -> 14% of each run, Pallas kernels for 40% -> 38%
where the time goes in v11:
time: 155 us; the launch traced here: 154 us
  Pallas kernels  112 us (72%)
  matrix products  25.1 us (16%)
  starting transfers between devices  7.12 us (5%)
  other arithmetic  6.33 us (4%)
  local copies, waits for them, and re-layouts  3.1 us (2%)
    pallas_call x2, Pallas kernels, kernel_scan(): pl.pallas_call(functools.partial(group_kernel, size, reverse, 2), out_sha...  112 us
    dot_general x4, matrix products, backward_block(): lax.dot_general(grad_pre, w_first, (((1,), (1,)), ((), ())), preferred_el...  15.6 us
    ppermute x2, starting transfers between devices, shifted(): return lax.ppermute(block, axis, route)  7.12 us
    dot_general x3, matrix products, finish_block(): jnp.dot(hidden, w_second, preferred_element_type=jnp.float32)  6.85 us
  transfers between devices with their start and end apart: 2, of which 0 were waited for; matrix products, arithmetic and copies ran while one was open for 14% of the time, Pallas kernels for 38%

profile of v11, /device:TPU:1, one launch (start us, length us, event | category | flops | bytes accessed | tf_op | source)
XLA Modules:
  0.0 154.2 jit_solution(2042114074857136795)
XLA Ops:
  0.6 4.5 %collective-permute-start.1 = (f32[128,512]{1,0:T(8,128)}, f32[128,512]{1,0:T(8,128)}, u32[]{:S(2)}, u32[]{:S(2)}) collective-permute-start(f32[128,512]{1,0:T(8,128)} %bitcast.127), channel_id=1, source_target_pairs={{0,1},{1,2},{2,3},{3,4},{4,5},{5,6},{6,7},{7,8},{8,9},{9,10},{10,1... | collective-permute-start | bytes 786440 | tf_op jit(solution)/shard_map/ppermute | solution.py:14
  5.1 2.6 %collective-permute-start = (f32[128,512]{1,0:T(8,128)}, f32[128,512]{1,0:T(8,128)S(1)}, u32[]{:S(2)}, u32[]{:S(2)}) collective-permute-start(f32[128,512]{1,0:T(8,128)} %bitcast.128), channel_id=1, source_target_pairs={{1,0},{2,1},{3,2},{4,3},{5,4},{6,5},{7,6},{8,7},{9,8},{10,9},{11,1... | collective-permute-start | bytes 786440 | tf_op jit(solution)/shard_map/ppermute | solution.py:14
  7.8 1.1 multiply_reduce_fusion.7
  8.8 0.8 fusion.133
  9.6 0.8 fusion.132
  10.4 3.2 %multiply_reduce_fusion.6 = (f32[128]{0:T(128)S(1)}, f32[128,512]{1,0:T(8,128)S(1)}) fusion(bf16[2,2048,512]{2,1,0:T(8,128)(2,1)} %param.9, bf16[2,512,2048]{2,1,0:T(8,128)(2,1)} %param.8, f32[1,128,512]{2,1,0:T(8,128)} %param.6, f32[512]{0:T(512)S(1)} %bitcast.136, f32[128]{0:T(128)S(1)} %add_rsqrt_fusion.3, f32[512]{0:T(512)S(1)} %bitcast.129), kind=kOutput, calls=%fused_computation.92 | convolution fusion | flops 538640256 | bytes 4985856 | tf_op jit(solution)/shard_map/dot_general | solution.py:247
  13.6 3.0 %fusion.70 = f32[128,512]{1,0:T(8,128)S(1)} fusion(f32[128,512]{1,0:T(8,128)S(1)} %collective-permute-done, bf16[2,2048,512]{2,1,0:T(8,128)(2,1)} %param.9, bf16[2,512,2048]{2,1,0:T(8,128)(2,1)} %param.8, f32[128,512]{1,0:T(8,128)S(1)} %get-tuple-element.13, f32[512]{0:T(512)S(1)} %bitcast.140, f32[128]{0:T(128)S(1)} %add_rsqrt_fusion.2, f32[512]{0:T(512)S(1)} %bitcast.133), kind=kOutput, calls=%fused_computation.60 | convolution fusion | flops 538574848 | bytes 5247488 | tf_op jit(solution)/shard_map/dot_general | solution.py:247
  16.7 0.7 pad_maximum_fusion.3.packed_ref
  17.4 58.5 %shard_map.77 = f32[128,512]{1,0:T(8,128)} custom-call(f32[136,512]{1,0:T(8,128)} %pad_maximum_fusion.3.packed_ref), custom_call_target="tpu_custom_call" | custom-call | tf_op jit(solution)/shard_map/pallas_call | solution.py:218
  75.9 1.2 multiply_reduce_fusion.5
  77.1 2.2 %fusion.30 = f32[128,2048]{1,0:T(8,128)S(1)} fusion(bf16[2,512,2048]{2,1,0:T(8,128)(2,1)} %param.8, f32[128,512]{1,0:T(8,128)S(1)} %get-tuple-element.3, f32[512]{0:T(512)S(1)} %bitcast.137, f32[128]{0:T(128)S(1)} %get-tuple-element.9), kind=kOutput, calls=%fused_computation.34 | convolution fusion | flops 268632064 | bytes 3410432 | tf_op jit(solution)/shard_map/dot_general | solution.py:241
  79.4 0.6 multiply_reduce_fusion.4
  80.0 1.5 copy-done
  81.5 0.5 fusion.16
  82.0 3.9 %multiply_reduce_fusion.3 = (f32[128]{0:T(128)S(1)}, f32[128,512]{1,0:T(8,128)S(1)}) fusion(f32[128,512]{1,0:T(8,128)S(1)} %get-tuple-element.15, f32[512]{0:T(512)S(1)} %bitcast.142, bf16[2,512,2048]{2,1,0:T(8,128)(2,1)} %param.8, bf16[2,2048,512]{2,1,0:T(8,128)(2,1)} %param.9, f32[128,2048]{1,0:T(8,128)S(1)} %fusion.16, f32[1,128,512]{2,1,0:T(8,128)S(1)} %copy-done.1), kind=kOutput, calls=%fused_computation.86 | convolution fusion | flops 539492224 | bytes 6031872 | tf_op jit(solution)/shard_map/dot_general | solution.py:259
  86.0 3.9 %multiply_reduce_fusion.2 = (f32[128]{0:T(128)S(1)}, f32[128,512]{1,0:T(8,128)S(1)}) fusion(f32[128,512]{1,0:T(8,128)S(1)} %get-tuple-element.3, f32[512]{0:T(512)S(1)} %bitcast.138, bf16[2,512,2048]{2,1,0:T(8,128)(2,1)} %param.8, bf16[2,2048,512]{2,1,0:T(8,128)(2,1)} %param.9, f32[128,2048]{1,0:T(8,128)S(1)} %fusion.30, ...), kind=kOutput, calls=%fused_computation.84 | convolution fusion | flops 539492224 | bytes 6031872 | tf_op jit(solution)/shard_map/dot_general | solution.py:259
  89.9 1.1 subtract_subtract_fusion
  91.0 0.7 pad_maximum_fusion.2.packed_ref
  91.8 53.3 %shard_map.78 = f32[128,512]{1,0:T(8,128)} custom-call(f32[136,512]{1,0:T(8,128)} %pad_maximum_fusion.2.packed_ref), custom_call_target="tpu_custom_call" | custom-call | tf_op jit(solution)/shard_map/pallas_call | solution.py:218
  145.0 4.0 %multiply_reduce_fusion.1 = (f32[128]{0:T(128)S(1)}, f32[128,512]{1,0:T(8,128)S(1)}) fusion(f32[128,512]{1,0:T(8,128)S(1)} %get-tuple-element.15, f32[512]{0:T(512)S(1)} %bitcast.143, bf16[2,512,2048]{2,1,0:T(8,128)(2,1)} %param.8, bf16[2,2048,512]{2,1,0:T(8,128)(2,1)} %param.9, f32[128,2048]{1,0:T(8,128)S(1)} %fusion.16, f32[128,512]{1,0:T(8,128)} %shard_map.78, ...), kind=kOutput, calls=%fused_computation.82 | convolution fusion | flops 539557760 | bytes 6294016 | tf_op jit(solution)/shard_map/dot_general | solution.py:259
  149.0 0.1 multiply_subtract_fusion
  149.2 3.9 %multiply_reduce_fusion = (f32[128]{0:T(128)S(1)}, f32[128,512]{1,0:T(8,128)S(1)}) fusion(f32[128,512]{1,0:T(8,128)S(1)} %get-tuple-element.3, f32[512]{0:T(512)S(1)} %bitcast.139, bf16[2,512,2048]{2,1,0:T(8,128)(2,1)} %param.8, bf16[2,2048,512]{2,1,0:T(8,128)(2,1)} %param.9, f32[128,2048]{1,0:T(8,128)S(1)} %fusion.30, f32[128,512]{1,0:T(8,128)S(1)} %multiply_subtract_fusion), kind=kOutput, calls=%fused_computation.80 | convolution fusion | flops 539492224 | bytes 6031872 | tf_op jit(solution)/shard_map/dot_general | solution.py:259
  153.1 0.1 subtract_bitcast_fusion
  153.2 1.0 pad_maximum_fusion
  (24 shorter events, 0.3 us)
Async XLA Ops:
  0.6 89.3 %collective-permute-start.1 = (f32[128,512]{1,0:T(8,128)}, f32[128,512]{1,0:T(8,128)}, u32[]{:S(2)}, u32[]{:S(2)}) collective-permute-start(f32[128,512]{1,0:T(8,128)} %bitcast.127), channel_id=1, source_target_pairs={{0,1},{1,2},{2,3},{3,4},{4,5},{5,6},{6,7},{7,8},{8,9},{9,10},{10,1... | collective-permute-start | bytes 786440 | tf_op jit(solution)/shard_map/ppermute | solution.py:14
  5.1 8.4 %collective-permute-start = (f32[128,512]{1,0:T(8,128)}, f32[128,512]{1,0:T(8,128)S(1)}, u32[]{:S(2)}, u32[]{:S(2)}) collective-permute-start(f32[128,512]{1,0:T(8,128)} %bitcast.128), channel_id=1, source_target_pairs={{1,0},{2,1},{3,2},{4,3},{5,4},{6,5},{7,6},{8,7},{9,8},{10,9},{11,1... | collective-permute-start | bytes 786440 | tf_op jit(solution)/shard_map/ppermute | solution.py:14
  10.4 3.2 %copy-start.4 = (f32[2,512]{1,0:T(2,128)S(1)}, f32[2,512]{1,0:T(2,128)}, u32[]{:S(2)}) copy-start(f32[2,512]{1,0:T(2,128)} %param.11) | copy-start | bytes 12292
  13.6 62.3 %copy-start.2 = (f32[1,128,512]{2,1,0:T(8,128)S(1)}, f32[1,128,512]{2,1,0:T(8,128)}, u32[]{:S(2)}) copy-start(f32[1,128,512]{2,1,0:T(8,128)} %param.6) | copy-start | bytes 786436
  75.9 3.4 %copy-start.5 = (bf16[2,2048,512]{2,1,0:T(8,128)(2,1)S(1)}, bf16[2,2048,512]{2,1,0:T(8,128)(2,1)}, u32[]{:S(2)}) copy-start(bf16[2,2048,512]{2,1,0:T(8,128)(2,1)} %param.9) | copy-start | bytes 12582916
  79.3 2.2 %copy-start = (bf16[2,512,2048]{2,1,0:T(8,128)(2,1)S(1)}, bf16[2,512,2048]{2,1,0:T(8,128)(2,1)}, u32[]{:S(2)}) copy-start(bf16[2,512,2048]{2,1,0:T(8,128)(2,1)} %param.8) | copy-start | bytes 12582916
  79.3 2.7 %copy-start.1 = (f32[1,128,512]{2,1,0:T(8,128)S(1)}, f32[1,128,512]{2,1,0:T(8,128)}, u32[]{:S(2)}) copy-start(f32[1,128,512]{2,1,0:T(8,128)} %param.7) | copy-start | bytes 786436
  145.0 4.0 %copy-start.3 = (f32[128,512]{1,0:T(8,128)S(1)}, f32[128,512]{1,0:T(8,128)}, u32[]{:S(2)}) copy-start(f32[128,512]{1,0:T(8,128)} %shard_map.78) | copy-start | bytes 786436

commit v12 on v9

--- a/solution.py
+++ b/solution.py
@@ -180,23 +180,31 @@
     for handle in sides + spread_copies:
         handle.wait_recv()
     at_start = ring == 0
-    for t in range(8):
-        owner = (index - t + 8) % 8
-        owner_ring, owner_core = (owner // 2, owner % 2)
-        band = pl.ds(pl.multiple_of(owner_ring * quarter, quarter), quarter)
-        piece = q_state[depth, :quarter, :] if t == 0 else gathered[t - 1]
-        left_side = owner_core == 0
-        low = jnp.where(first, final[1, band, :], final[2, band, :])
-        low_scale = jnp.where(first, final[1, factor_row, :], final[2, factor_row, :])
-        high = jnp.where(first, final[0, band, :], final[1, band, :])
-        high_scale = jnp.where(first, final[0, factor_row, :], final[1, factor_row, :])
-        before = jnp.where(left_side, low, high)
-        before_scale = jnp.where(left_side, low_scale, high_scale)
-        behind = jnp.where(at_start, piece, before + before_scale * piece)
-        element = jnp.where(left_side, pair[band, :], got[0, band, :])
-        element_scale = jnp.where(left_side, pair[factor_row, :], got[0, factor_row, :])
-        cols = pl.ds(pl.multiple_of(owner_core * half, half), half)
-        out_ref[band, cols] = jnp.where(first, behind, element + element_scale * behind)
+
+    def finish(side):
+        low, high = ((final.at[1], final.at[0]) if side == 0 else (final.at[2], final.at[1]))
+        for t in range(8):
+            owner = (index - t + 8) % 8
+            owner_core = (side - t) % 2
+            band = pl.ds(pl.multiple_of((owner // 2) * quarter, quarter), quarter)
+            piece = q_state[depth, :quarter, :] if t == 0 else gathered[t - 1]
+            before = low if owner_core == 0 else high
+            behind = jnp.where(at_start, piece, before[band, :] + before[factor_row, :] * piece)
+            cols = slice(owner_core * half, (owner_core + 1) * half)
+            if side == 0:
+                out_ref[band, cols] = behind
+            else:
+                element = pair if owner_core == 0 else got.at[0]
+                out_ref[band, cols] = element[band, :] + element[factor_row, :] * behind
+
+    @pl.when(first)
+    def _():
+        finish(0)
+
+    @pl.when(jnp.logical_not(first))
+    def _():
+        finish(1)
+
     for handle in started:
         handle.wait_send()
 

time: 153 us -> 153 us (level)
  transfers between devices with their start and end apart: 2 -> 2, of which waited for: 0 -> 0; matrix products, arithmetic and copies ran while one was open for 14% -> 15% of each run, Pallas kernels for 40% -> 40%
where the time goes in v12:
time: 153 us; the launch traced here: 151 us
  Pallas kernels  109 us (71%)
  matrix products  25.1 us (16%)
  starting transfers between devices  7.12 us (5%)
  other arithmetic  6.33 us (4%)
  local copies, waits for them, and re-layouts  3.09 us (2%)
    pallas_call x2, Pallas kernels, kernel_scan(): pl.pallas_call(functools.partial(group_kernel, size, reverse, 4), out_sha...  109 us
    dot_general x4, matrix products, backward_block(): lax.dot_general(grad_pre, w_first, (((1,), (1,)), ((), ())), preferred_el...  15.6 us
    ppermute x2, starting transfers between devices, shifted(): return lax.ppermute(block, axis, route)  7.12 us
    dot_general x3, matrix products, finish_block(): jnp.dot(hidden, w_second, preferred_element_type=jnp.float32)  6.85 us
  transfers between devices with their start and end apart: 2, of which 0 were waited for; matrix products, arithmetic and copies ran while one was open for 15% of the time, Pallas kernels for 40%

profile of v12, /device:TPU:1, one launch (start us, length us, event | category | flops | bytes accessed | tf_op | source)
XLA Modules:
  0.0 151.5 jit_solution(4912337795978233661)
XLA Ops:
  0.6 4.5 %collective-permute-start.1 = (f32[128,512]{1,0:T(8,128)}, f32[128,512]{1,0:T(8,128)}, u32[]{:S(2)}, u32[]{:S(2)}) collective-permute-start(f32[128,512]{1,0:T(8,128)} %bitcast.127), channel_id=1, source_target_pairs={{0,1},{1,2},{2,3},{3,4},{4,5},{5,6},{6,7},{7,8},{8,9},{9,10},{10,1... | collective-permute-start | bytes 786440 | tf_op jit(solution)/shard_map/ppermute | solution.py:14
  5.1 2.6 %collective-permute-start = (f32[128,512]{1,0:T(8,128)}, f32[128,512]{1,0:T(8,128)S(1)}, u32[]{:S(2)}, u32[]{:S(2)}) collective-permute-start(f32[128,512]{1,0:T(8,128)} %bitcast.128), channel_id=1, source_target_pairs={{1,0},{2,1},{3,2},{4,3},{5,4},{6,5},{7,6},{8,7},{9,8},{10,9},{11,1... | collective-permute-start | bytes 786440 | tf_op jit(solution)/shard_map/ppermute | solution.py:14
  7.8 1.1 multiply_reduce_fusion.7
  8.8 0.8 fusion.133
  9.6 0.8 fusion.132
  10.4 3.2 %multiply_reduce_fusion.6 = (f32[128]{0:T(128)S(1)}, f32[128,512]{1,0:T(8,128)S(1)}) fusion(bf16[2,2048,512]{2,1,0:T(8,128)(2,1)} %param.9, bf16[2,512,2048]{2,1,0:T(8,128)(2,1)} %param.8, f32[1,128,512]{2,1,0:T(8,128)} %param.6, f32[512]{0:T(512)S(1)} %bitcast.136, f32[128]{0:T(128)S(1)} %add_rsqrt_fusion.3, f32[512]{0:T(512)S(1)} %bitcast.129), kind=kOutput, calls=%fused_computation.92 | convolution fusion | flops 538640256 | bytes 4985856 | tf_op jit(solution)/shard_map/dot_general | solution.py:255
  13.6 3.0 %fusion.70 = f32[128,512]{1,0:T(8,128)S(1)} fusion(f32[128,512]{1,0:T(8,128)S(1)} %collective-permute-done, bf16[2,2048,512]{2,1,0:T(8,128)(2,1)} %param.9, bf16[2,512,2048]{2,1,0:T(8,128)(2,1)} %param.8, f32[128,512]{1,0:T(8,128)S(1)} %get-tuple-element.13, f32[512]{0:T(512)S(1)} %bitcast.140, f32[128]{0:T(128)S(1)} %add_rsqrt_fusion.2, f32[512]{0:T(512)S(1)} %bitcast.133), kind=kOutput, calls=%fused_computation.60 | convolution fusion | flops 538574848 | bytes 5247488 | tf_op jit(solution)/shard_map/dot_general | solution.py:255
  16.7 0.7 pad_maximum_fusion.3.packed_ref
  17.4 60.3 %shard_map.77 = f32[128,512]{1,0:T(8,128)} custom-call(f32[136,512]{1,0:T(8,128)} %pad_maximum_fusion.3.packed_ref), custom_call_target="tpu_custom_call" | custom-call | tf_op jit(solution)/shard_map/pallas_call | solution.py:226
  77.7 1.2 multiply_reduce_fusion.5
  79.0 2.2 %fusion.30 = f32[128,2048]{1,0:T(8,128)S(1)} fusion(bf16[2,512,2048]{2,1,0:T(8,128)(2,1)} %param.8, f32[128,512]{1,0:T(8,128)S(1)} %get-tuple-element.3, f32[512]{0:T(512)S(1)} %bitcast.137, f32[128]{0:T(128)S(1)} %get-tuple-element.9), kind=kOutput, calls=%fused_computation.34 | convolution fusion | flops 268632064 | bytes 3410432 | tf_op jit(solution)/shard_map/dot_general | solution.py:249
  81.2 0.6 multiply_reduce_fusion.4
  81.9 1.5 %copy-done = bf16[2,512,2048]{2,1,0:T(8,128)(2,1)S(1)} copy-done((bf16[2,512,2048]{2,1,0:T(8,128)(2,1)S(1)}, bf16[2,512,2048]{2,1,0:T(8,128)(2,1)}, u32[]{:S(2)}) %copy-start) | copy-done | bytes 4194328
  83.4 0.5 fusion.16
  83.9 3.9 %multiply_reduce_fusion.3 = (f32[128]{0:T(128)S(1)}, f32[128,512]{1,0:T(8,128)S(1)}) fusion(f32[128,512]{1,0:T(8,128)S(1)} %get-tuple-element.15, f32[512]{0:T(512)S(1)} %bitcast.142, bf16[2,512,2048]{2,1,0:T(8,128)(2,1)} %param.8, bf16[2,2048,512]{2,1,0:T(8,128)(2,1)} %param.9, f32[128,2048]{1,0:T(8,128)S(1)} %fusion.16, f32[1,128,512]{2,1,0:T(8,128)S(1)} %copy-done.1), kind=kOutput, calls=%fused_computation.86 | convolution fusion | flops 539492224 | bytes 6031872 | tf_op jit(solution)/shard_map/dot_general | solution.py:267
  87.9 3.9 %multiply_reduce_fusion.2 = (f32[128]{0:T(128)S(1)}, f32[128,512]{1,0:T(8,128)S(1)}) fusion(f32[128,512]{1,0:T(8,128)S(1)} %get-tuple-element.3, f32[512]{0:T(512)S(1)} %bitcast.138, bf16[2,512,2048]{2,1,0:T(8,128)(2,1)} %param.8, bf16[2,2048,512]{2,1,0:T(8,128)(2,1)} %param.9, f32[128,2048]{1,0:T(8,128)S(1)} %fusion.30, ...), kind=kOutput, calls=%fused_computation.84 | convolution fusion | flops 539492224 | bytes 6031872 | tf_op jit(solution)/shard_map/dot_general | solution.py:267
  91.8 1.1 subtract_subtract_fusion
  92.9 0.7 pad_maximum_fusion.2.packed_ref
  93.6 48.7 %shard_map.78 = f32[128,512]{1,0:T(8,128)} custom-call(f32[136,512]{1,0:T(8,128)} %pad_maximum_fusion.2.packed_ref), custom_call_target="tpu_custom_call" | custom-call | tf_op jit(solution)/shard_map/pallas_call | solution.py:226
  142.3 4.0 %multiply_reduce_fusion.1 = (f32[128]{0:T(128)S(1)}, f32[128,512]{1,0:T(8,128)S(1)}) fusion(f32[128,512]{1,0:T(8,128)S(1)} %get-tuple-element.15, f32[512]{0:T(512)S(1)} %bitcast.143, bf16[2,512,2048]{2,1,0:T(8,128)(2,1)} %param.8, bf16[2,2048,512]{2,1,0:T(8,128)(2,1)} %param.9, f32[128,2048]{1,0:T(8,128)S(1)} %fusion.16, f32[128,512]{1,0:T(8,128)} %shard_map.78, ...), kind=kOutput, calls=%fused_computation.82 | convolution fusion | flops 539557760 | bytes 6294016 | tf_op jit(solution)/shard_map/dot_general | solution.py:267
  146.3 0.1 multiply_subtract_fusion
  146.4 3.9 %multiply_reduce_fusion = (f32[128]{0:T(128)S(1)}, f32[128,512]{1,0:T(8,128)S(1)}) fusion(f32[128,512]{1,0:T(8,128)S(1)} %get-tuple-element.3, f32[512]{0:T(512)S(1)} %bitcast.139, bf16[2,512,2048]{2,1,0:T(8,128)(2,1)} %param.8, bf16[2,2048,512]{2,1,0:T(8,128)(2,1)} %param.9, f32[128,2048]{1,0:T(8,128)S(1)} %fusion.30, f32[128,512]{1,0:T(8,128)S(1)} %multiply_subtract_fusion), kind=kOutput, calls=%fused_computation.80 | convolution fusion | flops 539492224 | bytes 6031872 | tf_op jit(solution)/shard_map/dot_general | solution.py:267
  150.3 0.1 subtract_bitcast_fusion
  150.4 1.0 pad_maximum_fusion
  (24 shorter events, 0.3 us)
Async XLA Ops:
  0.6 91.1 %collective-permute-start.1 = (f32[128,512]{1,0:T(8,128)}, f32[128,512]{1,0:T(8,128)}, u32[]{:S(2)}, u32[]{:S(2)}) collective-permute-start(f32[128,512]{1,0:T(8,128)} %bitcast.127), channel_id=1, source_target_pairs={{0,1},{1,2},{2,3},{3,4},{4,5},{5,6},{6,7},{7,8},{8,9},{9,10},{10,1... | collective-permute-start | bytes 786440 | tf_op jit(solution)/shard_map/ppermute | solution.py:14
  5.1 8.4 %collective-permute-start = (f32[128,512]{1,0:T(8,128)}, f32[128,512]{1,0:T(8,128)S(1)}, u32[]{:S(2)}, u32[]{:S(2)}) collective-permute-start(f32[128,512]{1,0:T(8,128)} %bitcast.128), channel_id=1, source_target_pairs={{1,0},{2,1},{3,2},{4,3},{5,4},{6,5},{7,6},{8,7},{9,8},{10,9},{11,1... | collective-permute-start | bytes 786440 | tf_op jit(solution)/shard_map/ppermute | solution.py:14
  10.4 3.2 %copy-start.4 = (f32[2,512]{1,0:T(2,128)S(1)}, f32[2,512]{1,0:T(2,128)}, u32[]{:S(2)}) copy-start(f32[2,512]{1,0:T(2,128)} %param.11) | copy-start | bytes 12292
  13.6 64.1 %copy-start.2 = (f32[1,128,512]{2,1,0:T(8,128)S(1)}, f32[1,128,512]{2,1,0:T(8,128)}, u32[]{:S(2)}) copy-start(f32[1,128,512]{2,1,0:T(8,128)} %param.6) | copy-start | bytes 786436
  77.7 3.4 %copy-start.5 = (bf16[2,2048,512]{2,1,0:T(8,128)(2,1)S(1)}, bf16[2,2048,512]{2,1,0:T(8,128)(2,1)}, u32[]{:S(2)}) copy-start(bf16[2,2048,512]{2,1,0:T(8,128)(2,1)} %param.9) | copy-start | bytes 12582916
  81.2 2.2 %copy-start = (bf16[2,512,2048]{2,1,0:T(8,128)(2,1)S(1)}, bf16[2,512,2048]{2,1,0:T(8,128)(2,1)}, u32[]{:S(2)}) copy-start(bf16[2,512,2048]{2,1,0:T(8,128)(2,1)} %param.8) | copy-start | bytes 12582916
  81.2 2.7 %copy-start.1 = (f32[1,128,512]{2,1,0:T(8,128)S(1)}, f32[1,128,512]{2,1,0:T(8,128)}, u32[]{:S(2)}) copy-start(f32[1,128,512]{2,1,0:T(8,128)} %param.7) | copy-start | bytes 786436
  142.3 4.0 %copy-start.3 = (f32[128,512]{1,0:T(8,128)S(1)}, f32[128,512]{1,0:T(8,128)}, u32[]{:S(2)}) copy-start(f32[128,512]{1,0:T(8,128)} %shard_map.78) | copy-start | bytes 786436

commit v13 on v9

--- a/solution.py
+++ b/solution.py
@@ -22,7 +22,7 @@
     out = []
     for part in (along_z, groups // along_z):
         while part > 1:
-            step = 4 if part % 4 == 0 else 2
+            step = 2 if part % 8 == 0 else (4 if part % 4 == 0 else 2)
             out.append(step)
             part //= step
     return out

time: 153 us -> 145 us (0.948)
  Pallas kernels: 109 us -> 102 us
    pallas_call x2, Pallas kernels: 109 us -> 102 us  [kernel_scan(): pl.pallas_call(functools.partial(group_kernel, size, reverse, 4), out_sha...]
  transfers between devices with their start and end apart: 2 -> 2, of which waited for: 0 -> 0; matrix products, arithmetic and copies ran while one was open for 14% -> 15% of each run, Pallas kernels for 40% -> 38%
where the time goes in v13:
time: 145 us
  Pallas kernels  102 us (70%)
  matrix products  25.1 us (17%)
  starting transfers between devices  7.12 us (5%)
  other arithmetic  6.33 us (4%)
  local copies, waits for them, and re-layouts  3.09 us (2%)
    pallas_call x2, Pallas kernels, kernel_scan(): pl.pallas_call(functools.partial(group_kernel, size, reverse, 4), out_sha...  102 us
    dot_general x4, matrix products, backward_block(): lax.dot_general(grad_pre, w_first, (((1,), (1,)), ((), ())), preferred_el...  15.6 us
    ppermute x2, starting transfers between devices, shifted(): return lax.ppermute(block, axis, route)  7.12 us
    dot_general x3, matrix products, finish_block(): jnp.dot(hidden, w_second, preferred_element_type=jnp.float32)  6.85 us
  transfers between devices with their start and end apart: 2, of which 0 were waited for; matrix products, arithmetic and copies ran while one was open for 15% of the time, Pallas kernels for 38%

profile of v13, /device:TPU:1, one launch (start us, length us, event | category | flops | bytes accessed | tf_op | source)
XLA Modules:
  0.0 144.9 jit_solution(13069247924643854902)
XLA Ops:
  0.6 4.5 %collective-permute-start.1 = (f32[128,512]{1,0:T(8,128)}, f32[128,512]{1,0:T(8,128)}, u32[]{:S(2)}, u32[]{:S(2)}) collective-permute-start(f32[128,512]{1,0:T(8,128)} %bitcast.127), channel_id=1, source_target_pairs={{0,1},{1,2},{2,3},{3,4},{4,5},{5,6},{6,7},{7,8},{8,9},{9,10},{10,1... | collective-permute-start | bytes 786440 | tf_op jit(solution)/shard_map/ppermute | solution.py:14
  5.1 2.6 %collective-permute-start = (f32[128,512]{1,0:T(8,128)}, f32[128,512]{1,0:T(8,128)S(1)}, u32[]{:S(2)}, u32[]{:S(2)}) collective-permute-start(f32[128,512]{1,0:T(8,128)} %bitcast.128), channel_id=1, source_target_pairs={{1,0},{2,1},{3,2},{4,3},{5,4},{6,5},{7,6},{8,7},{9,8},{10,9},{11,1... | collective-permute-start | bytes 786440 | tf_op jit(solution)/shard_map/ppermute | solution.py:14
  7.8 1.1 multiply_reduce_fusion.7
  8.8 0.8 fusion.133
  9.6 0.8 fusion.132
  10.4 3.2 %multiply_reduce_fusion.6 = (f32[128]{0:T(128)S(1)}, f32[128,512]{1,0:T(8,128)S(1)}) fusion(bf16[2,2048,512]{2,1,0:T(8,128)(2,1)} %param.9, bf16[2,512,2048]{2,1,0:T(8,128)(2,1)} %param.8, f32[1,128,512]{2,1,0:T(8,128)} %param.6, f32[512]{0:T(512)S(1)} %bitcast.136, f32[128]{0:T(128)S(1)} %add_rsqrt_fusion.3, f32[512]{0:T(512)S(1)} %bitcast.129), kind=kOutput, calls=%fused_computation.92 | convolution fusion | flops 538640256 | bytes 4985856 | tf_op jit(solution)/shard_map/dot_general | solution.py:247
  13.6 3.0 %fusion.70 = f32[128,512]{1,0:T(8,128)S(1)} fusion(f32[128,512]{1,0:T(8,128)S(1)} %collective-permute-done, bf16[2,2048,512]{2,1,0:T(8,128)(2,1)} %param.9, bf16[2,512,2048]{2,1,0:T(8,128)(2,1)} %param.8, f32[128,512]{1,0:T(8,128)S(1)} %get-tuple-element.13, f32[512]{0:T(512)S(1)} %bitcast.140, f32[128]{0:T(128)S(1)} %add_rsqrt_fusion.2, f32[512]{0:T(512)S(1)} %bitcast.133), kind=kOutput, calls=%fused_computation.60 | convolution fusion | flops 538574848 | bytes 5247488 | tf_op jit(solution)/shard_map/dot_general | solution.py:247
  16.7 0.7 pad_maximum_fusion.3.packed_ref
  17.4 55.4 %shard_map.77 = f32[128,512]{1,0:T(8,128)} custom-call(f32[136,512]{1,0:T(8,128)} %pad_maximum_fusion.3.packed_ref), custom_call_target="tpu_custom_call" | custom-call | tf_op jit(solution)/shard_map/pallas_call | solution.py:218
  72.9 1.2 multiply_reduce_fusion.5
  74.1 2.2 %fusion.30 = f32[128,2048]{1,0:T(8,128)S(1)} fusion(bf16[2,512,2048]{2,1,0:T(8,128)(2,1)} %param.8, f32[128,512]{1,0:T(8,128)S(1)} %get-tuple-element.3, f32[512]{0:T(512)S(1)} %bitcast.137, f32[128]{0:T(128)S(1)} %get-tuple-element.9), kind=kOutput, calls=%fused_computation.34 | convolution fusion | flops 268632064 | bytes 3410432 | tf_op jit(solution)/shard_map/dot_general | solution.py:241
  76.3 0.6 multiply_reduce_fusion.4
  77.0 1.5 %copy-done = bf16[2,512,2048]{2,1,0:T(8,128)(2,1)S(1)} copy-done((bf16[2,512,2048]{2,1,0:T(8,128)(2,1)S(1)}, bf16[2,512,2048]{2,1,0:T(8,128)(2,1)}, u32[]{:S(2)}) %copy-start) | copy-done | bytes 4194328
  78.5 0.5 fusion.16
  79.0 3.9 %multiply_reduce_fusion.3 = (f32[128]{0:T(128)S(1)}, f32[128,512]{1,0:T(8,128)S(1)}) fusion(f32[128,512]{1,0:T(8,128)S(1)} %get-tuple-element.15, f32[512]{0:T(512)S(1)} %bitcast.142, bf16[2,512,2048]{2,1,0:T(8,128)(2,1)} %param.8, bf16[2,2048,512]{2,1,0:T(8,128)(2,1)} %param.9, f32[128,2048]{1,0:T(8,128)S(1)} %fusion.16, f32[1,128,512]{2,1,0:T(8,128)S(1)} %copy-done.1), kind=kOutput, calls=%fused_computation.86 | convolution fusion | flops 539492224 | bytes 6031872 | tf_op jit(solution)/shard_map/dot_general | solution.py:259
  83.0 3.9 %multiply_reduce_fusion.2 = (f32[128]{0:T(128)S(1)}, f32[128,512]{1,0:T(8,128)S(1)}) fusion(f32[128,512]{1,0:T(8,128)S(1)} %get-tuple-element.3, f32[512]{0:T(512)S(1)} %bitcast.138, bf16[2,512,2048]{2,1,0:T(8,128)(2,1)} %param.8, bf16[2,2048,512]{2,1,0:T(8,128)(2,1)} %param.9, f32[128,2048]{1,0:T(8,128)S(1)} %fusion.30, ...), kind=kOutput, calls=%fused_computation.84 | convolution fusion | flops 539492224 | bytes 6031872 | tf_op jit(solution)/shard_map/dot_general | solution.py:259
  86.9 1.1 subtract_subtract_fusion
  88.0 0.7 pad_maximum_fusion.2.packed_ref
  88.7 46.9 %shard_map.78 = f32[128,512]{1,0:T(8,128)} custom-call(f32[136,512]{1,0:T(8,128)} %pad_maximum_fusion.2.packed_ref), custom_call_target="tpu_custom_call" | custom-call | tf_op jit(solution)/shard_map/pallas_call | solution.py:218
  135.6 4.0 %multiply_reduce_fusion.1 = (f32[128]{0:T(128)S(1)}, f32[128,512]{1,0:T(8,128)S(1)}) fusion(f32[128,512]{1,0:T(8,128)S(1)} %get-tuple-element.15, f32[512]{0:T(512)S(1)} %bitcast.143, bf16[2,512,2048]{2,1,0:T(8,128)(2,1)} %param.8, bf16[2,2048,512]{2,1,0:T(8,128)(2,1)} %param.9, f32[128,2048]{1,0:T(8,128)S(1)} %fusion.16, f32[128,512]{1,0:T(8,128)} %shard_map.78, ...), kind=kOutput, calls=%fused_computation.82 | convolution fusion | flops 539557760 | bytes 6294016 | tf_op jit(solution)/shard_map/dot_general | solution.py:259
  139.6 0.1 multiply_subtract_fusion
  139.8 3.9 %multiply_reduce_fusion = (f32[128]{0:T(128)S(1)}, f32[128,512]{1,0:T(8,128)S(1)}) fusion(f32[128,512]{1,0:T(8,128)S(1)} %get-tuple-element.3, f32[512]{0:T(512)S(1)} %bitcast.139, bf16[2,512,2048]{2,1,0:T(8,128)(2,1)} %param.8, bf16[2,2048,512]{2,1,0:T(8,128)(2,1)} %param.9, f32[128,2048]{1,0:T(8,128)S(1)} %fusion.30, f32[128,512]{1,0:T(8,128)S(1)} %multiply_subtract_fusion), kind=kOutput, calls=%fused_computation.80 | convolution fusion | flops 539492224 | bytes 6031872 | tf_op jit(solution)/shard_map/dot_general | solution.py:259
  143.7 0.1 subtract_bitcast_fusion
  143.8 1.0 pad_maximum_fusion
  (24 shorter events, 0.3 us)
Async XLA Ops:
  0.6 86.3 %collective-permute-start.1 = (f32[128,512]{1,0:T(8,128)}, f32[128,512]{1,0:T(8,128)}, u32[]{:S(2)}, u32[]{:S(2)}) collective-permute-start(f32[128,512]{1,0:T(8,128)} %bitcast.127), channel_id=1, source_target_pairs={{0,1},{1,2},{2,3},{3,4},{4,5},{5,6},{6,7},{7,8},{8,9},{9,10},{10,1... | collective-permute-start | bytes 786440 | tf_op jit(solution)/shard_map/ppermute | solution.py:14
  5.1 8.4 %collective-permute-start = (f32[128,512]{1,0:T(8,128)}, f32[128,512]{1,0:T(8,128)S(1)}, u32[]{:S(2)}, u32[]{:S(2)}) collective-permute-start(f32[128,512]{1,0:T(8,128)} %bitcast.128), channel_id=1, source_target_pairs={{1,0},{2,1},{3,2},{4,3},{5,4},{6,5},{7,6},{8,7},{9,8},{10,9},{11,1... | collective-permute-start | bytes 786440 | tf_op jit(solution)/shard_map/ppermute | solution.py:14
  10.4 3.2 %copy-start.4 = (f32[2,512]{1,0:T(2,128)S(1)}, f32[2,512]{1,0:T(2,128)}, u32[]{:S(2)}) copy-start(f32[2,512]{1,0:T(2,128)} %param.11) | copy-start | bytes 12292
  13.6 59.2 %copy-start.2 = (f32[1,128,512]{2,1,0:T(8,128)S(1)}, f32[1,128,512]{2,1,0:T(8,128)}, u32[]{:S(2)}) copy-start(f32[1,128,512]{2,1,0:T(8,128)} %param.6) | copy-start | bytes 786436
  72.8 3.4 %copy-start.5 = (bf16[2,2048,512]{2,1,0:T(8,128)(2,1)S(1)}, bf16[2,2048,512]{2,1,0:T(8,128)(2,1)}, u32[]{:S(2)}) copy-start(bf16[2,2048,512]{2,1,0:T(8,128)(2,1)} %param.9) | copy-start | bytes 12582916
  76.3 2.2 %copy-start = (bf16[2,512,2048]{2,1,0:T(8,128)(2,1)S(1)}, bf16[2,512,2048]{2,1,0:T(8,128)(2,1)}, u32[]{:S(2)}) copy-start(bf16[2,512,2048]{2,1,0:T(8,128)(2,1)} %param.8) | copy-start | bytes 12582916
  76.3 2.7 %copy-start.1 = (f32[1,128,512]{2,1,0:T(8,128)S(1)}, f32[1,128,512]{2,1,0:T(8,128)}, u32[]{:S(2)}) copy-start(f32[1,128,512]{2,1,0:T(8,128)} %param.7) | copy-start | bytes 786436
  135.6 4.0 %copy-start.3 = (f32[128,512]{1,0:T(8,128)S(1)}, f32[128,512]{1,0:T(8,128)}, u32[]{:S(2)}) copy-start(f32[128,512]{1,0:T(8,128)} %shard_map.78) | copy-start | bytes 786436

commit v14 on v13

--- a/solution.py
+++ b/solution.py
@@ -45,7 +45,7 @@
         levels.append((width_now, list(range(1, step))))
         width_now *= step
     links = [(level, k) for level, (_, ks) in enumerate(levels) for k in ks]
-    slot_c, slot_e, slot_f = (3, 4 + len(levels), 5 + len(levels))
+    slot_c, slot_e, slot_f = (4, 5 + len(levels), 6 + len(levels))
     index = order % 8
 
     def device(q):
@@ -59,6 +59,7 @@
     source = order - 8 + 2 * (3 - ring)
     sinks = [order + 8 + 2 * (k - 3) for k in range(4)]
     targets = [order + 8 + 2 * (k - ring) for k in range(4)]
+    targets += [in_ring(3), in_ring(-3)]
     targets += [order - 8 + 2 * (k - ring) for k in range(4)]
     for spread_width, ks in levels:
         targets += [order + 8 * k * spread_width for k in ks] + [order - 8 * k * spread_width for k in ks]
@@ -96,31 +97,35 @@
     mine_ref = packed_ref.at[:, pl.ds(pl.multiple_of(core * half, half), half)]
     other_ref = packed_ref.at[:, pl.ds(pl.multiple_of((1 - core) * half, half), half)]
     pending = [copy(block(other_ref, k), block(got.at[0], k), 0, k, partner) for k in range(pieces + 1)]
-    for stage in range(3):
-        following = []
-        for piece in range(pieces + 1):
-            first_row, count = spans[piece]
-            part = slice(first_row, first_row + count)
-            pending[piece].wait_recv()
-            came = got[stage, part, :]
-            if stage == 0:
-                mine = mine_ref[part, :]
-                later = jnp.where(first, came, mine)
-                earlier = jnp.where(first, mine, came)
-                scale = jnp.where(first, got[0, factor_row, :], mine_ref[factor_row, :])
-                value = later * earlier if piece == 0 else later + scale * earlier
+    ahead = []
+    for piece in range(pieces + 1):
+        first_row, count = spans[piece]
+        part = slice(first_row, first_row + count)
+        pending[piece].wait_recv()
+        came = got[0, part, :]
+        mine = mine_ref[part, :]
+        later = jnp.where(first, came, mine)
+        earlier = jnp.where(first, mine, came)
+        scale = jnp.where(first, got[0, factor_row, :], mine_ref[factor_row, :])
+        state[0, part, :] = later * earlier if piece == 0 else later + scale * earlier
+        ahead.append(
+            [copy(block(state.at[0], piece), block(got.at[step], piece), step, piece, in_ring(step)) for step in (1, 2, 3)]
+        )
+    for piece in range(pieces + 1):
+        first_row, count = spans[piece]
+        part = slice(first_row, first_row + count)
+        value = state[0, part, :]
+        scale = state[0, factor_row, :]
+        for step in (1, 2, 3):
+            ahead[piece][step - 1].wait_recv()
+            came = got[step, part, :]
+            reach = ring >= step
+            if piece == 0:
+                value = jnp.where(reach, value * came, value)
             else:
-                held = state[stage - 1, part, :]
-                scale = state[stage - 1, factor_row, :]
-                combined = held * came if piece == 0 else held + scale * came
-                value = jnp.where(ring >= stage, combined, held)
-            state[stage, part, :] = value
-            if stage < 2:
-                step = 1 if stage == 0 else 2
-                following.append(
-                    copy(block(state.at[stage], piece), block(got.at[stage + 1], piece), stage + 1, piece, in_ring(step))
-                )
-        pending = following
+                value = jnp.where(reach, value + scale * came, value)
+                scale = jnp.where(reach, scale * got[step, factor_row, :], scale)
+        state[2, part, :] = value
 
     sides = [copy(state.at[2], final.at[k], slot_f, k, order + 1 + k) for k in range(3)]
     sides.append(copy(mine_ref, pair, slot_f, 3, partner))
@@ -164,7 +169,7 @@
     for level, (spread_width, ks) in enumerate(levels):
         arrivals = []
         for k in ks:
-            arrivals.append((k, copy(q_state.at[level], q_got.at[landing], 4 + level, k - 1, order + 8 * k * spread_width), landing))
+            arrivals.append((k, copy(q_state.at[level], q_got.at[landing], 5 + level, k - 1, order + 8 * k * spread_width), landing))
             landing += 1
         held = q_state[level]
         for k, handle, spot in arrivals:
@@ -221,15 +226,15 @@
         in_specs=[pl.BlockSpec(memory_space=pltpu.VMEM)],
         out_specs=pl.BlockSpec(memory_space=pltpu.VMEM),
         scratch_shapes=[
-            pltpu.VMEM((3, rows + 8, half), jnp.float32),
+            pltpu.VMEM((4, rows + 8, half), jnp.float32),
             pltpu.VMEM((3, rows + 8, half), jnp.float32),
             pltpu.VMEM((links + 1, quarter + 8, half), jnp.float32),
             pltpu.VMEM((levels + 1, quarter + 8, half), jnp.float32),
             pltpu.VMEM((7, quarter, half), jnp.float32),
             pltpu.VMEM((3, rows + 8, half), jnp.float32),
             pltpu.VMEM((rows + 8, half), jnp.float32),
-            pltpu.SemaphoreType.DMA((6 + levels, 8)),
-            pltpu.SemaphoreType.DMA((6 + levels, 8)),
+            pltpu.SemaphoreType.DMA((7 + levels, 8)),
+            pltpu.SemaphoreType.DMA((7 + levels, 8)),
         ],
         compiler_params=pltpu.CompilerParams(collective_id=ident, has_side_effects=True),
     )(packed)

time: 145 us -> 147 us (1.014)
  Pallas kernels: 102 us -> 104 us
where the time goes in v14:
time: 147 us; the launch traced here: 146 us
  Pallas kernels  104 us (71%)
  matrix products  25.1 us (17%)
  starting transfers between devices  7.12 us (5%)
  other arithmetic  6.33 us (4%)
  local copies, waits for them, and re-layouts  3.1 us (2%)
    pallas_call x2, Pallas kernels, kernel_scan(): pl.pallas_call(functools.partial(group_kernel, size, reverse, 4), out_sha...  104 us
    dot_general x4, matrix products, backward_block(): lax.dot_general(grad_pre, w_first, (((1,), (1,)), ((), ())), preferred_el...  15.6 us
    ppermute x2, starting transfers between devices, shifted(): return lax.ppermute(block, axis, route)  7.12 us
    dot_general x3, matrix products, finish_block(): jnp.dot(hidden, w_second, preferred_element_type=jnp.float32)  6.85 us
  transfers between devices with their start and end apart: 2, of which 0 were waited for; matrix products, arithmetic and copies ran while one was open for 15% of the time, Pallas kernels for 38%

profile of v14, /device:TPU:1, one launch (start us, length us, event | category | flops | bytes accessed | tf_op | source)
XLA Modules:
  0.0 146.2 jit_solution(9232610895413665132)
XLA Ops:
  0.6 4.5 %collective-permute-start.1 = (f32[128,512]{1,0:T(8,128)}, f32[128,512]{1,0:T(8,128)}, u32[]{:S(2)}, u32[]{:S(2)}) collective-permute-start(f32[128,512]{1,0:T(8,128)} %bitcast.127), channel_id=1, source_target_pairs={{0,1},{1,2},{2,3},{3,4},{4,5},{5,6},{6,7},{7,8},{8,9},{9,10},{10,1... | collective-permute-start | bytes 786440 | tf_op jit(solution)/shard_map/ppermute | solution.py:14
  5.1 2.6 %collective-permute-start = (f32[128,512]{1,0:T(8,128)}, f32[128,512]{1,0:T(8,128)S(1)}, u32[]{:S(2)}, u32[]{:S(2)}) collective-permute-start(f32[128,512]{1,0:T(8,128)} %bitcast.128), channel_id=1, source_target_pairs={{1,0},{2,1},{3,2},{4,3},{5,4},{6,5},{7,6},{8,7},{9,8},{10,9},{11,1... | collective-permute-start | bytes 786440 | tf_op jit(solution)/shard_map/ppermute | solution.py:14
  7.8 1.1 multiply_reduce_fusion.7
  8.8 0.8 fusion.133
  9.6 0.8 fusion.132
  10.4 3.2 %multiply_reduce_fusion.6 = (f32[128]{0:T(128)S(1)}, f32[128,512]{1,0:T(8,128)S(1)}) fusion(bf16[2,2048,512]{2,1,0:T(8,128)(2,1)} %param.9, bf16[2,512,2048]{2,1,0:T(8,128)(2,1)} %param.8, f32[1,128,512]{2,1,0:T(8,128)} %param.6, f32[512]{0:T(512)S(1)} %bitcast.136, f32[128]{0:T(128)S(1)} %add_rsqrt_fusion.3, f32[512]{0:T(512)S(1)} %bitcast.129), kind=kOutput, calls=%fused_computation.92 | convolution fusion | flops 538640256 | bytes 4985856 | tf_op jit(solution)/shard_map/dot_general | solution.py:252
  13.6 3.0 %fusion.70 = f32[128,512]{1,0:T(8,128)S(1)} fusion(f32[128,512]{1,0:T(8,128)S(1)} %collective-permute-done, bf16[2,2048,512]{2,1,0:T(8,128)(2,1)} %param.9, bf16[2,512,2048]{2,1,0:T(8,128)(2,1)} %param.8, f32[128,512]{1,0:T(8,128)S(1)} %get-tuple-element.13, f32[512]{0:T(512)S(1)} %bitcast.140, f32[128]{0:T(128)S(1)} %add_rsqrt_fusion.2, f32[512]{0:T(512)S(1)} %bitcast.133), kind=kOutput, calls=%fused_computation.60 | convolution fusion | flops 538574848 | bytes 5247488 | tf_op jit(solution)/shard_map/dot_general | solution.py:252
  16.7 0.7 pad_maximum_fusion.3.packed_ref
  17.4 56.2 %shard_map.77 = f32[128,512]{1,0:T(8,128)} custom-call(f32[136,512]{1,0:T(8,128)} %pad_maximum_fusion.3.packed_ref), custom_call_target="tpu_custom_call" | custom-call | tf_op jit(solution)/shard_map/pallas_call | solution.py:223
  73.6 1.2 multiply_reduce_fusion.5
  74.9 2.2 %fusion.30 = f32[128,2048]{1,0:T(8,128)S(1)} fusion(bf16[2,512,2048]{2,1,0:T(8,128)(2,1)} %param.8, f32[128,512]{1,0:T(8,128)S(1)} %get-tuple-element.3, f32[512]{0:T(512)S(1)} %bitcast.137, f32[128]{0:T(128)S(1)} %get-tuple-element.9), kind=kOutput, calls=%fused_computation.34 | convolution fusion | flops 268632064 | bytes 3410432 | tf_op jit(solution)/shard_map/dot_general | solution.py:246
  77.1 0.6 multiply_reduce_fusion.4
  77.7 1.5 %copy-done = bf16[2,512,2048]{2,1,0:T(8,128)(2,1)S(1)} copy-done((bf16[2,512,2048]{2,1,0:T(8,128)(2,1)S(1)}, bf16[2,512,2048]{2,1,0:T(8,128)(2,1)}, u32[]{:S(2)}) %copy-start) | copy-done | bytes 4194328
  79.3 0.5 fusion.16
  79.8 3.9 %multiply_reduce_fusion.3 = (f32[128]{0:T(128)S(1)}, f32[128,512]{1,0:T(8,128)S(1)}) fusion(f32[128,512]{1,0:T(8,128)S(1)} %get-tuple-element.15, f32[512]{0:T(512)S(1)} %bitcast.142, bf16[2,512,2048]{2,1,0:T(8,128)(2,1)} %param.8, bf16[2,2048,512]{2,1,0:T(8,128)(2,1)} %param.9, f32[128,2048]{1,0:T(8,128)S(1)} %fusion.16, f32[1,128,512]{2,1,0:T(8,128)S(1)} %copy-done.1), kind=kOutput, calls=%fused_computation.86 | convolution fusion | flops 539492224 | bytes 6031872 | tf_op jit(solution)/shard_map/dot_general | solution.py:264
  83.8 3.9 %multiply_reduce_fusion.2 = (f32[128]{0:T(128)S(1)}, f32[128,512]{1,0:T(8,128)S(1)}) fusion(f32[128,512]{1,0:T(8,128)S(1)} %get-tuple-element.3, f32[512]{0:T(512)S(1)} %bitcast.138, bf16[2,512,2048]{2,1,0:T(8,128)(2,1)} %param.8, bf16[2,2048,512]{2,1,0:T(8,128)(2,1)} %param.9, f32[128,2048]{1,0:T(8,128)S(1)} %fusion.30, ...), kind=kOutput, calls=%fused_computation.84 | convolution fusion | flops 539492224 | bytes 6031872 | tf_op jit(solution)/shard_map/dot_general | solution.py:264
  87.7 1.1 subtract_subtract_fusion
  88.8 0.7 pad_maximum_fusion.2.packed_ref
  89.5 47.5 %shard_map.78 = f32[128,512]{1,0:T(8,128)} custom-call(f32[136,512]{1,0:T(8,128)} %pad_maximum_fusion.2.packed_ref), custom_call_target="tpu_custom_call" | custom-call | tf_op jit(solution)/shard_map/pallas_call | solution.py:223
  137.0 4.0 %multiply_reduce_fusion.1 = (f32[128]{0:T(128)S(1)}, f32[128,512]{1,0:T(8,128)S(1)}) fusion(f32[128,512]{1,0:T(8,128)S(1)} %get-tuple-element.15, f32[512]{0:T(512)S(1)} %bitcast.143, bf16[2,512,2048]{2,1,0:T(8,128)(2,1)} %param.8, bf16[2,2048,512]{2,1,0:T(8,128)(2,1)} %param.9, f32[128,2048]{1,0:T(8,128)S(1)} %fusion.16, f32[128,512]{1,0:T(8,128)} %shard_map.78, ...), kind=kOutput, calls=%fused_computation.82 | convolution fusion | flops 539557760 | bytes 6294016 | tf_op jit(solution)/shard_map/dot_general | solution.py:264
  141.0 0.1 multiply_subtract_fusion
  141.2 3.9 %multiply_reduce_fusion = (f32[128]{0:T(128)S(1)}, f32[128,512]{1,0:T(8,128)S(1)}) fusion(f32[128,512]{1,0:T(8,128)S(1)} %get-tuple-element.3, f32[512]{0:T(512)S(1)} %bitcast.139, bf16[2,512,2048]{2,1,0:T(8,128)(2,1)} %param.8, bf16[2,2048,512]{2,1,0:T(8,128)(2,1)} %param.9, f32[128,2048]{1,0:T(8,128)S(1)} %fusion.30, f32[128,512]{1,0:T(8,128)S(1)} %multiply_subtract_fusion), kind=kOutput, calls=%fused_computation.80 | convolution fusion | flops 539492224 | bytes 6031872 | tf_op jit(solution)/shard_map/dot_general | solution.py:264
  145.0 0.1 subtract_bitcast_fusion
  145.2 1.0 pad_maximum_fusion
  (24 shorter events, 0.3 us)
Async XLA Ops:
  0.6 87.0 %collective-permute-start.1 = (f32[128,512]{1,0:T(8,128)}, f32[128,512]{1,0:T(8,128)}, u32[]{:S(2)}, u32[]{:S(2)}) collective-permute-start(f32[128,512]{1,0:T(8,128)} %bitcast.127), channel_id=1, source_target_pairs={{0,1},{1,2},{2,3},{3,4},{4,5},{5,6},{6,7},{7,8},{8,9},{9,10},{10,1... | collective-permute-start | bytes 786440 | tf_op jit(solution)/shard_map/ppermute | solution.py:14
  5.1 8.4 %collective-permute-start = (f32[128,512]{1,0:T(8,128)}, f32[128,512]{1,0:T(8,128)S(1)}, u32[]{:S(2)}, u32[]{:S(2)}) collective-permute-start(f32[128,512]{1,0:T(8,128)} %bitcast.128), channel_id=1, source_target_pairs={{1,0},{2,1},{3,2},{4,3},{5,4},{6,5},{7,6},{8,7},{9,8},{10,9},{11,1... | collective-permute-start | bytes 786440 | tf_op jit(solution)/shard_map/ppermute | solution.py:14
  10.4 3.2 %copy-start.4 = (f32[2,512]{1,0:T(2,128)S(1)}, f32[2,512]{1,0:T(2,128)}, u32[]{:S(2)}) copy-start(f32[2,512]{1,0:T(2,128)} %param.11) | copy-start | bytes 12292
  13.6 60.0 %copy-start.2 = (f32[1,128,512]{2,1,0:T(8,128)S(1)}, f32[1,128,512]{2,1,0:T(8,128)}, u32[]{:S(2)}) copy-start(f32[1,128,512]{2,1,0:T(8,128)} %param.6) | copy-start | bytes 786436
  73.6 3.4 %copy-start.5 = (bf16[2,2048,512]{2,1,0:T(8,128)(2,1)S(1)}, bf16[2,2048,512]{2,1,0:T(8,128)(2,1)}, u32[]{:S(2)}) copy-start(bf16[2,2048,512]{2,1,0:T(8,128)(2,1)} %param.9) | copy-start | bytes 12582916
  77.1 2.2 %copy-start = (bf16[2,512,2048]{2,1,0:T(8,128)(2,1)S(1)}, bf16[2,512,2048]{2,1,0:T(8,128)(2,1)}, u32[]{:S(2)}) copy-start(bf16[2,512,2048]{2,1,0:T(8,128)(2,1)} %param.8) | copy-start | bytes 12582916
  77.1 2.7 %copy-start.1 = (f32[1,128,512]{2,1,0:T(8,128)S(1)}, f32[1,128,512]{2,1,0:T(8,128)}, u32[]{:S(2)}) copy-start(f32[1,128,512]{2,1,0:T(8,128)} %param.7) | copy-start | bytes 786436
  137.0 4.0 %copy-start.3 = (f32[128,512]{1,0:T(8,128)S(1)}, f32[128,512]{1,0:T(8,128)}, u32[]{:S(2)}) copy-start(f32[128,512]{1,0:T(8,128)} %shard_map.78) | copy-start | bytes 786436

commit v15 on v13

--- a/solution.py
+++ b/solution.py
@@ -20,9 +20,9 @@
 def radices(groups):
     along_z = min(groups, 8)
     out = []
-    for part in (along_z, groups // along_z):
+    for axis, part in enumerate((along_z, groups // along_z)):
         while part > 1:
-            step = 2 if part % 8 == 0 else (4 if part % 4 == 0 else 2)
+            step = 2 if part % 8 == 0 or axis == 1 else (4 if part % 4 == 0 else 2)
             out.append(step)
             part //= step
     return out

time: 145 us -> 152 us (1.048)
  Pallas kernels: 102 us -> 109 us
    pallas_call x2, Pallas kernels: 102 us -> 109 us  [kernel_scan(): pl.pallas_call(functools.partial(group_kernel, size, reverse, 4), out_sha...]
  transfers between devices with their start and end apart: 2 -> 2, of which waited for: 0 -> 0; matrix products, arithmetic and copies ran while one was open for 15% -> 14% of each run, Pallas kernels for 38% -> 39%
where the time goes in v15:
time: 152 us
  Pallas kernels  109 us (72%)
  matrix products  25.1 us (17%)
  starting transfers between devices  7.12 us (5%)
  other arithmetic  6.33 us (4%)
  local copies, waits for them, and re-layouts  3.1 us (2%)
    pallas_call x2, Pallas kernels, kernel_scan(): pl.pallas_call(functools.partial(group_kernel, size, reverse, 4), out_sha...  109 us
    dot_general x4, matrix products, backward_block(): lax.dot_general(grad_pre, w_first, (((1,), (1,)), ((), ())), preferred_el...  15.6 us
    ppermute x2, starting transfers between devices, shifted(): return lax.ppermute(block, axis, route)  7.12 us
    dot_general x3, matrix products, finish_block(): jnp.dot(hidden, w_second, preferred_element_type=jnp.float32)  6.85 us
  transfers between devices with their start and end apart: 2, of which 0 were waited for; matrix products, arithmetic and copies ran while one was open for 14% of the time, Pallas kernels for 39%

profile of v15, /device:TPU:1, one launch (start us, length us, event | category | flops | bytes accessed | tf_op | source)
XLA Modules:
  0.0 151.7 jit_solution(12453576556669625091)
XLA Ops:
  0.6 4.5 %collective-permute-start.1 = (f32[128,512]{1,0:T(8,128)}, f32[128,512]{1,0:T(8,128)}, u32[]{:S(2)}, u32[]{:S(2)}) collective-permute-start(f32[128,512]{1,0:T(8,128)} %bitcast.127), channel_id=1, source_target_pairs={{0,1},{1,2},{2,3},{3,4},{4,5},{5,6},{6,7},{7,8},{8,9},{9,10},{10,1... | collective-permute-start | bytes 786440 | tf_op jit(solution)/shard_map/ppermute | solution.py:14
  5.1 2.6 %collective-permute-start = (f32[128,512]{1,0:T(8,128)}, f32[128,512]{1,0:T(8,128)S(1)}, u32[]{:S(2)}, u32[]{:S(2)}) collective-permute-start(f32[128,512]{1,0:T(8,128)} %bitcast.128), channel_id=1, source_target_pairs={{1,0},{2,1},{3,2},{4,3},{5,4},{6,5},{7,6},{8,7},{9,8},{10,9},{11,1... | collective-permute-start | bytes 786440 | tf_op jit(solution)/shard_map/ppermute | solution.py:14
  7.8 1.1 multiply_reduce_fusion.7
  8.8 0.8 fusion.133
  9.6 0.8 fusion.132
  10.4 3.2 %multiply_reduce_fusion.6 = (f32[128]{0:T(128)S(1)}, f32[128,512]{1,0:T(8,128)S(1)}) fusion(bf16[2,2048,512]{2,1,0:T(8,128)(2,1)} %param.9, bf16[2,512,2048]{2,1,0:T(8,128)(2,1)} %param.8, f32[1,128,512]{2,1,0:T(8,128)} %param.6, f32[512]{0:T(512)S(1)} %bitcast.136, f32[128]{0:T(128)S(1)} %add_rsqrt_fusion.3, f32[512]{0:T(512)S(1)} %bitcast.129), kind=kOutput, calls=%fused_computation.92 | convolution fusion | flops 538640256 | bytes 4985856 | tf_op jit(solution)/shard_map/dot_general | solution.py:247
  13.6 3.0 %fusion.70 = f32[128,512]{1,0:T(8,128)S(1)} fusion(f32[128,512]{1,0:T(8,128)S(1)} %collective-permute-done, bf16[2,2048,512]{2,1,0:T(8,128)(2,1)} %param.9, bf16[2,512,2048]{2,1,0:T(8,128)(2,1)} %param.8, f32[128,512]{1,0:T(8,128)S(1)} %get-tuple-element.13, f32[512]{0:T(512)S(1)} %bitcast.140, f32[128]{0:T(128)S(1)} %add_rsqrt_fusion.2, f32[512]{0:T(512)S(1)} %bitcast.133), kind=kOutput, calls=%fused_computation.60 | convolution fusion | flops 538574848 | bytes 5247488 | tf_op jit(solution)/shard_map/dot_general | solution.py:247
  16.7 0.7 pad_maximum_fusion.3.packed_ref
  17.4 59.0 %shard_map.77 = f32[128,512]{1,0:T(8,128)} custom-call(f32[136,512]{1,0:T(8,128)} %pad_maximum_fusion.3.packed_ref), custom_call_target="tpu_custom_call" | custom-call | tf_op jit(solution)/shard_map/pallas_call | solution.py:218
  76.5 1.2 multiply_reduce_fusion.5
  77.7 2.2 %fusion.30 = f32[128,2048]{1,0:T(8,128)S(1)} fusion(bf16[2,512,2048]{2,1,0:T(8,128)(2,1)} %param.8, f32[128,512]{1,0:T(8,128)S(1)} %get-tuple-element.3, f32[512]{0:T(512)S(1)} %bitcast.137, f32[128]{0:T(128)S(1)} %get-tuple-element.9), kind=kOutput, calls=%fused_computation.34 | convolution fusion | flops 268632064 | bytes 3410432 | tf_op jit(solution)/shard_map/dot_general | solution.py:241
  79.9 0.6 multiply_reduce_fusion.4
  80.6 1.5 %copy-done = bf16[2,512,2048]{2,1,0:T(8,128)(2,1)S(1)} copy-done((bf16[2,512,2048]{2,1,0:T(8,128)(2,1)S(1)}, bf16[2,512,2048]{2,1,0:T(8,128)(2,1)}, u32[]{:S(2)}) %copy-start) | copy-done | bytes 4194328
  82.1 0.5 fusion.16
  82.6 3.9 %multiply_reduce_fusion.3 = (f32[128]{0:T(128)S(1)}, f32[128,512]{1,0:T(8,128)S(1)}) fusion(f32[128,512]{1,0:T(8,128)S(1)} %get-tuple-element.15, f32[512]{0:T(512)S(1)} %bitcast.142, bf16[2,512,2048]{2,1,0:T(8,128)(2,1)} %param.8, bf16[2,2048,512]{2,1,0:T(8,128)(2,1)} %param.9, f32[128,2048]{1,0:T(8,128)S(1)} %fusion.16, f32[1,128,512]{2,1,0:T(8,128)S(1)} %copy-done.1), kind=kOutput, calls=%fused_computation.86 | convolution fusion | flops 539492224 | bytes 6031872 | tf_op jit(solution)/shard_map/dot_general | solution.py:259
  86.6 3.9 %multiply_reduce_fusion.2 = (f32[128]{0:T(128)S(1)}, f32[128,512]{1,0:T(8,128)S(1)}) fusion(f32[128,512]{1,0:T(8,128)S(1)} %get-tuple-element.3, f32[512]{0:T(512)S(1)} %bitcast.138, bf16[2,512,2048]{2,1,0:T(8,128)(2,1)} %param.8, bf16[2,2048,512]{2,1,0:T(8,128)(2,1)} %param.9, f32[128,2048]{1,0:T(8,128)S(1)} %fusion.30, ...), kind=kOutput, calls=%fused_computation.84 | convolution fusion | flops 539492224 | bytes 6031872 | tf_op jit(solution)/shard_map/dot_general | solution.py:259
  90.5 1.1 subtract_subtract_fusion
  91.6 0.7 pad_maximum_fusion.2.packed_ref
  92.3 50.2 %shard_map.78 = f32[128,512]{1,0:T(8,128)} custom-call(f32[136,512]{1,0:T(8,128)} %pad_maximum_fusion.2.packed_ref), custom_call_target="tpu_custom_call" | custom-call | tf_op jit(solution)/shard_map/pallas_call | solution.py:218
  142.5 4.0 %multiply_reduce_fusion.1 = (f32[128]{0:T(128)S(1)}, f32[128,512]{1,0:T(8,128)S(1)}) fusion(f32[128,512]{1,0:T(8,128)S(1)} %get-tuple-element.15, f32[512]{0:T(512)S(1)} %bitcast.143, bf16[2,512,2048]{2,1,0:T(8,128)(2,1)} %param.8, bf16[2,2048,512]{2,1,0:T(8,128)(2,1)} %param.9, f32[128,2048]{1,0:T(8,128)S(1)} %fusion.16, f32[128,512]{1,0:T(8,128)} %shard_map.78, ...), kind=kOutput, calls=%fused_computation.82 | convolution fusion | flops 539557760 | bytes 6294016 | tf_op jit(solution)/shard_map/dot_general | solution.py:259
  146.5 0.1 multiply_subtract_fusion
  146.7 3.9 %multiply_reduce_fusion = (f32[128]{0:T(128)S(1)}, f32[128,512]{1,0:T(8,128)S(1)}) fusion(f32[128,512]{1,0:T(8,128)S(1)} %get-tuple-element.3, f32[512]{0:T(512)S(1)} %bitcast.139, bf16[2,512,2048]{2,1,0:T(8,128)(2,1)} %param.8, bf16[2,2048,512]{2,1,0:T(8,128)(2,1)} %param.9, f32[128,2048]{1,0:T(8,128)S(1)} %fusion.30, f32[128,512]{1,0:T(8,128)S(1)} %multiply_subtract_fusion), kind=kOutput, calls=%fused_computation.80 | convolution fusion | flops 539492224 | bytes 6031872 | tf_op jit(solution)/shard_map/dot_general | solution.py:259
  150.6 0.1 subtract_bitcast_fusion
  150.7 1.0 pad_maximum_fusion
  (24 shorter events, 0.3 us)
Async XLA Ops:
  0.6 89.9 %collective-permute-start.1 = (f32[128,512]{1,0:T(8,128)}, f32[128,512]{1,0:T(8,128)}, u32[]{:S(2)}, u32[]{:S(2)}) collective-permute-start(f32[128,512]{1,0:T(8,128)} %bitcast.127), channel_id=1, source_target_pairs={{0,1},{1,2},{2,3},{3,4},{4,5},{5,6},{6,7},{7,8},{8,9},{9,10},{10,1... | collective-permute-start | bytes 786440 | tf_op jit(solution)/shard_map/ppermute | solution.py:14
  5.1 8.4 %collective-permute-start = (f32[128,512]{1,0:T(8,128)}, f32[128,512]{1,0:T(8,128)S(1)}, u32[]{:S(2)}, u32[]{:S(2)}) collective-permute-start(f32[128,512]{1,0:T(8,128)} %bitcast.128), channel_id=1, source_target_pairs={{1,0},{2,1},{3,2},{4,3},{5,4},{6,5},{7,6},{8,7},{9,8},{10,9},{11,1... | collective-permute-start | bytes 786440 | tf_op jit(solution)/shard_map/ppermute | solution.py:14
  10.4 3.2 %copy-start.4 = (f32[2,512]{1,0:T(2,128)S(1)}, f32[2,512]{1,0:T(2,128)}, u32[]{:S(2)}) copy-start(f32[2,512]{1,0:T(2,128)} %param.11) | copy-start | bytes 12292
  13.6 62.9 %copy-start.2 = (f32[1,128,512]{2,1,0:T(8,128)S(1)}, f32[1,128,512]{2,1,0:T(8,128)}, u32[]{:S(2)}) copy-start(f32[1,128,512]{2,1,0:T(8,128)} %param.6) | copy-start | bytes 786436
  76.5 3.4 %copy-start.5 = (bf16[2,2048,512]{2,1,0:T(8,128)(2,1)S(1)}, bf16[2,2048,512]{2,1,0:T(8,128)(2,1)}, u32[]{:S(2)}) copy-start(bf16[2,2048,512]{2,1,0:T(8,128)(2,1)} %param.9) | copy-start | bytes 12582916
  79.9 2.2 %copy-start = (bf16[2,512,2048]{2,1,0:T(8,128)(2,1)S(1)}, bf16[2,512,2048]{2,1,0:T(8,128)(2,1)}, u32[]{:S(2)}) copy-start(bf16[2,512,2048]{2,1,0:T(8,128)(2,1)} %param.8) | copy-start | bytes 12582916
  79.9 2.7 %copy-start.1 = (f32[1,128,512]{2,1,0:T(8,128)S(1)}, f32[1,128,512]{2,1,0:T(8,128)}, u32[]{:S(2)}) copy-start(f32[1,128,512]{2,1,0:T(8,128)} %param.7) | copy-start | bytes 786436
  142.5 4.0 %copy-start.3 = (f32[128,512]{1,0:T(8,128)S(1)}, f32[128,512]{1,0:T(8,128)}, u32[]{:S(2)}) copy-start(f32[128,512]{1,0:T(8,128)} %shard_map.78) | copy-start | bytes 786436
